TPU v7x, 32 devices: a whole 2x2x4 slice. The times are simulated.
32 devices in a mesh: row: 4 (over y, x), col: 8 (over z, core).
Axes of the slice: x: 2, y: 2, z: 4, core: 2. Of those that a mesh axis runs over, the one named last changes fastest.
Arguments:
- patterns: bfloat16 [512, 256, 256], P(('row', 'col')), may hold values from -8 to 8, as said below
- ref_spectrum: float32 [2, 256, 256], replicated, may hold values from -6 to 6
- shifts: int32 [512, 2], P(('row', 'col')), may hold values from -16 to 16
- bin_owner: int32 [512, 1], P(('row', 'col')), may hold values from 0 to 7; in each aligned block of 16 rows (0 to 15, 16 to 31, ...) at most 4 rows name the same one
- bin_index: int32 [512], P(('row', 'col')), may hold values from 0 to 3
Outputs:
- final_reference: float32 [2, 256, 256], replicated
- weights: float32 [512], P(('row', 'col'))
- binned: float32 [128, 256, 256], P(('row', 'col'))
Inputs may be any that keep to these rules, and one draw needn't show every extreme that they name: `bin_owner`: in the 16 patterns of each block of probe positions, no value is named more than 4 times, a bound that some block reaches. `patterns`: each pattern is displaced by minus its shifts and by a residual shift that is not given.
All inputs are finite; a program needn't handle non-finite values.
Results may differ from a plain program's by a relative error of at most 0.0037.
Values may be sent and summed in bfloat16 or wider, within the bound.
No kernel may reach another device: no remote copies, remote signals or barrier semaphores. Data moves between devices by JAX's collectives and lax.ppermute only.
A program may use at most 128 MiB of HBM per device.

v0:
```python
import math

import jax
import jax.numpy as jnp
from jax import lax
from jax.sharding import PartitionSpec as P

BINS = 4
ITERS = 2


def dft_tables(extent):
    indices = jnp.arange(extent, dtype=jnp.int32)
    product = jnp.mod(indices[:, None] * indices[None, :], extent)
    angles = product.astype(jnp.float32) * (2.0 * math.pi / extent)
    return (jnp.cos(angles).astype(jnp.bfloat16), jnp.sin(angles).astype(jnp.bfloat16))


def stacked_tables(extent):
    cosine, sine = dft_tables(extent)
    fwd_one = jnp.stack([cosine, sine], axis=1)
    fwd_two = jnp.stack([jnp.stack([cosine, -sine]), jnp.stack([-sine, -cosine])])
    inv_one = jnp.stack([jnp.stack([cosine, sine], axis=1), jnp.stack([-sine, cosine], axis=1)])
    inv_two = jnp.stack([cosine, -sine])
    return (fwd_one, fwd_two, inv_one, inv_two)


def forward(pattern_block, fwd_one, fwd_two):
    half_section = jnp.einsum(
        "bij,jtk->bitk", pattern_block, fwd_one, preferred_element_type=jnp.float32
    ).astype(jnp.bfloat16)
    return jnp.einsum(
        "otij,bjtk->boik", fwd_two, half_section, preferred_element_type=jnp.float32
    ).astype(jnp.bfloat16)


def phase_ramp(shift_block, extent):
    freqs = jnp.arange(extent, dtype=jnp.int32)
    shift_rows = shift_block[:, 0][:, None, None]
    shift_cols = shift_block[:, 1][:, None, None]
    product = jnp.mod(freqs[None, :, None] * shift_rows + freqs[None, None, :] * shift_cols, extent)
    angles = product.astype(jnp.float32) * (2.0 * math.pi / extent)
    return (jnp.cos(angles), jnp.sin(angles))


def correlate(spec_block, cos_ramp, sin_ramp, ref_now, inv_one, inv_two):
    extent = spec_block.shape[-1]
    spec_re = spec_block[:, 0].astype(jnp.float32)
    spec_im = spec_block[:, 1].astype(jnp.float32)
    aligned_re = spec_re * cos_ramp + spec_im * sin_ramp
    aligned_im = spec_im * cos_ramp - spec_re * sin_ramp
    cross_re = aligned_re * ref_now[0] + aligned_im * ref_now[1]
    cross_im = aligned_im * ref_now[0] - aligned_re * ref_now[1]
    cross = jnp.stack([cross_re, cross_im], axis=1).astype(jnp.bfloat16)
    half_section = jnp.einsum(
        "btik,tkol->biol", cross, inv_one, preferred_element_type=jnp.float32
    ).astype(jnp.bfloat16)
    corr_map = jnp.einsum(
        "oij,bjol->bil", inv_two, half_section, preferred_element_type=jnp.float32
    ) / (extent * extent)
    peak_value = jnp.max(corr_map, axis=(1, 2))
    spread = jnp.sqrt(jnp.mean(corr_map * corr_map, axis=(1, 2)) + 1e-06)
    weight = peak_value / spread
    local_term = jnp.stack(
        [
            jnp.sum(weight[:, None, None] * aligned_re, axis=0),
            jnp.sum(weight[:, None, None] * aligned_im, axis=0),
        ]
    )
    return (weight, local_term)


def normalize(summed):
    power = jnp.mean(summed[0] * summed[0] + summed[1] * summed[1])
    return summed / jnp.sqrt(power + 1e-06)


def accumulate(patterns, first_weight, bin_owner, bin_index):
    pat_count, extent = (patterns.shape[0], patterns.shape[1])
    pixels = extent * extent
    col_count = lax.axis_size("col")
    scaled = (first_weight[:, None, None] * patterns.astype(jnp.float32)).astype(jnp.bfloat16)
    flat = scaled.reshape(pat_count, pixels)
    owners = bin_owner.reshape(-1)
    targets = owners * BINS + bin_index
    columns = jnp.arange(col_count * BINS, dtype=jnp.int32)
    selector = (columns[:, None] == targets[None, :]).astype(jnp.bfloat16)
    dense = jnp.dot(selector, flat, preferred_element_type=jnp.float32)
    mine = lax.psum_scatter(dense, "col", scatter_dimension=0, tiled=True)
    return mine.reshape(BINS, extent, extent)


def on_device(patterns, ref_spectrum, shifts, bin_owner, bin_index):
    extent = patterns.shape[1]
    fwd_one, fwd_two, inv_one, inv_two = stacked_tables(extent)
    spectra = forward(patterns, fwd_one, fwd_two)
    cos_ramp, sin_ramp = phase_ramp(shifts, extent)
    ref_now = ref_spectrum
    binned = None
    weight = None
    for iteration in range(ITERS):
        weight, local_term = correlate(spectra, cos_ramp, sin_ramp, ref_now, inv_one, inv_two)
        summed = lax.psum(local_term, ("row", "col"))
        ref_now = normalize(summed)
        if iteration == 0:
            binned = accumulate(patterns, weight, bin_owner, bin_index)
    return (ref_now, weight, binned)


def solution(mesh):
    placed = (
        P(("row", "col"), None, None),
        P(),
        P(("row", "col"), None),
        P(("row", "col"), None),
        P(("row", "col")),
    )
    return jax.shard_map(
        on_device,
        mesh=mesh,
        in_specs=placed,
        out_specs=(P(), P(("row", "col")), P(("row", "col"), None, None)),
        check_vma=False,
    )
```

profile of v0, /device:TPU:1, one launch (start us, length us, event | category | flops | bytes accessed | tf_op | source)
XLA Modules:
  0.0 575.6 jit_solution(9456165543976182999)
XLA Ops:
  7.2 1.1 fusion.73
  9.3 1.1 sine_convert_fusion.1
  10.4 1.0 fusion.75
  11.4 1.1 slice_bitcast_fusion.4
  13.5 2.8 copy.32
  18.1 7.1 %fusion.16 = bf16[16,2,256,256]{2,3,1,0:T(8,128)(2,1)} fusion(bf16[16,256,256]{2,1,0:T(8,128)(2,1)} %param.5, bf16[1,2,256,256]{3,2,1,0:T(8,128)(2,1)} %get-tuple-element.25, bf16[1,2,256,256]{3,2,1,0:T(8,128)(2,1)} %get-tuple-element.24, bf16[256,1,256]{0,2,1:T(8,128)(2,1)S(1)} %get-tuple-element.31, bf16[256,1,256]{0,2,1:T(8,128)(2,1)S(1)} %get-tuple-element.32), kind=kOutput, calls=%fused_computation.34 | convolution fusion | flops 3226992640 | bytes 7077888 | tf_op jit(solution)/shard_map/otij,bjtk->boik/dot_general | solution.py:32
  25.2 22.7 %add_convert_fusion.1 = (bf16[16,1,256,256]{2,3,0,1:T(8,128)(2,1)}, bf16[16,1,256,256]{2,3,0,1:T(8,128)(2,1)}) fusion(f32[256,256]{0,1:T(8,128)S(1)} %copy.25, f32[256,256]{0,1:T(8,128)S(1)} %copy.23, bf16[16,2,256,256]{2,3,1,0:T(8,128)(2,1)} %fusion.16, s32[16,256]{1,0:T(8,128)S(1)} %get-tuple-element.33, s32[16,256]{1,0:T(8,128)S(1)} %get-tuple-element.34), kind=kLoop, calls=%fused_computation.57 | loop fusion | flops 31457280 | bytes 8945664 | tf_op jit(solution)/shard_map/convert.4
  48.0 6.3 %multiply_reduce_fusion.5 = (f32[16]{0:T(128)S(1)}, f32[16]{0:T(128)S(1)}) fusion(bf16[1,256,256]{2,1,0:T(8,128)(2,1)S(1)} %get-tuple-element.29, bf16[1,256,256]{2,1,0:T(8,128)(2,1)S(1)} %cosine_convert_fusion, bf16[16,1,256,256]{2,3,0,1:T(8,128)(2,1)} %get-tuple-element.17, bf16[16,1,256,256]{2,3,0,1:T(8,128)(2,1)} %get-tuple-element.16, ...), kind=kOutput, calls=%fused_computation.55 | convolution fusion | flops 3230007296 | bytes 4980864 | tf_op jit(solution)/shard_map/oij,bjol->bil/dot_general | solution.py:58
  54.3 22.4 %multiply_reduce_fusion.4 = (f32[256,256]{0,1:T(8,128)S(1)}, f32[256,256]{0,1:T(8,128)S(1)}, bf16[16,256,256]{1,2,0:T(8,128)(2,1)}) fusion(f32[16]{0:T(128)S(1)} %rsqrt_multiply_fusion.1, s32[16,256]{1,0:T(8,128)S(1)} %get-tuple-element.33, s32[16,256]{1,0:T(8,128)S(1)} %get-tuple-element.34, bf16[16,2,256,256]{2,3,1,0:T(8,128)(2,1)} %fusion.16, ...), kind=kLoop, calls=%fused_computation.54 | loop fusion | flops 30277632 | bytes 8945728 | tf_op jit(solution)/shard_map/reduce_sum | solution.py:66
  77.6 3.6 copy.57
  81.2 125.6 %all-reduce.5.cloned.1.call-done = f32[2,256,256]{1,2,0:T(8,128)} async-done(((f32[2,256,256]{1,2,0:T(8,128)}), f32[2,256,256]{1,2,0:T(8,128)}) %all-reduce.5.cloned.1.call-update) | async-done | bytes 524304 | tf_op jit(solution)/shard_map/psum | solution.py:103
  206.8 1.7 fusion.61
  209.1 1.1 broadcast_divide_fusion.1
  210.3 22.6 %add_convert_fusion = (bf16[16,1,256,256]{2,3,0,1:T(8,128)(2,1)}, bf16[16,1,256,256]{2,3,0,1:T(8,128)(2,1)}) fusion(f32[256,256]{0,1:T(8,128)S(1)} %get-tuple-element.19, f32[256,256]{0,1:T(8,128)S(1)} %get-tuple-element.18, bf16[16,2,256,256]{2,3,1,0:T(8,128)(2,1)} %fusion.16, s32[16,256]{1,0:T(8,128)S(1)} %get-tuple-element.33, ...), kind=kLoop, calls=%fused_computation.52 | loop fusion | flops 31457280 | bytes 8945664 | tf_op jit(solution)/shard_map/convert.2
  232.9 6.3 %multiply_reduce_fusion.2 = (f32[16]{0:T(128)S(1)}, f32[16]{0:T(128)S(1)}) fusion(bf16[1,256,256]{2,1,0:T(8,128)(2,1)S(1)} %get-tuple-element.29, bf16[1,256,256]{2,1,0:T(8,128)(2,1)S(1)} %cosine_convert_fusion, bf16[16,1,256,256]{2,3,0,1:T(8,128)(2,1)} %get-tuple-element.15, bf16[16,1,256,256]{2,3,0,1:T(8,128)(2,1)} %get-tuple-element.14, ...), kind=kOutput, calls=%fused_computation.50 | convolution fusion | flops 3230007296 | bytes 4980864 | tf_op jit(solution)/shard_map/oij,bjol->bil/dot_general | solution.py:58
  239.2 21.4 %multiply_reduce_fusion.1 = (f32[256,256]{0,1:T(8,128)S(1)}, f32[256,256]{0,1:T(8,128)S(1)}) fusion(f32[16]{0:T(128)S(1)} %rsqrt_multiply_fusion, s32[16,256]{1,0:T(8,128)S(1)} %get-tuple-element.33, s32[16,256]{1,0:T(8,128)S(1)} %get-tuple-element.34, bf16[16,2,256,256]{2,3,1,0:T(8,128)(2,1)} %fusion.16), kind=kLoop, calls=%fused_computation.49 | loop fusion | flops 27131904 | bytes 4751424 | tf_op jit(solution)/shard_map/reduce_sum | solution.py:66
  261.5 4.4 fusion.77
  267.9 120.6 %all-reduce.7.cloned.1.call-done = f32[2,256,256]{1,2,0:T(8,128)} async-done(((f32[2,256,256]{1,2,0:T(8,128)}), f32[2,256,256]{1,2,0:T(8,128)}) %all-reduce.7.cloned.1.call-update) | async-done | bytes 524304 | tf_op jit(solution)/shard_map/psum | solution.py:103
  388.5 1.7 fusion.59
  390.9 1.1 broadcast_divide_fusion
  392.0 1.0 copy.34
  393.0 173.2 %all-reduce.9.cloned.1.call-done = f32[32,65536]{1,0:T(8,128)} async-done(((f32[32,65536]{1,0:T(8,128)}), f32[32,65536]{1,0:T(8,128)}) %all-reduce.9.cloned.1.call-update) | async-done | bytes 8388624
  566.1 1.8 constant_dynamic-slice_fusion
  567.9 1.2 copy.87
  (32 shorter events, 6.9 us)
Async XLA Ops:
  7.2 199.6 %all-reduce.5.cloned.1.call-start = ((), (), s32[]{:S(2)}) async-start(), calls=%async_computation | async-start | bytes 1048576 | tf_op jit(solution)/shard_map/psum | solution.py:103
  25.2 22.7 %copy-start = (bf16[1,256,2,256]{1,3,2,0:T(8,128)(2,1)S(1)}, bf16[1,256,2,256]{1,3,2,0:T(8,128)(2,1)}, u32[]{:S(2)}) copy-start(bf16[1,256,2,256]{1,3,2,0:T(8,128)(2,1)} %get-tuple-element.22) | copy-start | bytes 786436
  25.2 22.7 %copy-start.1 = (bf16[1,256,2,256]{1,3,2,0:T(8,128)(2,1)S(1)}, bf16[1,256,2,256]{1,3,2,0:T(8,128)(2,1)}, u32[]{:S(2)}) copy-start(bf16[1,256,2,256]{1,3,2,0:T(8,128)(2,1)} %get-tuple-element.23) | copy-start | bytes 786436
  76.6 4.5 copy-start.3
  76.7 4.5 copy-start.4
  77.5 310.9 %all-reduce.7.cloned.1.call-start = ((), (), s32[]{:S(2)}) async-start(), calls=%async_computation.1 | async-start | bytes 1048576 | tf_op jit(solution)/shard_map/psum | solution.py:103
  239.2 26.8 %copy-start.2 = (f32[16]{0:T(128)}, f32[16]{0:T(128)S(1)}, u32[]{:S(2)}) copy-start(f32[16]{0:T(128)S(1)} %rsqrt_multiply_fusion) | copy-start | bytes 196
  261.5 304.7 %all-reduce.9.cloned.1.call-start = ((), (), s32[]{:S(2)}) async-start(), calls=%async_computation.2 | async-start | bytes 16777216
  266.0 0.7 copy-start.5
Sparse Core Ops, SparseCore 0:
  77.6 129.0 all-reduce.4
  261.6 126.8 all-reduce.6
  390.8 175.2 all-reduce.8
where the time goes:
time: 577 us; the launch traced here: 576 us
  waiting for transfers between devices  419 us (73%)
  other arithmetic  102 us (18%)
  matrix products  24.1 us (4%)
  between operations  16 us (3%)
  local copies, waits for them, and re-layouts  13.7 us (2%)
    psum x2, waiting for transfers between devices, on_device(): summed = lax.psum(local_term, ('row', 'col'))  246 us
    unnamed x4, waiting for transfers between devices  173 us
    another operation x2, other arithmetic  45.3 us
    reduce_sum x2, other arithmetic, correlate(): jnp.sum(weight[:, None, None] * aligned_re, axis=0)  43.8 us
    dot_general x2, matrix products, correlate(): jnp.einsum('oij,bjol->bil', inv_two, half_section, preferred_element_type...  12.6 us
    unnamed x18, local copies, waits for them, and re-layouts  11.6 us
  transfers between devices with their start and end apart: 3, of which 3 were waited for; matrix products, arithmetic and copies ran while one was open for 2% of the time, Pallas kernels for 0%

commit v1 on v0

v1 whole, which is shorter than its diff:
```python
import functools
import math

import jax
import jax.numpy as jnp
import ml_dtypes
import numpy as np
from jax import lax
from jax.experimental import pallas as pl
from jax.experimental.pallas import tpu as pltpu
from jax.sharding import PartitionSpec as P

BINS = 4
ITERS = 2
K = 256
HALF = K // 2
ROWS = HALF + 16
REACH = 16
SLICES = 32
BOTH = ("row", "col")
F32 = jnp.float32
BF16 = jnp.bfloat16


@functools.cache
def tables():
    index = np.arange(K)
    angle = ((index[:, None] * index[None, :]) % K).astype(np.float32) * np.float32(2.0 * math.pi / K)
    cosine = np.cos(angle).astype(ml_dtypes.bfloat16).astype(np.float32)
    sine = np.sin(angle).astype(ml_dtypes.bfloat16).astype(np.float32)
    fwd_one = np.concatenate([cosine, sine], axis=1)
    fwd_two = np.zeros((2 * ROWS, 2 * K), np.float32)
    fwd_two[: HALF + 1, :K] = cosine[: HALF + 1]
    fwd_two[: HALF + 1, K:] = -sine[: HALF + 1]
    fwd_two[ROWS : ROWS + HALF + 1, :K] = -sine[: HALF + 1]
    fwd_two[ROWS : ROWS + HALF + 1, K:] = -cosine[: HALF + 1]
    inv_one = np.block([[cosine, sine], [-sine, cosine]])
    inv_two = np.concatenate([2.0 * cosine[:, :HALF], -2.0 * sine[:, :HALF]], axis=1)
    inv_two[:, 0] = cosine[:, 0]
    inv_two[:, HALF] = cosine[:, HALF]
    flip = np.zeros((K, K), np.float32)
    flip[(K - index) % K, index] = 1.0
    step = np.arange(-REACH, REACH + 1)
    phase = 2.0 * math.pi / K * ((step[:, None] * index[None, :]) % K)
    across = np.zeros((2, 40, K), np.float32)
    across[0, : 2 * REACH + 1] = np.cos(phase)
    across[1, : 2 * REACH + 1] = -np.sin(phase)
    down = np.zeros((2, ROWS, 128), np.float32)
    down[:, :, :40] = across[:, :, :ROWS].transpose(0, 2, 1)
    half = lambda a: a.astype(ml_dtypes.bfloat16)
    return dict(
        fwd_one=half(fwd_one),
        fwd_two=half(fwd_two),
        inv_one=half(inv_one),
        inv_two=half(inv_two),
        flip=half(flip),
        across=across,
        down=down,
    )


def dot(a, b):
    return jnp.dot(a, b, preferred_element_type=F32)


def split(a):
    high = a.astype(BF16)
    return (high, (a - high.astype(F32)).astype(BF16))


def hermitian_part(ref_ref, flip_ref, now_ref):
    flip_rows = flip_ref[:ROWS, :]
    flip_lanes = flip_ref[...]
    for part, sign in ((0, 1.0), (1, -1.0)):
        turned = jnp.zeros((ROWS, K), F32)
        for piece in split(ref_ref[part]):
            turned = turned + dot(dot(flip_rows, piece).astype(BF16), flip_lanes)
        now_ref[part * ROWS : (part + 1) * ROWS, :] = 0.5 * (ref_ref[part, :ROWS, :] + sign * turned)


def unpack(sums_ref, flip_ref):
    slices = sums_ref.shape[0]
    deep = 2 * HALF // slices
    rows = []
    for number in range(slices):
        piece = sums_ref[number].astype(F32)
        rows.append(jnp.concatenate([piece[:deep], piece[deep:]], axis=1))
    whole = jnp.concatenate(rows, axis=0)
    real, imag = whole[:HALF], whole[HALF:]
    first = jnp.concatenate([real[:8], imag[:8]], axis=0)
    turned = dot(first.astype(BF16), flip_ref[...])
    zero_re, zero_im = real[:1], imag[:1]
    turn_re, turn_im = turned[:1], turned[8:9]
    power = (
        2.0 * jnp.sum(whole * whole, axis=(0, 1), keepdims=True)
        - jnp.sum(zero_re * zero_re + zero_im * zero_im, axis=(0, 1), keepdims=True)
    ) * (1.0 / (K * K))
    is_first = lax.broadcasted_iota(jnp.int32, (HALF, K), 0) == 0
    real = jnp.where(is_first, 0.5 * (zero_re + turn_re), real)
    imag = jnp.where(is_first, 0.5 * (zero_im - turn_im), imag)
    last_re = 0.5 * (zero_im + turn_im)
    last_im = 0.5 * (turn_re - zero_re)
    return (real, imag, last_re, last_im, lax.rsqrt(power + 1e-06))


def pack(total_ref, out_ref):
    slices = out_ref.shape[0]
    deep = 2 * HALF // slices
    is_first = lax.broadcasted_iota(jnp.int32, (HALF, K), 0) == 0
    real = total_ref[:HALF, :]
    imag = total_ref[ROWS : ROWS + HALF, :]
    last_re = total_ref[HALF : HALF + 1, :]
    last_im = total_ref[ROWS + HALF : ROWS + HALF + 1, :]
    whole = jnp.concatenate(
        [jnp.where(is_first, real - last_im, real), jnp.where(is_first, imag + last_re, imag)], axis=0
    )
    for number in range(slices):
        piece = whole[number * deep : (number + 1) * deep]
        out_ref[number] = jnp.concatenate([piece[:, :128], piece[:, 128:]], axis=0).astype(BF16)


def correlate(spec, now_ref, inv_one_ref, inv_two_ref):
    spec_re, spec_im = spec[:ROWS].astype(F32), spec[ROWS:].astype(F32)
    now_re, now_im = now_ref[:ROWS, :], now_ref[ROWS:, :]
    cross = jnp.concatenate(
        [spec_re * now_re + spec_im * now_im, spec_im * now_re - spec_re * now_im], axis=1
    ).astype(BF16)
    mid = dot(cross, inv_one_ref[...])
    is_first = lax.broadcasted_iota(jnp.int32, (HALF, K), 0) == 0
    lower = jnp.where(is_first, mid[HALF : HALF + 1, :K], mid[:HALF, K:])
    mid = jnp.concatenate([mid[:HALF, :K], lower], axis=0).astype(BF16)
    corr = dot(inv_two_ref[...], mid)
    peak = jnp.max(corr, axis=(0, 1), keepdims=True) * (1.0 / (K * K))
    mean = jnp.sum(corr * corr, axis=(0, 1), keepdims=True) * (1.0 / float(K) ** 6)
    return peak / jnp.sqrt(mean + 1e-06)


def add_aligned(spec, weight, shift, down_ref, across_ref, total):
    index_y, index_x = shift
    lane = jnp.full((ROWS, 128), index_y, jnp.int32)
    down_re = weight * jnp.take_along_axis(down_ref[0], lane, axis=1, mode="promise_in_bounds")
    down_im = weight * jnp.take_along_axis(down_ref[1], lane, axis=1, mode="promise_in_bounds")
    down_re = jnp.concatenate([down_re, down_re], axis=1)
    down_im = jnp.concatenate([down_im, down_im], axis=1)
    across_re = across_ref[0, pl.ds(index_x, 1), :]
    across_im = across_ref[1, pl.ds(index_x, 1), :]
    ramp_re = down_re * across_re - down_im * across_im
    ramp_im = down_re * across_im + down_im * across_re
    spec_re, spec_im = spec[:ROWS].astype(F32), spec[ROWS:].astype(F32)
    return (
        total[0] + (spec_re * ramp_re - spec_im * ramp_im),
        total[1] + (spec_im * ramp_re + spec_re * ramp_im),
    )


def gather_step(specs, shifts_ref, first, now_ref, inv_one_ref, inv_two_ref, down_ref, across_ref, total_ref, weight_ref):
    total = (total_ref[:ROWS, :], total_ref[ROWS:, :])
    for number, spec in enumerate(specs):
        weight = correlate(spec, now_ref, inv_one_ref, inv_two_ref)
        weight_ref[pl.ds(first + number, 1), :] = jnp.broadcast_to(weight, (1, 128))
        shift = (shifts_ref[first + number, 0] + REACH, shifts_ref[first + number, 1] + REACH)
        total = add_aligned(spec, weight, shift, down_ref, across_ref, total)
    total_ref[:ROWS, :] = total[0]
    total_ref[ROWS:, :] = total[1]


def first_kernel(
    shifts_ref, pattern_ref, ref_ref, fwd_one_ref, fwd_two_ref, inv_one_ref, inv_two_ref, flip_ref, down_ref, across_ref,
    spec_ref, sums_ref, weight_ref, now_ref, total_ref, mid_ref,
):
    step = pl.program_id(0)
    count = pattern_ref.shape[0]

    @pl.when(step == 0)
    def _():
        hermitian_part(ref_ref, flip_ref, now_ref)
        total_ref[...] = jnp.zeros_like(total_ref)

    specs = []
    for number in range(count):
        half = dot(pattern_ref[number], fwd_one_ref[...]).astype(BF16)
        mid_ref[number, :K, :] = half[:, :K]
        mid_ref[number, K:, :] = half[:, K:]
        spec = dot(fwd_two_ref[...], mid_ref[number]).astype(BF16)
        spec_ref[number] = spec
        specs.append(spec)
    gather_step(
        specs, shifts_ref, step * count, now_ref, inv_one_ref, inv_two_ref, down_ref, across_ref, total_ref, weight_ref
    )

    @pl.when(step == pl.num_programs(0) - 1)
    def _():
        pack(total_ref, sums_ref)


def second_kernel(
    shifts_ref, spec_ref, old_ref, inv_one_ref, inv_two_ref, flip_ref, down_ref, across_ref,
    sums_ref, weight_ref, now_ref, total_ref,
):
    step = pl.program_id(0)
    count = spec_ref.shape[0]

    @pl.when(step == 0)
    def _():
        real, imag, last_re, last_im, scale = unpack(old_ref, flip_ref)
        is_first = lax.broadcasted_iota(jnp.int32, (ROWS - HALF, K), 0) == 0
        now_ref[:HALF, :] = real * scale
        now_ref[HALF:ROWS, :] = jnp.where(is_first, last_re * scale, 0.0)
        now_ref[ROWS : ROWS + HALF, :] = imag * scale
        now_ref[ROWS + HALF :, :] = jnp.where(is_first, last_im * scale, 0.0)
        total_ref[...] = jnp.zeros_like(total_ref)

    specs = [spec_ref[number] for number in range(count)]
    gather_step(
        specs, shifts_ref, step * count, now_ref, inv_one_ref, inv_two_ref, down_ref, across_ref, total_ref, weight_ref
    )

    @pl.when(step == pl.num_programs(0) - 1)
    def _():
        pack(total_ref, sums_ref)


def last_kernel(old_ref, flip_ref, out_ref):
    real, imag, last_re, last_im, scale = unpack(old_ref, flip_ref)
    out_ref[0, :HALF, :] = real * scale
    out_ref[1, :HALF, :] = imag * scale
    row = lax.broadcasted_iota(jnp.int32, (HALF, HALF), 0)
    column = lax.broadcasted_iota(jnp.int32, (HALF, HALF), 1)
    turn = jnp.where(row + column == HALF, 1.0, 0.0).astype(BF16)
    is_first = lax.broadcasted_iota(jnp.int32, (HALF, K), 0) == 0
    for part, (body, row_128) in enumerate(((real, last_re), (imag, last_im))):
        turned = dot(dot(turn, body.astype(BF16)).astype(BF16), flip_ref[...])
        turned = turned if part == 0 else -turned
        out_ref[part, HALF:, :] = jnp.where(is_first, row_128, turned) * scale


def add_kernel(in_ref, out_ref):
    total = in_ref[0].astype(F32)
    for number in range(1, in_ref.shape[0]):
        total = total + in_ref[number].astype(F32)
    total = total.astype(BF16)
    for number in range(out_ref.shape[0]):
        out_ref[number] = total


def bin_kernel(target_ref, pattern_ref, weight_ref, mine_ref, other_ref, total_ref):
    bins = mine_ref.shape[0]
    total_ref[...] = jnp.zeros_like(total_ref)
    for number in range(pattern_ref.shape[0]):
        weight = weight_ref[number : number + 1, :]
        weight = jnp.concatenate([weight, weight], axis=1)
        scaled = (weight * pattern_ref[number].astype(F32)).astype(BF16).astype(F32)
        slot = target_ref[number]
        total_ref[pl.ds(slot, 1)] += scaled[None]
    for number in range(bins):
        mine_ref[number] = total_ref[number].astype(BF16)
        other_ref[number] = total_ref[bins + number].astype(BF16)


def whole(array):
    return pl.BlockSpec(array.shape, lambda *_: (0,) * array.ndim)


PARAMS = pltpu.CompilerParams(vmem_limit_bytes=48 * 1024 * 1024)


def run_first(patterns, ref_spectrum, shifts, slices, block):
    t = tables()
    constants = [jnp.asarray(t[name]) for name in ("fwd_one", "fwd_two", "inv_one", "inv_two", "flip", "down", "across")]
    count = patterns.shape[0]
    return pl.pallas_call(
        first_kernel,
        out_shape=(
            jax.ShapeDtypeStruct((count, 2 * ROWS, K), BF16),
            jax.ShapeDtypeStruct((slices, 2 * K * K // 2 // slices // 128, 128), BF16),
            jax.ShapeDtypeStruct((count, 128), F32),
        ),
        grid_spec=pltpu.PrefetchScalarGridSpec(
            num_scalar_prefetch=1,
            grid=(count // block,),
            in_specs=[pl.BlockSpec((block, K, K), lambda i, s: (i, 0, 0)), whole(ref_spectrum)]
            + [whole(c) for c in constants],
            out_specs=(
                pl.BlockSpec((block, 2 * ROWS, K), lambda i, s: (i, 0, 0)),
                pl.BlockSpec((slices, 2 * K * K // 2 // slices // 128, 128), lambda i, s: (0, 0, 0)),
                pl.BlockSpec((count, 128), lambda i, s: (0, 0)),
            ),
            scratch_shapes=[
                pltpu.VMEM((2 * ROWS, K), F32),
                pltpu.VMEM((2 * ROWS, K), F32),
                pltpu.VMEM((block, 2 * K, K), BF16),
            ],
        ),
        compiler_params=PARAMS,
        cost_estimate=pl.CostEstimate(flops=int(5e9), bytes_accessed=int(8e6), transcendentals=0),
        name="forward_and_correlate",
    )(shifts, patterns, ref_spectrum, *constants)


def run_second(spectra, sums, shifts, block):
    t = tables()
    constants = [jnp.asarray(t[name]) for name in ("inv_one", "inv_two", "flip", "down", "across")]
    count = spectra.shape[0]
    return pl.pallas_call(
        second_kernel,
        out_shape=(jax.ShapeDtypeStruct(sums.shape, BF16), jax.ShapeDtypeStruct((count, 128), F32)),
        grid_spec=pltpu.PrefetchScalarGridSpec(
            num_scalar_prefetch=1,
            grid=(count // block,),
            in_specs=[pl.BlockSpec((block, 2 * ROWS, K), lambda i, s: (i, 0, 0)), whole(sums)]
            + [whole(c) for c in constants],
            out_specs=(
                pl.BlockSpec(sums.shape, lambda i, s: (0, 0, 0)),
                pl.BlockSpec((count, 128), lambda i, s: (0, 0)),
            ),
            scratch_shapes=[pltpu.VMEM((2 * ROWS, K), F32), pltpu.VMEM((2 * ROWS, K), F32)],
        ),
        compiler_params=PARAMS,
        cost_estimate=pl.CostEstimate(flops=int(3e9), bytes_accessed=int(4e6), transcendentals=0),
        name="correlate_again",
    )(shifts, spectra, sums, *constants)


def run_last(sums):
    flip = jnp.asarray(tables()["flip"])
    return pl.pallas_call(
        last_kernel, out_shape=jax.ShapeDtypeStruct((2, K, K), F32), compiler_params=PARAMS, name="finish"
    )(sums, flip)


def sum_over_all(sums):
    devices = lax.axis_size("row") * lax.axis_size("col")
    pieces = sums.reshape(devices, sums.size // devices // 128, 128)
    pieces = lax.all_to_all(pieces, BOTH, 0, 0, tiled=True)
    pieces = pl.pallas_call(
        add_kernel, out_shape=jax.ShapeDtypeStruct(pieces.shape, BF16), compiler_params=PARAMS, name="add_pieces"
    )(pieces)
    return lax.all_to_all(pieces, BOTH, 0, 0, tiled=True).reshape(sums.shape)


def run_bins(patterns, weights, targets, bins, deep):
    count = patterns.shape[0]
    part = jax.ShapeDtypeStruct((bins // 2, K, K), BF16)
    return pl.pallas_call(
        bin_kernel,
        out_shape=(part, part),
        grid_spec=pltpu.PrefetchScalarGridSpec(
            num_scalar_prefetch=1,
            grid=(K // deep,),
            in_specs=[
                pl.BlockSpec((count, deep, K), lambda i, s: (0, i, 0)),
                pl.BlockSpec((count, 128), lambda i, s: (0, 0)),
            ],
            out_specs=(
                pl.BlockSpec((bins // 2, deep, K), lambda i, s: (0, i, 0)),
                pl.BlockSpec((bins // 2, deep, K), lambda i, s: (0, i, 0)),
            ),
            scratch_shapes=[pltpu.VMEM((bins, deep, K), F32)],
        ),
        compiler_params=PARAMS,
        cost_estimate=pl.CostEstimate(flops=int(4e6), bytes_accessed=int(8e6), transcendentals=0),
        name="bin_partials",
    )(targets, patterns, weights)


def on_device(patterns, ref_spectrum, shifts, bin_owner, bin_index):
    columns = lax.axis_size("col")
    slices = SLICES
    me = lax.axis_index("col")
    owner = bin_owner.reshape(-1)
    pairs = columns // 2
    targets = ((owner % 2) ^ (me % 2)) * (pairs * BINS) + (owner // 2) * BINS + bin_index

    spectra, sums, first_weight = run_first(patterns, ref_spectrum, shifts, slices, 2)
    total = sum_over_all(sums)
    mine, other = run_bins(patterns, first_weight, targets, columns * BINS, 32)
    other = lax.ppermute(other, "col", [(i, i ^ 1) for i in range(columns)])
    chip = (mine.astype(F32) + other.astype(F32)).astype(BF16)
    groups = [list(range(core, columns, 2)) for core in range(2)]
    arrived = lax.all_to_all(chip, "col", 0, 0, axis_index_groups=groups, tiled=True)
    binned = arrived.reshape(pairs, BINS, K, K).astype(F32).sum(axis=0)

    sums, weight = run_second(spectra, total, shifts, 2)
    total = sum_over_all(sums)
    return (run_last(total), weight[:, 0], binned)


def solution(mesh):
    placed = (P(BOTH, None, None), P(), P(BOTH, None), P(BOTH, None), P(BOTH))
    return jax.shard_map(
        on_device,
        mesh=mesh,
        in_specs=placed,
        out_specs=(P(), P(BOTH), P(BOTH, None, None)),
        check_vma=False,
    )
```

time: 577 us -> 144 us (0.25)
  waiting for transfers between devices: 419 us -> 51 us
  other arithmetic: 102 us -> 5.5 us
  blocking collectives: 0 us -> 34.9 us
  Pallas kernels: 0 us -> 31.4 us
  matrix products: 24.1 us -> 0 us
  between operations: 16 us -> 0.74 us
  starting transfers between devices: 0.12 us -> 6.04 us
    psum x2 -> x0, waiting for transfers between devices: 246 us -> none  [on_device(): summed = lax.psum(local_term, ('row', 'col'))]
    unnamed x4 -> x0, waiting for transfers between devices: 173 us -> none
    all_to_all x0 -> x2, waiting for transfers between devices: none -> 51 us  [the longest x1 46.2 us: on_device(): lax.all_to_all(chip, 'col', 0, 0, axis_index_groups=groups, tiled=True)]
    another operation x6 -> x0, other arithmetic: 48.7 us -> none
    reduce_sum x4 -> x1, other arithmetic: 47.2 us -> 1.25 us  [on_device(): binned = arrived.reshape(pairs, BINS, K, K).astype(F32).sum(axis=0)]
    all_to_all x0 -> x3, blocking collectives: none -> 34.9 us  [the longest x2 25.1 us: sum_over_all(): pieces = lax.all_to_all(pieces, BOTH, 0, 0, tiled=True)]
    pallas_call x0 -> x6, Pallas kernels: none -> 31.4 us  [the longest x1 13.7 us: run_first(): pl.pallas_call(first_kernel, out_shape=(jax.ShapeDtypeStruct((count, 2 *...]
    dot_general x4 -> x0, matrix products: 24.1 us -> none  [the longest x2 12.6 us: correlate(): jnp.einsum('oij,bjol->bil', inv_two, half_section, preferred_element_type...]
  transfers between devices with their start and end apart: 3 -> 3, of which waited for: 3 -> 2; matrix products, arithmetic and copies ran while one was open for 2% -> 3% of each run, Pallas kernels for 0% -> 8%
where the time goes in v1:
time: 144 us; the launch traced here: 142 us
  waiting for transfers between devices  51 us (35%)
  blocking collectives  34.9 us (24%)
  Pallas kernels  31.4 us (22%)
  local copies, waits for them, and re-layouts  12.2 us (8%)
  starting transfers between devices  6.04 us (4%)
  other arithmetic  5.5 us (4%)
    all_to_all x1, waiting for transfers between devices, on_device(): lax.all_to_all(chip, 'col', 0, 0, axis_index_groups=groups, tiled=True)  46.2 us
    all_to_all x2, blocking collectives, sum_over_all(): pieces = lax.all_to_all(pieces, BOTH, 0, 0, tiled=True)  25.1 us
    pallas_call x1, Pallas kernels, run_first(): pl.pallas_call(first_kernel, out_shape=(jax.ShapeDtypeStruct((count, 2 *...  13.7 us
    unnamed x31, local copies, waits for them, and re-layouts  11.6 us
    all_to_all x1, blocking collectives, sum_over_all(): return lax.all_to_all(pieces, BOTH, 0, 0, tiled=True).reshape(sums.shape)  9.88 us
    pallas_call x1, Pallas kernels, run_second(): pl.pallas_call(second_kernel, out_shape=(jax.ShapeDtypeStruct(sums.shape,...  8.69 us
    pallas_call x1, Pallas kernels, run_bins(): pl.pallas_call(bin_kernel, out_shape=(part, part), grid_spec=pltpu.Prefet...  7.03 us
    all_to_all x1, waiting for transfers between devices, sum_over_all(): return lax.all_to_all(pieces, BOTH, 0, 0, tiled=True).reshape(sums.shape)  4.8 us
  transfers between devices with their start and end apart: 3, of which 2 were waited for; matrix products, arithmetic and copies ran while one was open for 3% of the time, Pallas kernels for 8%

profile of v1, /device:TPU:1, one launch (start us, length us, event | category | flops | bytes accessed | tf_op | source)
XLA Modules:
  0.0 141.9 jit_solution(16456626654485487169)
XLA Ops:
  0.6 0.8 copy.18.shifts_ref
  2.1 1.6 %copy-done = bf16[16,256,256]{2,1,0:T(8,128)(2,1)S(1)} copy-done((bf16[16,256,256]{2,1,0:T(8,128)(2,1)S(1)}, bf16[16,256,256]{2,1,0:T(8,128)(2,1)}, u32[]{:S(2)}) %copy-start) | copy-done | bytes 2097176
  3.7 0.9 copy-done.1
  4.6 1.0 copy-done.3
  5.6 1.0 copy-done.4
  6.7 1.0 copy-done.6
  7.6 0.9 copy-done.7
  8.6 0.9 copy-done.8
  9.5 0.9 copy-done.10
  10.4 0.9 copy-done.12
  11.3 13.7 %forward_and_correlate.1 = (bf16[16,288,256]{2,1,0:T(8,128)(2,1)}, bf16[32,16,128]{2,1,0:T(8,128)(2,1)S(1)}, f32[16,128]{1,0:T(8,128)S(1)}) custom-call(s32[16,2]{1,0:T(8,128)S(1)} %copy.18.shifts_ref, bf16[16,256,256]{2,1,0:T(8,128)(2,1)S(1)} %copy-done, f32[2,256,256]{2,1,0:T(8,128)S(1)} %copy-done.3, bf16[256,512]{1,0:T(8,128)(2,1)S(1)} %copy-done.7, ...), custom_call_target="tpu_custom_call" | custom-call | flops 5000000000 | bytes 8000000 | tf_op jit(solution)/shard_map/forward_and_correlate/pallas_call | solution.py:271
  25.0 7.0 %bin_partials.1 = (bf16[16,256,256]{2,1,0:T(8,128)(2,1)S(1)}, bf16[16,256,256]{2,1,0:T(8,128)(2,1)}) custom-call(s32[16]{0:T(128)S(1)} %fusion.3.target_ref, bf16[16,256,256]{2,1,0:T(8,128)(2,1)} %pattern_ref.3, f32[16,128]{1,0:T(8,128)S(1)} %get-tuple-element.14.weight_ref), custom_call_target="tpu_custom_call" | custom-call | flops 4000000 | bytes 8000000 | tf_op jit(solution)/shard_map/bin_partials/pallas_call | solution.py:344
  32.1 15.2 %all_to_all.25.in_ref = bf16[32,16,128]{2,1,0:T(8,128)(2,1)S(1)} all-to-all(bf16[32,16,128]{2,1,0:T(8,128)(2,1)S(1)} %get-tuple-element.11), channel_id=1, replica_groups=mesh['row'=4,'col'=8] {'row','col'}, dimensions={0} | all-to-all | bytes 262144 | tf_op jit(solution)/shard_map/all_to_all | solution.py:334
  47.3 9.9 %all_to_all.26.old_ref = bf16[32,16,128]{2,1,0:T(8,128)(2,1)S(1)} all-to-all(bf16[32,16,128]{2,1,0:T(8,128)(2,1)S(1)} %add_pieces.2), channel_id=1, replica_groups=mesh['row'=4,'col'=8] {'row','col'}, dimensions={0} | all-to-all | bytes 262144 | tf_op jit(solution)/shard_map/all_to_all | solution.py:338
  57.2 1.7 %copy-done.14 = bf16[16,288,256]{2,1,0:T(8,128)(2,1)S(1)} copy-done((bf16[16,288,256]{2,1,0:T(8,128)(2,1)S(1)}, bf16[16,288,256]{2,1,0:T(8,128)(2,1)}, u32[]{:S(2)}) %copy-start.14) | copy-done | bytes 2359320
  58.9 8.7 %correlate_again.1 = (bf16[32,16,128]{2,1,0:T(8,128)(2,1)S(1)}, f32[16,128]{1,0:T(8,128)S(1)}) custom-call(s32[16,2]{1,0:T(8,128)S(1)} %copy.18.shifts_ref, bf16[16,288,256]{2,1,0:T(8,128)(2,1)S(1)} %copy-done.14, bf16[32,16,128]{2,1,0:T(8,128)(2,1)S(1)} %all_to_all.26.old_ref, bf16[512,512]{1,0:T(8,128)(2,1)S(1)} %copy-done.5, ...), custom_call_target="tpu_custom_call" | custom-call | flops 3000000000 | bytes 4000000 | tf_op jit(solution)/shard_map/correlate_again/pallas_call | solution.py:304
  67.6 9.9 %all_to_all.27.in_ref = bf16[32,16,128]{2,1,0:T(8,128)(2,1)S(1)} all-to-all(bf16[32,16,128]{2,1,0:T(8,128)(2,1)S(1)} %get-tuple-element.12), channel_id=1, replica_groups=mesh['row'=4,'col'=8] {'row','col'}, dimensions={0} | all-to-all | bytes 262144 | tf_op jit(solution)/shard_map/all_to_all | solution.py:334
  78.1 2.4 %all-to-all-start.3 = ((bf16[32,16,128]{2,1,0:T(8,128)(2,1)}), bf16[32,16,128]{2,1,0:T(8,128)(2,1)S(1)}, u32[]{:S(2)}, u32[]{:S(2)}) async-start(bf16[32,16,128]{2,1,0:T(8,128)(2,1)} %add_pieces.3), calls=%async_computation.3 | async-start | bytes 262144 | tf_op jit(solution)/shard_map/all_to_all | solution.py:338
  80.5 3.6 %add_convert_fusion = bf16[16,256,256]{2,1,0:T(8,128)(2,1)} fusion(bf16[16,256,256]{2,1,0:T(8,128)(2,1)} %collective-permute-done, bf16[16,256,256]{2,1,0:T(8,128)(2,1)S(1)} %get-tuple-element.15), kind=kLoop, calls=%fused_computation.1 | loop fusion | flops 4194304 | bytes 6291456 | tf_op jit(solution)/shard_map/convert_element_type | solution.py:378
  84.1 4.8 %all-to-all-done.3.old_ref = bf16[32,16,128]{2,1,0:T(8,128)(2,1)S(1)} async-done(((bf16[32,16,128]{2,1,0:T(8,128)(2,1)}), bf16[32,16,128]{2,1,0:T(8,128)(2,1)S(1)}, u32[]{:S(2)}, u32[]{:S(2)}) %all-to-all-start.3) | async-done | bytes 131104 | tf_op jit(solution)/shard_map/all_to_all | solution.py:338
  88.9 3.6 %all-to-all-start.4 = ((bf16[16,256,256]{2,1,0:T(8,128)(2,1)}), bf16[16,256,256]{2,1,0:T(8,128)(2,1)S(1)}, u32[]{:S(2)}, u32[]{:S(2)}) async-start(bf16[16,256,256]{2,1,0:T(8,128)(2,1)} %add_convert_fusion), calls=%async_computation.4 | async-start | bytes 4194304 | tf_op jit(solution)/shard_map/all_to_all | solution.py:380
  93.1 1.3 finish.1
  94.4 46.2 %all-to-all-done.4 = bf16[16,256,256]{2,1,0:T(8,128)(2,1)S(1)} async-done(((bf16[16,256,256]{2,1,0:T(8,128)(2,1)}), bf16[16,256,256]{2,1,0:T(8,128)(2,1)S(1)}, u32[]{:S(2)}, u32[]{:S(2)}) %all-to-all-start.4) | async-done | bytes 2097184 | tf_op jit(solution)/shard_map/all_to_all | solution.py:380
  140.6 1.3 convert_reduce_fusion
  (26 shorter events, 2.2 us)
Async XLA Ops:
  2.1 1.6 %copy-start = (bf16[16,256,256]{2,1,0:T(8,128)(2,1)S(1)}, bf16[16,256,256]{2,1,0:T(8,128)(2,1)}, u32[]{:S(2)}) copy-start(bf16[16,256,256]{2,1,0:T(8,128)(2,1)} %pattern_ref.3) | copy-start | bytes 6291460
  3.7 0.9 copy-start.1
  4.6 1.0 copy-start.3
  5.6 1.0 copy-start.4
  6.7 1.0 copy-start.6
  7.6 0.9 copy-start.7
  8.6 0.9 copy-start.8
  9.5 0.9 copy-start.10
  10.4 0.9 copy-start.12
  24.9 32.2 %copy-start.2 = (bf16[256,256]{1,0:T(8,128)(2,1)S(1)}, bf16[256,256]{1,0:T(8,128)(2,1)}, u32[]{:S(2)}) copy-start(bf16[256,256]{1,0:T(8,128)(2,1)} %constant.60.clone.flip_ref) | copy-start | bytes 393220
  24.9 32.2 %copy-start.5 = (bf16[512,512]{1,0:T(8,128)(2,1)S(1)}, bf16[512,512]{1,0:T(8,128)(2,1)}, u32[]{:S(2)}) copy-start(bf16[512,512]{1,0:T(8,128)(2,1)} %constant.58.clone.inv_one_ref) | copy-start | bytes 1572868
  24.9 32.2 %copy-start.9 = (f32[2,144,128]{2,1,0:T(8,128)S(1)}, f32[2,144,128]{2,1,0:T(8,128)}, u32[]{:S(2)}) copy-start(f32[2,144,128]{2,1,0:T(8,128)} %constant.61.clone.down_ref) | copy-start | bytes 442372
  24.9 32.2 %copy-start.11 = (bf16[256,256]{1,0:T(8,128)(2,1)S(1)}, bf16[256,256]{1,0:T(8,128)(2,1)}, u32[]{:S(2)}) copy-start(bf16[256,256]{1,0:T(8,128)(2,1)} %constant.59.clone.inv_two_ref) | copy-start | bytes 393220
  25.0 32.2 %copy-start.13 = (f32[2,40,256]{2,1,0:T(8,128)S(1)}, f32[2,40,256]{2,1,0:T(8,128)}, u32[]{:S(2)}) copy-start(f32[2,40,256]{2,1,0:T(8,128)} %constant.62.clone.across_ref) | copy-start | bytes 245764
  32.0 48.5 %collective-permute-start = (bf16[16,256,256]{2,1,0:T(8,128)(2,1)}, bf16[16,256,256]{2,1,0:T(8,128)(2,1)}, u32[]{:S(2)}, u32[]{:S(2)}) collective-permute-start(bf16[16,256,256]{2,1,0:T(8,128)(2,1)} %get-tuple-element.16), channel_id=1, source_target_pairs={{0,1},{1,0},{2,3},{3,2},{4,5},{5,4},{6,7},{7,6},{8,9},{9,8},{10,11... | collective-permute-start | bytes 6291464 | tf_op jit(solution)/shard_map/ppermute | solution.py:377
  57.2 1.7 %copy-start.14 = (bf16[16,288,256]{2,1,0:T(8,128)(2,1)S(1)}, bf16[16,288,256]{2,1,0:T(8,128)(2,1)}, u32[]{:S(2)}) copy-start(bf16[16,288,256]{2,1,0:T(8,128)(2,1)} %get-tuple-element.10.spec_ref) | copy-start | bytes 7077892
  78.1 10.8 %all-to-all-start.3 = ((bf16[32,16,128]{2,1,0:T(8,128)(2,1)}), bf16[32,16,128]{2,1,0:T(8,128)(2,1)S(1)}, u32[]{:S(2)}, u32[]{:S(2)}) async-start(bf16[32,16,128]{2,1,0:T(8,128)(2,1)} %add_pieces.3), calls=%async_computation.3 | async-start | bytes 262144 | tf_op jit(solution)/shard_map/all_to_all | solution.py:338
  88.9 51.7 %all-to-all-start.4 = ((bf16[16,256,256]{2,1,0:T(8,128)(2,1)}), bf16[16,256,256]{2,1,0:T(8,128)(2,1)S(1)}, u32[]{:S(2)}, u32[]{:S(2)}) async-start(bf16[16,256,256]{2,1,0:T(8,128)(2,1)} %add_convert_fusion), calls=%async_computation.4 | async-start | bytes 4194304 | tf_op jit(solution)/shard_map/all_to_all | solution.py:380

commit v2 on v0

v2 whole, which is shorter than its diff:
```python
import functools
import math

import jax
import jax.numpy as jnp
import ml_dtypes
import numpy as np
from jax import lax
from jax.experimental import pallas as pl
from jax.experimental.pallas import tpu as pltpu
from jax.sharding import PartitionSpec as P

BINS = 4
ITERS = 2
K = 256
HALF = K // 2
ROWS = HALF + 16
REACH = 16
DEEP = 8
SLICES = HALF // DEEP
BOTH = ("row", "col")
F32 = jnp.float32
BF16 = jnp.bfloat16


@functools.cache
def tables():
    index = np.arange(K)
    angle = ((index[:, None] * index[None, :]) % K).astype(np.float32) * np.float32(2.0 * math.pi / K)
    cosine = np.cos(angle).astype(ml_dtypes.bfloat16).astype(np.float32)
    sine = np.sin(angle).astype(ml_dtypes.bfloat16).astype(np.float32)
    order = np.concatenate([index[:HALF], [HALF], K - index[1:HALF]])
    fwd_one = np.concatenate([cosine[:, : HALF + 1], sine[:, 1:HALF]], axis=1)
    fwd_two = np.zeros((2 * ROWS, K), np.float32)
    fwd_two[: HALF + 1] = cosine[: HALF + 1]
    fwd_two[ROWS : ROWS + HALF + 1] = -sine[: HALF + 1]
    inv_one = np.block([[cosine[order], sine[order]], [-sine[order], cosine[order]]])
    inv_two = np.concatenate([2.0 * cosine[:, :HALF], -2.0 * sine[:, :HALF]], axis=1)
    inv_two[:, 0] = cosine[:, 0]
    inv_two[:, HALF] = cosine[:, HALF]
    reorder = np.zeros((K, K), np.float32)
    reorder[order, index] = 1.0
    turn = np.zeros((ROWS, K), np.float32)
    turn[index[: HALF + 1], (K - index[: HALF + 1]) % K] = 1.0
    step = np.arange(-REACH, REACH + 1)
    phase = 2.0 * math.pi / K * ((step[:, None] * index[None, :]) % K)
    across = np.zeros((2, 40, K), np.float32)
    across[0, : 2 * REACH + 1] = np.cos(phase)[:, order]
    across[1, : 2 * REACH + 1] = -np.sin(phase)[:, order]
    down = np.zeros((2, ROWS, 128), np.float32)
    down[0, : HALF + 1, : 2 * REACH + 1] = np.cos(phase)[:, : HALF + 1].T
    down[1, : HALF + 1, : 2 * REACH + 1] = -np.sin(phase)[:, : HALF + 1].T
    half = lambda a: a.astype(ml_dtypes.bfloat16)
    return dict(
        fwd_one=half(fwd_one),
        fwd_two=half(fwd_two),
        inv_one=half(inv_one),
        inv_two=half(inv_two),
        reorder=half(reorder),
        back=half(reorder.T.copy()),
        turn=half(turn),
        across=across,
        down=down,
    )


def dot(a, b):
    return jnp.dot(a, b, preferred_element_type=F32)


def split(a):
    high = a.astype(BF16)
    return (high, (a - high.astype(F32)).astype(BF16))


def negate_columns(a):
    turned = jnp.concatenate([a[:, HALF:], a[:, :HALF]], axis=1)
    lane = lax.broadcasted_iota(jnp.int32, a.shape, 1)
    return jnp.where((lane == 0) | (lane == HALF), a, turned)


def hermitian_part(ref_ref, reorder_ref, turn_ref, now_ref):
    for part, sign in ((0, 1.0), (1, -1.0)):
        straight = jnp.zeros((ROWS, K), F32)
        turned = jnp.zeros((ROWS, K), F32)
        for piece in split(ref_ref[part]):
            piece = dot(piece, reorder_ref[...]).astype(BF16)
            straight = straight + piece[:ROWS].astype(F32)
            turned = turned + dot(turn_ref[...], piece)
        now_ref[part * ROWS : (part + 1) * ROWS, :] = 0.5 * (straight + sign * negate_columns(turned))


def unpack(core, keep_ref, other_ref):
    halves = []
    for ref in (keep_ref, other_ref):
        rows = []
        for number in range(SLICES):
            piece = ref[number].astype(F32)
            rows.append(jnp.concatenate([piece[:DEEP], piece[DEEP:]], axis=1))
        halves.append(jnp.concatenate(rows, axis=0))
    keep, other = halves
    real, imag = jnp.where(core == 0, keep, other), jnp.where(core == 0, other, keep)
    zero_re, zero_im = real[:1], imag[:1]
    turn_re, turn_im = negate_columns(real[:8])[:1], negate_columns(imag[:8])[:1]
    power = (
        2.0 * jnp.sum(real * real + imag * imag, axis=(0, 1), keepdims=True)
        - jnp.sum(zero_re * zero_re + zero_im * zero_im, axis=(0, 1), keepdims=True)
    ) * (1.0 / (K * K))
    is_first = lax.broadcasted_iota(jnp.int32, (HALF, K), 0) == 0
    real = jnp.where(is_first, 0.5 * (zero_re + turn_re), real)
    imag = jnp.where(is_first, 0.5 * (zero_im - turn_im), imag)
    last_re = 0.5 * (zero_im + turn_im)
    last_im = 0.5 * (turn_re - zero_re)
    return (real, imag, last_re, last_im, lax.rsqrt(power + 1e-06))


def pack(core, total_ref, keep_ref, send_ref):
    is_first = lax.broadcasted_iota(jnp.int32, (HALF, K), 0) == 0
    real = total_ref[:HALF, :]
    imag = total_ref[ROWS : ROWS + HALF, :]
    last_re = total_ref[HALF : HALF + 1, :]
    last_im = total_ref[ROWS + HALF : ROWS + HALF + 1, :]
    real, imag = jnp.where(is_first, real - last_im, real), jnp.where(is_first, imag + last_re, imag)
    for ref, half in ((keep_ref, jnp.where(core == 0, real, imag)), (send_ref, jnp.where(core == 0, imag, real))):
        for number in range(SLICES):
            piece = half[number * DEEP : (number + 1) * DEEP]
            ref[number] = jnp.concatenate([piece[:, :128], piece[:, 128:]], axis=0).astype(ref.dtype)


def forward(first, size, pattern_ref, spec_ref, fwd_one_ref, fwd_two_ref):
    flat = pattern_ref[pl.ds(first, size)].reshape(size * K, K)
    half = dot(flat, fwd_one_ref[...]).astype(BF16)
    is_zero = lax.broadcasted_iota(jnp.int32, (ROWS, HALF), 1) == 0
    for number in range(size):
        both = dot(fwd_two_ref[...], half[number * K : (number + 1) * K])
        cu, cv = both[:ROWS, :HALF], both[:ROWS, HALF:]
        su, sv = both[ROWS:, :HALF], both[ROWS:, HALF:]
        real = jnp.concatenate([cu + jnp.where(is_zero, 0.0, sv), jnp.where(is_zero, cv, cu - sv)], axis=1)
        imag = jnp.concatenate([su - jnp.where(is_zero, 0.0, cv), jnp.where(is_zero, sv, su + cv)], axis=1)
        spec_ref[first + number] = jnp.concatenate([real, imag], axis=0).astype(BF16)


def correlate(first, size, spec_ref, now_ref, cross_ref, inv_one_ref, inv_two_ref, weight_ref):
    for number in range(size):
        spec_re = spec_ref[first + number, :ROWS, :].astype(F32)
        spec_im = spec_ref[first + number, ROWS:, :].astype(F32)
        now_re, now_im = now_ref[:ROWS, :], now_ref[ROWS:, :]
        rows = slice(number * ROWS, (number + 1) * ROWS)
        cross_ref[rows, :K] = (spec_re * now_re + spec_im * now_im).astype(BF16)
        cross_ref[rows, K:] = (spec_im * now_re - spec_re * now_im).astype(BF16)
    both = dot(cross_ref[...], inv_one_ref[...])
    is_first = lax.broadcasted_iota(jnp.int32, (HALF, K), 0) == 0
    for number in range(size):
        mid = both[number * ROWS : (number + 1) * ROWS]
        lower = jnp.where(is_first, mid[HALF : HALF + 1, :K], mid[:HALF, K:])
        corr = dot(inv_two_ref[...], jnp.concatenate([mid[:HALF, :K], lower], axis=0).astype(BF16))
        peak = jnp.max(corr, axis=(0, 1), keepdims=True) * (1.0 / (K * K))
        mean = jnp.sum(corr * corr, axis=(0, 1), keepdims=True) * (1.0 / float(K) ** 6)
        weight = peak / jnp.sqrt(mean + 1e-06)
        weight_ref[pl.ds(first + number, 1), :] = jnp.broadcast_to(weight, (1, 128))


def add_aligned(first, size, scalars_ref, spec_ref, weight_ref, down_ref, across_ref, total_ref):
    total_re, total_im = total_ref[:ROWS, :], total_ref[ROWS:, :]
    for number in range(size):
        weight = weight_ref[pl.ds(first + number, 1), :]
        lane = jnp.full((ROWS, 128), scalars_ref[2 * (first + number)] + REACH, jnp.int32)
        down_re = jnp.take_along_axis(down_ref[0], lane, axis=1, mode="promise_in_bounds")
        down_im = jnp.take_along_axis(down_ref[1], lane, axis=1, mode="promise_in_bounds")
        down_re = jnp.concatenate([down_re, down_re], axis=1)
        down_im = jnp.concatenate([down_im, down_im], axis=1)
        weight = jnp.concatenate([weight, weight], axis=1)
        column = scalars_ref[2 * (first + number) + 1] + REACH
        across_re = weight * across_ref[0, pl.ds(column, 1), :]
        across_im = weight * across_ref[1, pl.ds(column, 1), :]
        ramp_re = down_re * across_re - down_im * across_im
        ramp_im = down_re * across_im + down_im * across_re
        spec_re = spec_ref[first + number, :ROWS, :].astype(F32)
        spec_im = spec_ref[first + number, ROWS:, :].astype(F32)
        total_re = total_re + (spec_re * ramp_re - spec_im * ramp_im)
        total_im = total_im + (spec_im * ramp_re + spec_re * ramp_im)
    total_ref[:ROWS, :] = total_re
    total_ref[ROWS:, :] = total_im


def add_bins(first, size, scalars_ref, pattern_ref, weight_ref, bins_ref):
    for number in range(size):
        weight = weight_ref[pl.ds(first + number, 1), :]
        weight = jnp.concatenate([weight, weight], axis=1)
        scaled = (weight * pattern_ref[first + number].astype(F32)).astype(BF16)
        slot = scalars_ref[TARGET + first + number]
        bins_ref[slot] = bins_ref[slot] + scaled


def copies(sources, targets, sems):
    return [pltpu.make_async_copy(a, b, sems.at[i]) for i, (a, b) in enumerate(zip(sources, targets))]


GROUP = 4
COUNT = 16
TARGET = 2 * COUNT
CORE = 3 * COUNT


def first_kernel(
    scalars_ref, pattern_hbm, *refs,
):
    constants, refs = refs[:9], refs[9:]
    spec_hbm, keep_ref, send_ref, weight_ref = refs[:4]
    binned_hbm, refs = refs[4:7], refs[7:]
    held, refs = refs[:9], refs[9:]
    pattern_ref, spec_ref, now_ref, total_ref, cross_ref, bins_ref, const_sem, pattern_sem, spec_sem, bins_sem = refs
    ref_ref, reorder_ref, turn_ref, fwd_one_ref, fwd_two_ref, inv_one_ref, inv_two_ref, down_ref, across_ref = held
    count = pattern_ref.shape[0]
    groups = count // GROUP

    def group(ref, number):
        return ref.at[pl.ds(number * GROUP, GROUP)]

    def fetch(number):
        return pltpu.make_async_copy(group(pattern_hbm, number), group(pattern_ref, number), pattern_sem.at[number])

    def store(number):
        return pltpu.make_async_copy(group(spec_ref, number), group(spec_hbm, number), spec_sem.at[number])

    incoming = copies(constants, held, const_sem)
    for copy in incoming[:3]:
        copy.start()
    fetch(0).start()
    for copy in incoming[3:]:
        copy.start()
    for number in range(1, groups):
        fetch(number).start()
    total_ref[...] = jnp.zeros_like(total_ref)
    weight_ref[...] = jnp.zeros_like(weight_ref)
    bins_ref[...] = jnp.zeros_like(bins_ref)
    spec_ref[:GROUP] = jnp.zeros_like(spec_ref[:GROUP])
    for copy in incoming[:3]:
        copy.wait()
    hermitian_part(ref_ref, reorder_ref, turn_ref, now_ref)
    for copy in incoming[3:]:
        copy.wait()

    def finish(first):
        add_aligned(first, GROUP, scalars_ref, spec_ref, weight_ref, down_ref, across_ref, total_ref)

    def body(number, _):
        first = number * GROUP
        fetch(number).wait()
        last = jnp.maximum(first - GROUP, 0)
        finish(last)
        forward(first, GROUP, pattern_ref, spec_ref, fwd_one_ref, fwd_two_ref)
        store(number).start()
        correlate(first, GROUP, spec_ref, now_ref, cross_ref, inv_one_ref, inv_two_ref, weight_ref)
        add_bins(first, GROUP, scalars_ref, pattern_ref, weight_ref, bins_ref)
        return 0

    lax.fori_loop(0, groups, body, 0)
    place, sources = 0, []
    for target in binned_hbm:
        sources.append(bins_ref.at[pl.ds(place, target.shape[0])])
        place += target.shape[0]
    outgoing = copies(sources, binned_hbm, bins_sem)
    for copy in outgoing:
        copy.start()
    finish(count - GROUP)
    pack(scalars_ref[CORE], total_ref, keep_ref, send_ref)
    for copy in outgoing:
        copy.wait()
    for number in range(groups):
        store(number).wait()


def second_kernel(
    scalars_ref, spec_hbm, old_ref, old_other_ref, *refs,
):
    constants, refs = refs[:4], refs[4:]
    keep_ref, send_ref, weight_ref = refs[:3]
    held, refs = refs[3:7], refs[7:]
    spec_ref, now_ref, total_ref, cross_ref, const_sem, spec_sem = refs
    inv_one_ref, inv_two_ref, down_ref, across_ref = held
    count = spec_ref.shape[0]
    groups = count // GROUP

    def group(ref, number):
        return ref.at[pl.ds(number * GROUP, GROUP)]

    def fetch(number):
        return pltpu.make_async_copy(group(spec_hbm, number), group(spec_ref, number), spec_sem.at[number])

    incoming = copies(constants, held, const_sem)
    fetch(0).start()
    for copy in incoming:
        copy.start()
    for number in range(1, groups):
        fetch(number).start()
    total_ref[...] = jnp.zeros_like(total_ref)
    weight_ref[...] = jnp.zeros_like(weight_ref)
    real, imag, last_re, last_im, scale = unpack(scalars_ref[CORE], old_ref, old_other_ref)
    is_first = lax.broadcasted_iota(jnp.int32, (ROWS - HALF, K), 0) == 0
    now_ref[:HALF, :] = real * scale
    now_ref[HALF:ROWS, :] = jnp.where(is_first, last_re * scale, 0.0)
    now_ref[ROWS : ROWS + HALF, :] = imag * scale
    now_ref[ROWS + HALF :, :] = jnp.where(is_first, last_im * scale, 0.0)
    for copy in incoming:
        copy.wait()

    def finish(first):
        add_aligned(first, GROUP, scalars_ref, spec_ref, weight_ref, down_ref, across_ref, total_ref)

    def body(number, _):
        first = number * GROUP
        fetch(number).wait()
        finish(jnp.maximum(first - GROUP, 0))
        correlate(first, GROUP, spec_ref, now_ref, cross_ref, inv_one_ref, inv_two_ref, weight_ref)
        return 0

    lax.fori_loop(0, groups, body, 0)
    finish(count - GROUP)
    pack(scalars_ref[CORE], total_ref, keep_ref, send_ref)


def last_kernel(scalars_ref, old_ref, old_other_ref, back_ref, out_ref):
    real, imag, last_re, last_im, scale = unpack(scalars_ref[CORE], old_ref, old_other_ref)
    row = lax.broadcasted_iota(jnp.int32, (HALF, HALF), 0)
    column = lax.broadcasted_iota(jnp.int32, (HALF, HALF), 1)
    turn = jnp.where(row + column == HALF, 1.0, 0.0).astype(BF16)
    is_first = lax.broadcasted_iota(jnp.int32, (HALF, K), 0) == 0
    for part, (body, row_128) in enumerate(((real, last_re), (imag, last_im))):
        turned = negate_columns(dot(turn, body.astype(BF16)))
        turned = jnp.where(is_first, row_128, turned if part == 0 else -turned)
        both = jnp.concatenate([body, turned], axis=0)
        natural = sum(dot(piece, back_ref[...]) for piece in split(both))
        out_ref[part] = natural * scale


ANY = pl.BlockSpec(memory_space=pl.ANY)
PARAMS = pltpu.CompilerParams(vmem_limit_bytes=56 * 1024 * 1024)


HALF_SPEC = pl.BlockSpec((SLICES, 2 * DEEP, 128), lambda *_: (0, 0, 0))


def half_sum(dtype):
    return jax.ShapeDtypeStruct((SLICES, 2 * DEEP, 128), dtype)


def constant(*names):
    return [jnp.asarray(tables()[name]) for name in names]


def held_like(arrays):
    return [pltpu.VMEM(a.shape, a.dtype) for a in arrays]


def run_first(patterns, ref_spectrum, scalars, bins):
    arrays = [ref_spectrum] + constant(
        "reorder", "turn", "fwd_one", "fwd_two", "inv_one", "inv_two", "down", "across"
    )
    count = patterns.shape[0]
    spectra = jax.ShapeDtypeStruct((count, 2 * ROWS, K), BF16)
    part = lambda size: jax.ShapeDtypeStruct((size, K, K), BF16)
    parts = (part(bins // 2), part(bins // 2 - BINS), part(BINS))
    return pl.pallas_call(
        first_kernel,
        out_shape=(spectra, half_sum(F32), half_sum(BF16), jax.ShapeDtypeStruct((count, 128), F32), *parts),
        grid_spec=pltpu.PrefetchScalarGridSpec(
            num_scalar_prefetch=1,
            grid=(1,),
            in_specs=[ANY] * (1 + len(arrays)),
            out_specs=(
                ANY,
                HALF_SPEC,
                HALF_SPEC,
                pl.BlockSpec((count, 128), lambda i, *_: (0, 0)),
                ANY,
                ANY,
                ANY,
            ),
            scratch_shapes=held_like(arrays)
            + [
                pltpu.VMEM(patterns.shape, BF16),
                pltpu.VMEM(spectra.shape, BF16),
                pltpu.VMEM((2 * ROWS, K), F32),
                pltpu.VMEM((2 * ROWS, K), F32),
                pltpu.VMEM((GROUP * ROWS, 2 * K), BF16),
                pltpu.VMEM((bins, K, K), BF16),
                pltpu.SemaphoreType.DMA((len(arrays),)),
                pltpu.SemaphoreType.DMA((count // GROUP,)),
                pltpu.SemaphoreType.DMA((count // GROUP,)),
                pltpu.SemaphoreType.DMA((3,)),
            ],
        ),
        compiler_params=PARAMS,
        cost_estimate=pl.CostEstimate(flops=int(5e9), bytes_accessed=int(12e6), transcendentals=0),
        name="forward_and_correlate",
    )(scalars, patterns, *arrays)


def run_second(spectra, keep, other, scalars):
    arrays = constant("inv_one", "inv_two", "down", "across")
    count = spectra.shape[0]
    return pl.pallas_call(
        second_kernel,
        out_shape=(half_sum(F32), half_sum(BF16), jax.ShapeDtypeStruct((count, 128), F32)),
        grid_spec=pltpu.PrefetchScalarGridSpec(
            num_scalar_prefetch=1,
            grid=(1,),
            in_specs=[ANY, HALF_SPEC, HALF_SPEC] + [ANY] * len(arrays),
            out_specs=(HALF_SPEC, HALF_SPEC, pl.BlockSpec((count, 128), lambda i, s: (0, 0))),
            scratch_shapes=held_like(arrays)
            + [
                pltpu.VMEM(spectra.shape, BF16),
                pltpu.VMEM((2 * ROWS, K), F32),
                pltpu.VMEM((2 * ROWS, K), F32),
                pltpu.VMEM((GROUP * ROWS, 2 * K), BF16),
                pltpu.SemaphoreType.DMA((len(arrays),)),
                pltpu.SemaphoreType.DMA((count // GROUP,)),
            ],
        ),
        compiler_params=PARAMS,
        cost_estimate=pl.CostEstimate(flops=int(3e9), bytes_accessed=int(4e6), transcendentals=0),
        name="correlate_again",
    )(scalars, spectra, keep, other, *arrays)


def run_last(keep, other, scalars):
    whole = lambda shape: pl.BlockSpec(shape, lambda *_: (0,) * len(shape))
    return pl.pallas_call(
        last_kernel,
        out_shape=jax.ShapeDtypeStruct((2, K, K), F32),
        grid_spec=pltpu.PrefetchScalarGridSpec(
            num_scalar_prefetch=1,
            grid=(1,),
            in_specs=[HALF_SPEC, HALF_SPEC, whole((K, K))],
            out_specs=whole((2, K, K)),
        ),
        compiler_params=PARAMS,
        cost_estimate=pl.CostEstimate(flops=int(1e8), bytes_accessed=int(1e6), transcendentals=0),
        name="finish",
    )(scalars, keep, other, *constant("back"))


def add_halves(*halves):
    values = [half.astype(F32) for half in halves]
    while len(values) > 1:
        values = [values[i] + values[i + 1] for i in range(0, len(values), 2)]
    return values[0].astype(BF16)


def on_device(patterns, ref_spectrum, shifts, bin_owner, bin_index):
    columns, lines = lax.axis_size("col"), lax.axis_size("row")
    me = lax.axis_index("col")
    owner = bin_owner.reshape(-1)
    chips = columns // 2
    targets = ((owner ^ me) % 2) * (chips * BINS) + ((owner // 2) ^ (me // 2)) * BINS + bin_index
    scalars = jnp.concatenate([shifts.reshape(-1), targets, (me % 2).reshape(1).astype(jnp.int32)])

    def send(array, far, axis="col"):
        return lax.ppermute(array, axis, [(i, i ^ far) for i in range(lax.axis_size(axis))])

    def over_chips(half):
        return [half] + [send(half, 2 * far) for far in range(1, chips)]

    def over_lines(half):
        return [half] + [send(half, far, "row") for far in range(1, lines)]

    spectra, keep, away, _, mine, other, other_far = run_first(patterns, ref_spectrum, scalars, columns * BINS)
    half = add_halves(keep, send(away, 1))
    half, other, other_far = lax.optimization_barrier((half, other, other_far))
    half = add_halves(*over_chips(half))
    other, other_far = send(other, 1), send(other_far, 1)
    mine = mine.reshape(chips, BINS, K, K)
    other = other.reshape(chips - 1, BINS, K, K)

    def chip_bins(far, *more, low=0, high=BINS):
        there = other[far] if far < chips - 1 else other_far
        arrays = [array[low:high].astype(F32) for array in (mine[far], there, *more)]
        return sum(arrays[1:], arrays[0])

    binned = chip_bins(0)
    if chips == 4:
        block = chip_bins(3).astype(BF16)
        half, block = lax.optimization_barrier((half, block))
        pairs = lambda hops: [(2 * a + core, 2 * b + core) for a, b in hops for core in range(2)]
        passing = lax.ppermute(block, "col", pairs([(0, 1), (3, 2)]))
        middle = lax.ppermute(block, "col", pairs([(1, 2), (2, 1)]))
        half = add_halves(*over_lines(half))
        other_half = send(half, 1)
        half, passing, middle = lax.optimization_barrier((half, passing, middle))
        cut = BINS - 1
        blocks = [
            (chip_bins(1, low=low, high=high).astype(BF16), chip_bins(2, passing, low=low, high=high).astype(BF16))
            for low, high in ((0, cut), (cut, BINS))
        ]
        half, other_half, blocks = lax.optimization_barrier((half, other_half, blocks))
        lower = (send(blocks[0][0], 2), send(blocks[0][1], 4))
        keep, away, weight = run_second(spectra, half, other_half, scalars)
        away, lower = lax.optimization_barrier((away, lower))
        half = add_halves(*over_lines(add_halves(keep, send(away, 1))))
        upper = (send(blocks[1][0], 2), send(blocks[1][1], 4))
        half, lower, upper = lax.optimization_barrier((half, lower, upper))
        binned = binned + middle.astype(F32)
        for a, b in zip(lower, upper):
            binned = binned + jnp.concatenate([a, b]).astype(F32)
    else:
        half = add_halves(*over_lines(half))
        for far in range(1, chips):
            binned = binned + send(chip_bins(far).astype(BF16), 2 * far).astype(F32)
        keep, away, weight = run_second(spectra, half, send(half, 1), scalars)
        half = add_halves(*over_lines(add_halves(keep, send(away, 1))))
    half = add_halves(*over_chips(half))
    return (run_last(half, send(half, 1), scalars), weight[:, 0], binned)


def solution(mesh):
    placed = (P(BOTH, None, None), P(), P(BOTH, None), P(BOTH, None), P(BOTH))
    return jax.shard_map(
        on_device,
        mesh=mesh,
        in_specs=placed,
        out_specs=(P(), P(BOTH), P(BOTH, None, None)),
        check_vma=False,
    )
```

time: 577 us -> 95.5 us (0.17)
  waiting for transfers between devices: 419 us -> 24.3 us
  other arithmetic: 102 us -> 6.06 us
  starting transfers between devices: 0.12 us -> 37.8 us
  matrix products: 24.1 us -> 0 us
  Pallas kernels: 0 us -> 23.2 us
  between operations: 16 us -> 0.8 us
  local copies, waits for them, and re-layouts: 13.7 us -> 2.81 us
    psum x2 -> x0, waiting for transfers between devices: 246 us -> none  [on_device(): summed = lax.psum(local_term, ('row', 'col'))]
    unnamed x4 -> x0, waiting for transfers between devices: 173 us -> none
    another operation x6 -> x0, other arithmetic: 48.7 us -> none
    reduce_sum x4 -> x0, other arithmetic: 47.2 us -> none  [the longest x2 43.8 us: correlate(): jnp.sum(weight[:, None, None] * aligned_re, axis=0)]
    ppermute x0 -> x24, starting transfers between devices: none -> 37.8 us  [the longest x22 34.3 us: send(): lax.ppermute(array, axis, [(i, i ^ far) for i in range(lax.axis_size(axis...]
    ppermute x0 -> x24, waiting for transfers between devices: none -> 24.3 us  [the longest x22 24.3 us: send(): lax.ppermute(array, axis, [(i, i ^ far) for i in range(lax.axis_size(axis...]
    dot_general x4 -> x0, matrix products: 24.1 us -> none  [the longest x2 12.6 us: correlate(): jnp.einsum('oij,bjol->bil', inv_two, half_section, preferred_element_type...]
    pallas_call x0 -> x3, Pallas kernels: none -> 23.2 us  [the longest x1 11.9 us: run_first(): pl.pallas_call(first_kernel, out_shape=(spectra, half_sum(F32), half_sum(...]
  transfers between devices with their start and end apart: 3 -> 24, of which waited for: 3 -> 14; matrix products, arithmetic and copies ran while one was open for 2% -> 4% of each run, Pallas kernels for 0% -> 9%
where the time goes in v2:
time: 95.5 us; the launch traced here: 95 us
  starting transfers between devices  37.8 us (40%)
  waiting for transfers between devices  24.3 us (25%)
  Pallas kernels  23.2 us (24%)
  other arithmetic  6.06 us (6%)
  local copies, waits for them, and re-layouts  2.81 us (3%)
    ppermute x22, starting transfers between devices, send(): lax.ppermute(array, axis, [(i, i ^ far) for i in range(lax.axis_size(axis...  34.3 us
    ppermute x22, waiting for transfers between devices, send(): lax.ppermute(array, axis, [(i, i ^ far) for i in range(lax.axis_size(axis...  24.3 us
    pallas_call x1, Pallas kernels, run_first(): pl.pallas_call(first_kernel, out_shape=(spectra, half_sum(F32), half_sum(...  11.9 us
    pallas_call x1, Pallas kernels, run_second(): pl.pallas_call(second_kernel, out_shape=(half_sum(F32), half_sum(BF16), j...  8.47 us
    ppermute x1, starting transfers between devices, on_device(): passing = lax.ppermute(block, 'col', pairs([(0, 1), (3, 2)]))  2.87 us
    pallas_call x1, Pallas kernels, run_last(): pl.pallas_call(last_kernel, out_shape=jax.ShapeDtypeStruct((2, K, K), F32...  2.84 us
    convert_element_type x6, other arithmetic, add_halves(): return values[0].astype(BF16)  2 us
  transfers between devices with their start and end apart: 24, of which 14 were waited for; matrix products, arithmetic and copies ran while one was open for 4% of the time, Pallas kernels for 9%

profile of v2, /device:TPU:1, one launch (start us, length us, event | category | flops | bytes accessed | tf_op | source)
XLA Modules:
  0.0 95.0 jit_solution(8901740003884097084)
XLA Ops:
  2.8 11.9 %forward_and_correlate.1 = (bf16[16,288,256]{2,1,0:T(8,128)(2,1)}, f32[16,16,128]{2,1,0:T(8,128)}, bf16[16,16,128]{2,1,0:T(8,128)(2,1)}, f32[16,128]{1,0:T(8,128...) custom-call(s32[49]{0:T(128)} %pad_add_fusion.scalars_ref, ...), custom_call_target="tpu_custom_call" | custom-call | flops 5000000000 | bytes 12000000 | tf_op jit(solution)/shard_map/forward_and_correlate/pallas_call | solution.py:364
  14.8 1.4 %collective-permute-done = bf16[16,16,128]{2,1,0:T(8,128)(2,1)S(1)} collective-permute-done((bf16[16,16,128]{2,1,0:T(8,128)(2,1)}, bf16[16,16,128]{2,1,0:T(8,128)(2,1)S(1)}, u32[]{:S(2)}, u32[]{:S(2)}) %collective-permute-start) | collective-permute-done | bytes 65568 | tf_op jit(solution)/shard_map/ppermute | solution.py:460
  17.7 2.5 %collective-permute-start.1 = (bf16[16,16,128]{2,1,0:T(8,128)(2,1)S(1)}, bf16[16,16,128]{2,1,0:T(8,128)(2,1)S(1)}, u32[]{:S(2)}, u32[]{:S(2)}) collective-permute-start(bf16[16,16,128]{2,1,0:T(8,128)(2,1)S(1)} %add_convert_fusion.10), channel_id=1, source_target_pairs={{0,2},{1,3},{2,0},{3,1},{4,6},{5,7},{6,4},{7,5},{8,10},{9,11},{10,... | collective-permute-start | bytes 196616 | tf_op jit(solution)/shard_map/ppermute | solution.py:460
  20.2 2.3 %collective-permute-start.2 = (bf16[16,16,128]{2,1,0:T(8,128)(2,1)S(1)}, bf16[16,16,128]{2,1,0:T(8,128)(2,1)S(1)}, u32[]{:S(2)}, u32[]{:S(2)}) collective-permute-start(bf16[16,16,128]{2,1,0:T(8,128)(2,1)S(1)} %add_convert_fusion.10), channel_id=1, source_target_pairs={{0,4},{1,5},{2,6},{3,7},{4,0},{5,1},{6,2},{7,3},{8,12},{9,13},{10,... | collective-permute-start | bytes 196616 | tf_op jit(solution)/shard_map/ppermute | solution.py:460
  22.5 2.0 %collective-permute-done.2 = bf16[16,16,128]{2,1,0:T(8,128)(2,1)S(1)} collective-permute-done((bf16[16,16,128]{2,1,0:T(8,128)(2,1)S(1)}, bf16[16,16,128]{2,1,0:T(8,128)(2,1)S(1)}, u32[]{:S(2)}, u32[]{:S(2)}) %collective-permute-start.2) | collective-permute-done | bytes 65568 | tf_op jit(solution)/shard_map/ppermute | solution.py:460
  24.5 3.1 %collective-permute-done.3 = bf16[16,16,128]{2,1,0:T(8,128)(2,1)S(1)} collective-permute-done((bf16[16,16,128]{2,1,0:T(8,128)(2,1)S(1)}, bf16[16,16,128]{2,1,0:T(8,128)(2,1)S(1)}, u32[]{:S(2)}, u32[]{:S(2)}) %collective-permute-start.3) | collective-permute-done | bytes 65568 | tf_op jit(solution)/shard_map/ppermute | solution.py:460
  28.7 2.9 %collective-permute-start.8 = (bf16[4,256,256]{2,1,0:T(8,128)(2,1)S(1)}, bf16[4,256,256]{2,1,0:T(8,128)(2,1)S(1)}, u32[]{:S(2)}, u32[]{:S(2)}) collective-permute-start(bf16[4,256,256]{2,1,0:T(8,128)(2,1)S(1)} %add_convert_fusion), channel_id=1, source_target_pairs={{0,2},{1,3},{6,4},{7,5},{8,10},{9,11},{14,12},{15,13},{16,18},{17,... | collective-permute-start | bytes 1572872 | tf_op jit(solution)/shard_map/ppermute | solution.py:486
  32.3 1.3 %collective-permute-start.5 = (bf16[16,16,128]{2,1,0:T(8,128)(2,1)S(1)}, bf16[16,16,128]{2,1,0:T(8,128)(2,1)S(1)}, u32[]{:S(2)}, u32[]{:S(2)}) collective-permute-start(bf16[16,16,128]{2,1,0:T(8,128)(2,1)S(1)} %add_convert_fusion.9), channel_id=1, source_target_pairs={{0,8},{8,0},{16,24},{24,16},{1,9},{9,1},{17,25},{25,17},{2,10},{10... | collective-permute-start | bytes 196616 | tf_op jit(solution)/shard_map/ppermute | solution.py:460
  35.5 2.2 %collective-permute-start.7 = (bf16[16,16,128]{2,1,0:T(8,128)(2,1)S(1)}, bf16[16,16,128]{2,1,0:T(8,128)(2,1)S(1)}, u32[]{:S(2)}, u32[]{:S(2)}) collective-permute-start(bf16[16,16,128]{2,1,0:T(8,128)(2,1)S(1)} %add_convert_fusion.9), channel_id=1, source_target_pairs={{0,24},{8,16},{16,8},{24,0},{1,25},{9,17},{17,9},{25,1},{2,26},{10... | collective-permute-start | bytes 196616 | tf_op jit(solution)/shard_map/ppermute | solution.py:460
  37.7 2.0 %collective-permute-done.7 = bf16[16,16,128]{2,1,0:T(8,128)(2,1)S(1)} collective-permute-done((bf16[16,16,128]{2,1,0:T(8,128)(2,1)S(1)}, bf16[16,16,128]{2,1,0:T(8,128)(2,1)S(1)}, u32[]{:S(2)}, u32[]{:S(2)}) %collective-permute-start.7) | collective-permute-done | bytes 65568 | tf_op jit(solution)/shard_map/ppermute | solution.py:460
  39.7 4.2 %collective-permute-start.10 = (bf16[16,16,128]{2,1,0:T(8,128)(2,1)S(1)}, bf16[16,16,128]{2,1,0:T(8,128)(2,1)S(1)}, u32[]{:S(2)}, u32[]{:S(2)}) collective-permute-start(bf16[16,16,128]{2,1,0:T(8,128)(2,1)S(1)} %add_convert_fusion.8.old_ref), channel_id=1, source_target_pairs={{0,1},{1,0},{2,3},{3,2},{4,5},{5,4},{6,7},{7,6},{8,9},{9,8},{10,11... | collective-permute-start | bytes 196616 | tf_op jit(solution)/shard_map/ppermute | solution.py:460
  44.8 1.8 %collective-permute-start.12 = (bf16[3,256,256]{2,1,0:T(8,128)(2,1)S(1)}, bf16[3,256,256]{2,1,0:T(8,128)(2,1)S(1)}, u32[]{:S(2)}, u32[]{:S(2)}) collective-permute-start(bf16[3,256,256]{2,1,0:T(8,128)(2,1)S(1)} %get-tuple-element.51), channel_id=1, source_target_pairs={{0,2},{1,3},{2,0},{3,1},{4,6},{5,7},{6,4},{7,5},{8,10},{9,11},{10,... | collective-permute-start | bytes 1179656 | tf_op jit(solution)/shard_map/ppermute | solution.py:460
  47.2 8.5 %correlate_again.1 = (f32[16,16,128]{2,1,0:T(8,128)}, bf16[16,16,128]{2,1,0:T(8,128)(2,1)}, f32[16,128]{1,0:T(8,128)}) custom-call(s32[49]{0:T(128)} %pad_add_fusion.scalars_ref, bf16[16,288,256]{2,1,0:T(8,128)(2,1)} %get-tuple-element.34.spec_hbm, bf16[16,16,128]{2,1,0:T(8,128)(2,1)} %copy-done.2, bf16[16,16,128]{2,1,0:T(8,128)(2,1)} %copy-done.4, ...), custom_call_target="tpu_custom_call" | custom-call | flops 3000000000 | bytes 4000000 | tf_op jit(solution)/shard_map/correlate_again/pallas_call | solution.py:403
  55.7 6.6 %collective-permute-done.12 = bf16[3,256,256]{2,1,0:T(8,128)(2,1)S(1)} collective-permute-done((bf16[3,256,256]{2,1,0:T(8,128)(2,1)S(1)}, bf16[3,256,256]{2,1,0:T(8,128)(2,1)S(1)}, u32[]{:S(2)}, u32[]{:S(2)}) %collective-permute-start.12) | collective-permute-done | bytes 393248 | tf_op jit(solution)/shard_map/ppermute | solution.py:460
  62.5 5.0 %collective-permute-start.14 = (bf16[16,16,128]{2,1,0:T(8,128)(2,1)}, bf16[16,16,128]{2,1,0:T(8,128)(2,1)S(1)}, u32[]{:S(2)}, u32[]{:S(2)}) collective-permute-start(bf16[16,16,128]{2,1,0:T(8,128)(2,1)} %get-tuple-element.53), channel_id=1, source_target_pairs={{0,1},{1,0},{2,3},{3,2},{4,5},{5,4},{6,7},{7,6},{8,9},{9,8},{10,11... | collective-permute-start | bytes 196616 | tf_op jit(solution)/shard_map/ppermute | solution.py:460
  69.6 1.3 %collective-permute-start.15 = (bf16[16,16,128]{2,1,0:T(8,128)(2,1)S(1)}, bf16[16,16,128]{2,1,0:T(8,128)(2,1)S(1)}, u32[]{:S(2)}, u32[]{:S(2)}) collective-permute-start(bf16[16,16,128]{2,1,0:T(8,128)(2,1)S(1)} %add_convert_fusion.7), channel_id=1, source_target_pairs={{0,8},{8,0},{16,24},{24,16},{1,9},{9,1},{17,25},{25,17},{2,10},{10... | collective-permute-start | bytes 196616 | tf_op jit(solution)/shard_map/ppermute | solution.py:460
  72.3 1.4 %collective-permute-start.19 = (bf16[1,256,256]{2,1,0:T(8,128)(2,1)S(1)}, bf16[1,256,256]{2,1,0:T(8,128)(2,1)S(1)}, u32[]{:S(2)}, u32[]{:S(2)}) collective-permute-start(bf16[1,256,256]{2,1,0:T(8,128)(2,1)S(1)} %get-tuple-element.57), channel_id=1, source_target_pairs={{0,4},{1,5},{2,6},{3,7},{4,0},{5,1},{6,2},{7,3},{8,12},{9,13},{10,... | collective-permute-start | bytes 393224 | tf_op jit(solution)/shard_map/ppermute | solution.py:460
  74.0 2.1 %collective-permute-done.17 = bf16[16,16,128]{2,1,0:T(8,128)(2,1)S(1)} collective-permute-done((bf16[16,16,128]{2,1,0:T(8,128)(2,1)S(1)}, bf16[16,16,128]{2,1,0:T(8,128)(2,1)S(1)}, u32[]{:S(2)}, u32[]{:S(2)}) %collective-permute-start.17) | collective-permute-done | bytes 65568 | tf_op jit(solution)/shard_map/ppermute | solution.py:460
  76.1 2.5 %collective-permute-done.18 = bf16[1,256,256]{2,1,0:T(8,128)(2,1)S(1)} collective-permute-done((bf16[1,256,256]{2,1,0:T(8,128)(2,1)S(1)}, bf16[1,256,256]{2,1,0:T(8,128)(2,1)S(1)}, u32[]{:S(2)}, u32[]{:S(2)}) %collective-permute-start.18) | collective-permute-done | bytes 131104 | tf_op jit(solution)/shard_map/ppermute | solution.py:460
  80.1 2.0 %collective-permute-start.22 = (bf16[16,16,128]{2,1,0:T(8,128)(2,1)S(1)}, bf16[16,16,128]{2,1,0:T(8,128)(2,1)S(1)}, u32[]{:S(2)}, u32[]{:S(2)}) collective-permute-start(bf16[16,16,128]{2,1,0:T(8,128)(2,1)S(1)} %add_convert_fusion.6), channel_id=1, source_target_pairs={{0,6},{1,7},{2,4},{3,5},{4,2},{5,3},{6,0},{7,1},{8,14},{9,15},{10,... | collective-permute-start | bytes 196616 | tf_op jit(solution)/shard_map/ppermute | solution.py:460
  82.1 1.3 %slice_reduce_fusion = f32[16]{0:T(128)} fusion(f32[16,128]{1,0:T(8,128)} %get-tuple-element.59), kind=kLoop, calls=%fused_computation.12 | loop fusion | bytes 128 | tf_op jit(solution)/shard_map/slice | solution.py:513
  85.5 4.8 %collective-permute-start.23 = (bf16[16,16,128]{2,1,0:T(8,128)(2,1)S(1)}, bf16[16,16,128]{2,1,0:T(8,128)(2,1)S(1)}, u32[]{:S(2)}, u32[]{:S(2)}) collective-permute-start(bf16[16,16,128]{2,1,0:T(8,128)(2,1)S(1)} %add_convert_fusion.5.old_ref), channel_id=1, source_target_pairs={{0,1},{1,0},{2,3},{3,2},{4,5},{5,4},{6,7},{7,6},{8,9},{9,8},{10,11... | collective-permute-start | bytes 196616 | tf_op jit(solution)/shard_map/ppermute | solution.py:460
  90.3 1.3 %convert_add_fusion = f32[4,256,256]{2,1,0:T(8,128)} fusion(bf16[4,256,256]{2,1,0:T(8,128)(2,1)S(1)} %collective-permute-done.9, bf16[12,256,256]{2,1,0:T(8,128)(2,1)S(1)} %collective-permute-done.11, bf16[1,256,256]{2,1,0:T(8,128)(2,1)S(1)} %collective-permute-done.18, bf16[3,256,256]{2,1,0:T(8,128)(2,1)S(1)} %collective-permute-done.12, ...), kind=kLoop, calls=%fused_computation | loop fusion | flops 2883584 | bytes 3670016 | tf_op jit(solution)/shard_map/add | solution.py:505
  92.2 2.8 %finish.1 = f32[2,256,256]{2,1,0:T(8,128)} custom-call(s32[49]{0:T(128)} %pad_add_fusion.scalars_ref, bf16[16,16,128]{2,1,0:T(8,128)(2,1)} %copy-done.1, bf16[16,16,128]{2,1,0:T(8,128)(2,1)} %copy-done.3, bf16[256,256]{1,0:T(8,128)(2,1)} %constant.65.clone.refs_1_.back_ref), custom_call_target="tpu_custom_call" | custom-call | flops 100000000 | bytes 1000000 | tf_op jit(solution)/shard_map/finish/pallas_call | solution.py:429
  (52 shorter events, 17.2 us)
Async XLA Ops:
  14.7 1.5 %collective-permute-start = (bf16[16,16,128]{2,1,0:T(8,128)(2,1)}, bf16[16,16,128]{2,1,0:T(8,128)(2,1)S(1)}, u32[]{:S(2)}, u32[]{:S(2)}) collective-permute-start(bf16[16,16,128]{2,1,0:T(8,128)(2,1)} %get-tuple-element.36), channel_id=1, source_target_pairs={{0,1},{1,0},{2,3},{3,2},{4,5},{5,4},{6,7},{7,6},{8,9},{9,8},{10,11... | collective-permute-start | bytes 196616 | tf_op jit(solution)/shard_map/ppermute | solution.py:460
  17.1 26.8 %collective-permute-start.11 = (bf16[12,256,256]{2,1,0:T(8,128)(2,1)}, bf16[12,256,256]{2,1,0:T(8,128)(2,1)S(1)}, u32[]{:S(2)}, u32[]{:S(2)}) collective-permute-start(bf16[12,256,256]{2,1,0:T(8,128)(2,1)} %get-tuple-element.45), channel_id=1, source_target_pairs={{0,1},{1,0},{2,3},{3,2},{4,5},{5,4},{6,7},{7,6},{8,9},{9,8},{10,11... | collective-permute-start | bytes 4718600 | tf_op jit(solution)/shard_map/ppermute | solution.py:460
  17.4 10.2 %collective-permute-start.4 = (bf16[4,256,256]{2,1,0:T(8,128)(2,1)}, bf16[4,256,256]{2,1,0:T(8,128)(2,1)S(1)}, u32[]{:S(2)}, u32[]{:S(2)}) collective-permute-start(bf16[4,256,256]{2,1,0:T(8,128)(2,1)} %get-tuple-element.41), channel_id=1, source_target_pairs={{0,1},{1,0},{2,3},{3,2},{4,5},{5,4},{6,7},{7,6},{8,9},{9,8},{10,11... | collective-permute-start | bytes 1572872 | tf_op jit(solution)/shard_map/ppermute | solution.py:460
  17.7 4.8 %collective-permute-start.1 = (bf16[16,16,128]{2,1,0:T(8,128)(2,1)S(1)}, bf16[16,16,128]{2,1,0:T(8,128)(2,1)S(1)}, u32[]{:S(2)}, u32[]{:S(2)}) collective-permute-start(bf16[16,16,128]{2,1,0:T(8,128)(2,1)S(1)} %add_convert_fusion.10), channel_id=1, source_target_pairs={{0,2},{1,3},{2,0},{3,1},{4,6},{5,7},{6,4},{7,5},{8,10},{9,11},{10,... | collective-permute-start | bytes 196616 | tf_op jit(solution)/shard_map/ppermute | solution.py:460
  20.2 4.3 %collective-permute-start.2 = (bf16[16,16,128]{2,1,0:T(8,128)(2,1)S(1)}, bf16[16,16,128]{2,1,0:T(8,128)(2,1)S(1)}, u32[]{:S(2)}, u32[]{:S(2)}) collective-permute-start(bf16[16,16,128]{2,1,0:T(8,128)(2,1)S(1)} %add_convert_fusion.10), channel_id=1, source_target_pairs={{0,4},{1,5},{2,6},{3,7},{4,0},{5,1},{6,2},{7,3},{8,12},{9,13},{10,... | collective-permute-start | bytes 196616 | tf_op jit(solution)/shard_map/ppermute | solution.py:460
  22.5 5.0 %collective-permute-start.3 = (bf16[16,16,128]{2,1,0:T(8,128)(2,1)S(1)}, bf16[16,16,128]{2,1,0:T(8,128)(2,1)S(1)}, u32[]{:S(2)}, u32[]{:S(2)}) collective-permute-start(bf16[16,16,128]{2,1,0:T(8,128)(2,1)S(1)} %add_convert_fusion.10), channel_id=1, source_target_pairs={{0,6},{1,7},{2,4},{3,5},{4,2},{5,3},{6,0},{7,1},{8,14},{9,15},{10,... | collective-permute-start | bytes 196616 | tf_op jit(solution)/shard_map/ppermute | solution.py:460
  28.7 15.2 %collective-permute-start.8 = (bf16[4,256,256]{2,1,0:T(8,128)(2,1)S(1)}, bf16[4,256,256]{2,1,0:T(8,128)(2,1)S(1)}, u32[]{:S(2)}, u32[]{:S(2)}) collective-permute-start(bf16[4,256,256]{2,1,0:T(8,128)(2,1)S(1)} %add_convert_fusion), channel_id=1, source_target_pairs={{0,2},{1,3},{6,4},{7,5},{8,10},{9,11},{14,12},{15,13},{16,18},{17,... | collective-permute-start | bytes 1572872 | tf_op jit(solution)/shard_map/ppermute | solution.py:486
  31.6 12.3 %collective-permute-start.9 = (bf16[4,256,256]{2,1,0:T(8,128)(2,1)S(1)}, bf16[4,256,256]{2,1,0:T(8,128)(2,1)S(1)}, u32[]{:S(2)}, u32[]{:S(2)}) collective-permute-start(bf16[4,256,256]{2,1,0:T(8,128)(2,1)S(1)} %add_convert_fusion), channel_id=1, source_target_pairs={{2,4},{3,5},{4,2},{5,3},{10,12},{11,13},{12,10},{13,11},{18,20},{1... | collective-permute-start | bytes 1572872 | tf_op jit(solution)/shard_map/ppermute | solution.py:487
  32.3 3.2 %collective-permute-start.5 = (bf16[16,16,128]{2,1,0:T(8,128)(2,1)S(1)}, bf16[16,16,128]{2,1,0:T(8,128)(2,1)S(1)}, u32[]{:S(2)}, u32[]{:S(2)}) collective-permute-start(bf16[16,16,128]{2,1,0:T(8,128)(2,1)S(1)} %add_convert_fusion.9), channel_id=1, source_target_pairs={{0,8},{8,0},{16,24},{24,16},{1,9},{9,1},{17,25},{25,17},{2,10},{10... | collective-permute-start | bytes 196616 | tf_op jit(solution)/shard_map/ppermute | solution.py:460
  33.6 4.1 %collective-permute-start.6 = (bf16[16,16,128]{2,1,0:T(8,128)(2,1)S(1)}, bf16[16,16,128]{2,1,0:T(8,128)(2,1)S(1)}, u32[]{:S(2)}, u32[]{:S(2)}) collective-permute-start(bf16[16,16,128]{2,1,0:T(8,128)(2,1)S(1)} %add_convert_fusion.9), channel_id=1, source_target_pairs={{0,16},{8,24},{16,0},{24,8},{1,17},{9,25},{17,1},{25,9},{2,18},{10... | collective-permute-start | bytes 196616 | tf_op jit(solution)/shard_map/ppermute | solution.py:460
  35.5 4.2 %collective-permute-start.7 = (bf16[16,16,128]{2,1,0:T(8,128)(2,1)S(1)}, bf16[16,16,128]{2,1,0:T(8,128)(2,1)S(1)}, u32[]{:S(2)}, u32[]{:S(2)}) collective-permute-start(bf16[16,16,128]{2,1,0:T(8,128)(2,1)S(1)} %add_convert_fusion.9), channel_id=1, source_target_pairs={{0,24},{8,16},{16,8},{24,0},{1,25},{9,17},{17,9},{25,1},{2,26},{10... | collective-permute-start | bytes 196616 | tf_op jit(solution)/shard_map/ppermute | solution.py:460
  39.7 5.1 %collective-permute-start.10 = (bf16[16,16,128]{2,1,0:T(8,128)(2,1)S(1)}, bf16[16,16,128]{2,1,0:T(8,128)(2,1)S(1)}, u32[]{:S(2)}, u32[]{:S(2)}) collective-permute-start(bf16[16,16,128]{2,1,0:T(8,128)(2,1)S(1)} %add_convert_fusion.8.old_ref), channel_id=1, source_target_pairs={{0,1},{1,0},{2,3},{3,2},{4,5},{5,4},{6,7},{7,6},{8,9},{9,8},{10,11... | collective-permute-start | bytes 196616 | tf_op jit(solution)/shard_map/ppermute | solution.py:460
  44.8 17.5 %collective-permute-start.12 = (bf16[3,256,256]{2,1,0:T(8,128)(2,1)S(1)}, bf16[3,256,256]{2,1,0:T(8,128)(2,1)S(1)}, u32[]{:S(2)}, u32[]{:S(2)}) collective-permute-start(bf16[3,256,256]{2,1,0:T(8,128)(2,1)S(1)} %get-tuple-element.51), channel_id=1, source_target_pairs={{0,2},{1,3},{2,0},{3,1},{4,6},{5,7},{6,4},{7,5},{8,10},{9,11},{10,... | collective-permute-start | bytes 1179656 | tf_op jit(solution)/shard_map/ppermute | solution.py:460
  46.6 15.9 %collective-permute-start.13 = (bf16[3,256,256]{2,1,0:T(8,128)(2,1)S(1)}, bf16[3,256,256]{2,1,0:T(8,128)(2,1)S(1)}, u32[]{:S(2)}, u32[]{:S(2)}) collective-permute-start(bf16[3,256,256]{2,1,0:T(8,128)(2,1)S(1)} %get-tuple-element.52), channel_id=1, source_target_pairs={{0,4},{1,5},{2,6},{3,7},{4,0},{5,1},{6,2},{7,3},{8,12},{9,13},{10,... | collective-permute-start | bytes 1179656 | tf_op jit(solution)/shard_map/ppermute | solution.py:460
  62.5 6.2 %collective-permute-start.14 = (bf16[16,16,128]{2,1,0:T(8,128)(2,1)}, bf16[16,16,128]{2,1,0:T(8,128)(2,1)S(1)}, u32[]{:S(2)}, u32[]{:S(2)}) collective-permute-start(bf16[16,16,128]{2,1,0:T(8,128)(2,1)} %get-tuple-element.53), channel_id=1, source_target_pairs={{0,1},{1,0},{2,3},{3,2},{4,5},{5,4},{6,7},{7,6},{8,9},{9,8},{10,11... | collective-permute-start | bytes 196616 | tf_op jit(solution)/shard_map/ppermute | solution.py:460
  69.6 4.1 %collective-permute-start.15 = (bf16[16,16,128]{2,1,0:T(8,128)(2,1)S(1)}, bf16[16,16,128]{2,1,0:T(8,128)(2,1)S(1)}, u32[]{:S(2)}, u32[]{:S(2)}) collective-permute-start(bf16[16,16,128]{2,1,0:T(8,128)(2,1)S(1)} %add_convert_fusion.7), channel_id=1, source_target_pairs={{0,8},{8,0},{16,24},{24,16},{1,9},{9,1},{17,25},{25,17},{2,10},{10... | collective-permute-start | bytes 196616 | tf_op jit(solution)/shard_map/ppermute | solution.py:460
  70.8 3.1 %collective-permute-start.16 = (bf16[16,16,128]{2,1,0:T(8,128)(2,1)S(1)}, bf16[16,16,128]{2,1,0:T(8,128)(2,1)S(1)}, u32[]{:S(2)}, u32[]{:S(2)}) collective-permute-start(bf16[16,16,128]{2,1,0:T(8,128)(2,1)S(1)} %add_convert_fusion.7), channel_id=1, source_target_pairs={{0,16},{8,24},{16,0},{24,8},{1,17},{9,25},{17,1},{25,9},{2,18},{10... | collective-permute-start | bytes 196616 | tf_op jit(solution)/shard_map/ppermute | solution.py:460
  72.1 4.0 %collective-permute-start.17 = (bf16[16,16,128]{2,1,0:T(8,128)(2,1)S(1)}, bf16[16,16,128]{2,1,0:T(8,128)(2,1)S(1)}, u32[]{:S(2)}, u32[]{:S(2)}) collective-permute-start(bf16[16,16,128]{2,1,0:T(8,128)(2,1)S(1)} %add_convert_fusion.7), channel_id=1, source_target_pairs={{0,24},{8,16},{16,8},{24,0},{1,25},{9,17},{17,9},{25,1},{2,26},{10... | collective-permute-start | bytes 196616 | tf_op jit(solution)/shard_map/ppermute | solution.py:460
  72.3 6.3 %collective-permute-start.18 = (bf16[1,256,256]{2,1,0:T(8,128)(2,1)S(1)}, bf16[1,256,256]{2,1,0:T(8,128)(2,1)S(1)}, u32[]{:S(2)}, u32[]{:S(2)}) collective-permute-start(bf16[1,256,256]{2,1,0:T(8,128)(2,1)S(1)} %get-tuple-element.56), channel_id=1, source_target_pairs={{0,2},{1,3},{2,0},{3,1},{4,6},{5,7},{6,4},{7,5},{8,10},{9,11},{10,... | collective-permute-start | bytes 393224 | tf_op jit(solution)/shard_map/ppermute | solution.py:460
  72.3 6.3 %collective-permute-start.19 = (bf16[1,256,256]{2,1,0:T(8,128)(2,1)S(1)}, bf16[1,256,256]{2,1,0:T(8,128)(2,1)S(1)}, u32[]{:S(2)}, u32[]{:S(2)}) collective-permute-start(bf16[1,256,256]{2,1,0:T(8,128)(2,1)S(1)} %get-tuple-element.57), channel_id=1, source_target_pairs={{0,4},{1,5},{2,6},{3,7},{4,0},{5,1},{6,2},{7,3},{8,12},{9,13},{10,... | collective-permute-start | bytes 393224 | tf_op jit(solution)/shard_map/ppermute | solution.py:460
  78.6 4.9 %collective-permute-start.20 = (bf16[16,16,128]{2,1,0:T(8,128)(2,1)S(1)}, bf16[16,16,128]{2,1,0:T(8,128)(2,1)S(1)}, u32[]{:S(2)}, u32[]{:S(2)}) collective-permute-start(bf16[16,16,128]{2,1,0:T(8,128)(2,1)S(1)} %add_convert_fusion.6), channel_id=1, source_target_pairs={{0,2},{1,3},{2,0},{3,1},{4,6},{5,7},{6,4},{7,5},{8,10},{9,11},{10,... | collective-permute-start | bytes 196616 | tf_op jit(solution)/shard_map/ppermute | solution.py:460
  79.6 5.0 %collective-permute-start.21 = (bf16[16,16,128]{2,1,0:T(8,128)(2,1)S(1)}, bf16[16,16,128]{2,1,0:T(8,128)(2,1)S(1)}, u32[]{:S(2)}, u32[]{:S(2)}) collective-permute-start(bf16[16,16,128]{2,1,0:T(8,128)(2,1)S(1)} %add_convert_fusion.6), channel_id=1, source_target_pairs={{0,4},{1,5},{2,6},{3,7},{4,0},{5,1},{6,2},{7,3},{8,12},{9,13},{10,... | collective-permute-start | bytes 196616 | tf_op jit(solution)/shard_map/ppermute | solution.py:460
  80.1 5.4 %collective-permute-start.22 = (bf16[16,16,128]{2,1,0:T(8,128)(2,1)S(1)}, bf16[16,16,128]{2,1,0:T(8,128)(2,1)S(1)}, u32[]{:S(2)}, u32[]{:S(2)}) collective-permute-start(bf16[16,16,128]{2,1,0:T(8,128)(2,1)S(1)} %add_convert_fusion.6), channel_id=1, source_target_pairs={{0,6},{1,7},{2,4},{3,5},{4,2},{5,3},{6,0},{7,1},{8,14},{9,15},{10,... | collective-permute-start | bytes 196616 | tf_op jit(solution)/shard_map/ppermute | solution.py:460
  85.5 6.1 %collective-permute-start.23 = (bf16[16,16,128]{2,1,0:T(8,128)(2,1)S(1)}, bf16[16,16,128]{2,1,0:T(8,128)(2,1)S(1)}, u32[]{:S(2)}, u32[]{:S(2)}) collective-permute-start(bf16[16,16,128]{2,1,0:T(8,128)(2,1)S(1)} %add_convert_fusion.5.old_ref), channel_id=1, source_target_pairs={{0,1},{1,0},{2,3},{3,2},{4,5},{5,4},{6,7},{7,6},{8,9},{9,8},{10,11... | collective-permute-start | bytes 196616 | tf_op jit(solution)/shard_map/ppermute | solution.py:460
  (5 other events, 45.9 us)

commit v3 on v2

v3 whole, which is shorter than its diff:
```python
import functools
import math

import jax
import jax.numpy as jnp
import ml_dtypes
import numpy as np
from jax import lax
from jax.experimental import pallas as pl
from jax.experimental.pallas import tpu as pltpu
from jax.sharding import PartitionSpec as P

BINS = 4
ITERS = 2
K = 256
HALF = K // 2
ROWS = HALF + 16
REACH = 16
DEEP = 8
SLICES = HALF // DEEP
BOTH = ("row", "col")
F32 = jnp.float32
BF16 = jnp.bfloat16


@functools.cache
def cosine_row():
    angle = np.arange(HALF).astype(np.float32) * np.float32(2.0 * math.pi / K)
    return np.broadcast_to(np.cos(angle).astype(np.float32), (8, HALF))


def iota(shape, axis):
    return lax.broadcasted_iota(jnp.int32, shape, axis)


def cosine(row_ref, turns):
    rows, lanes = turns.shape
    row = jnp.broadcast_to(row_ref[:1, :], (rows, HALF))
    found = []
    for first in range(0, lanes, HALF):
        part = turns[:, first : first + HALF]
        value = jnp.take_along_axis(row, part & (HALF - 1), axis=1, mode="promise_in_bounds")
        found.append(jnp.where((part & HALF) == 0, value, -value))
    return found[0] if len(found) == 1 else jnp.concatenate(found, axis=1)


QUARTER = K // 4


def column_order(index):
    return jnp.where(index <= HALF, index, HALF - index)


def fill_forward(row_ref, fwd_one_ref, fwd_two_ref):
    lane = iota((K, K), 1)
    turns = iota((K, K), 0) * jnp.where(lane <= HALF, lane, lane - HALF)
    fwd_one_ref[...] = cosine(row_ref, turns - jnp.where(lane <= HALF, 0, QUARTER)).astype(BF16)
    row = iota((ROWS, K), 0)
    turns = row * iota((ROWS, K), 1)
    for part in range(2):
        table = jnp.where(row <= HALF, cosine(row_ref, turns + part * QUARTER), 0.0)
        fwd_two_ref[part * ROWS : (part + 1) * ROWS, :] = table.astype(BF16)


def fill_inverse(row_ref, inv_one_ref, inv_two_ref):
    row, lane = iota((K, K), 0), iota((K, K), 1)
    turns = column_order(row) * lane
    even, odd = cosine(row_ref, turns).astype(BF16), cosine(row_ref, turns - QUARTER).astype(BF16)
    inv_one_ref[:K, :K] = even
    inv_one_ref[:K, K:] = odd
    inv_one_ref[K:, :K] = -odd
    inv_one_ref[K:, K:] = even
    turns = row * jnp.where(lane <= HALF, lane, lane - HALF) + jnp.where(lane <= HALF, 0, QUARTER)
    scale = jnp.where((lane == 0) | (lane == HALF), 1.0, 2.0)
    inv_two_ref[...] = (scale * cosine(row_ref, turns).astype(BF16).astype(F32)).astype(BF16)


def one_at(rows, lanes):
    return jnp.where(rows == lanes, 1.0, 0.0).astype(BF16)


def dot(a, b):
    return jnp.dot(a, b, preferred_element_type=F32)


def split(a):
    high = a.astype(BF16)
    return (high, (a - high.astype(F32)).astype(BF16))


def negate_columns(a):
    turned = jnp.concatenate([a[:, HALF:], a[:, :HALF]], axis=1)
    lane = lax.broadcasted_iota(jnp.int32, a.shape, 1)
    return jnp.where((lane == 0) | (lane == HALF), a, turned)


def hermitian_part(ref_ref, now_ref):
    reorder = one_at(iota((K, K), 0), column_order(iota((K, K), 1)) & (K - 1))
    row = iota((ROWS, K), 0)
    turn = one_at(jnp.where(row <= HALF, (K - row) & (K - 1), -1), iota((ROWS, K), 1))
    for part, sign in ((0, 1.0), (1, -1.0)):
        straight = jnp.zeros((ROWS, K), F32)
        turned = jnp.zeros((ROWS, K), F32)
        for piece in split(ref_ref[part]):
            piece = dot(piece, reorder).astype(BF16)
            straight = straight + piece[:ROWS].astype(F32)
            turned = turned + dot(turn, piece)
        now_ref[part * ROWS : (part + 1) * ROWS, :] = 0.5 * (straight + sign * negate_columns(turned))


def unpack(core, keep_ref, other_ref):
    halves = []
    for ref in (keep_ref, other_ref):
        rows = []
        for number in range(SLICES):
            piece = ref[number].astype(F32)
            rows.append(jnp.concatenate([piece[:DEEP], piece[DEEP:]], axis=1))
        halves.append(jnp.concatenate(rows, axis=0))
    keep, other = halves
    real, imag = jnp.where(core == 0, keep, other), jnp.where(core == 0, other, keep)
    zero_re, zero_im = real[:1], imag[:1]
    turn_re, turn_im = negate_columns(real[:8])[:1], negate_columns(imag[:8])[:1]
    power = (
        2.0 * jnp.sum(real * real + imag * imag, axis=(0, 1), keepdims=True)
        - jnp.sum(zero_re * zero_re + zero_im * zero_im, axis=(0, 1), keepdims=True)
    ) * (1.0 / (K * K))
    is_first = lax.broadcasted_iota(jnp.int32, (HALF, K), 0) == 0
    real = jnp.where(is_first, 0.5 * (zero_re + turn_re), real)
    imag = jnp.where(is_first, 0.5 * (zero_im - turn_im), imag)
    last_re = 0.5 * (zero_im + turn_im)
    last_im = 0.5 * (turn_re - zero_re)
    return (real, imag, last_re, last_im, lax.rsqrt(power + 1e-06))


def pack(core, total_ref, keep_ref, send_ref):
    is_first = lax.broadcasted_iota(jnp.int32, (HALF, K), 0) == 0
    real = total_ref[:HALF, :]
    imag = total_ref[ROWS : ROWS + HALF, :]
    last_re = total_ref[HALF : HALF + 1, :]
    last_im = total_ref[ROWS + HALF : ROWS + HALF + 1, :]
    real, imag = jnp.where(is_first, real - last_im, real), jnp.where(is_first, imag + last_re, imag)
    for ref, half in ((keep_ref, jnp.where(core == 0, real, imag)), (send_ref, jnp.where(core == 0, imag, real))):
        for number in range(SLICES):
            piece = half[number * DEEP : (number + 1) * DEEP]
            ref[number] = jnp.concatenate([piece[:, :128], piece[:, 128:]], axis=0).astype(ref.dtype)


def forward(first, size, pattern_ref, spec_ref, fwd_one_ref, fwd_two_ref):
    flat = pattern_ref[pl.ds(first, size)].reshape(size * K, K)
    half = dot(flat, fwd_one_ref[...]).astype(BF16)
    is_zero = lax.broadcasted_iota(jnp.int32, (ROWS, HALF), 1) == 0
    for number in range(size):
        both = dot(fwd_two_ref[...], half[number * K : (number + 1) * K])
        cu, cv = both[:ROWS, :HALF], both[:ROWS, HALF:]
        su, sv = both[ROWS:, :HALF], both[ROWS:, HALF:]
        real = jnp.concatenate([cu + jnp.where(is_zero, 0.0, sv), jnp.where(is_zero, cv, cu - sv)], axis=1)
        imag = jnp.concatenate([su - jnp.where(is_zero, 0.0, cv), jnp.where(is_zero, sv, su + cv)], axis=1)
        spec_ref[first + number] = jnp.concatenate([real, imag], axis=0).astype(BF16)


def correlate(first, size, spec_ref, now_ref, cross_ref, inv_one_ref, inv_two_ref, weight_ref):
    for number in range(size):
        spec_re = spec_ref[first + number, :ROWS, :].astype(F32)
        spec_im = spec_ref[first + number, ROWS:, :].astype(F32)
        now_re, now_im = now_ref[:ROWS, :], now_ref[ROWS:, :]
        rows = slice(number * ROWS, (number + 1) * ROWS)
        cross_ref[rows, :K] = (spec_re * now_re + spec_im * now_im).astype(BF16)
        cross_ref[rows, K:] = (spec_im * now_re - spec_re * now_im).astype(BF16)
    both = dot(cross_ref[...], inv_one_ref[...])
    is_first = lax.broadcasted_iota(jnp.int32, (HALF, K), 0) == 0
    for number in range(size):
        mid = both[number * ROWS : (number + 1) * ROWS]
        lower = jnp.where(is_first, mid[HALF : HALF + 1, :K], mid[:HALF, K:])
        corr = dot(inv_two_ref[...], jnp.concatenate([mid[:HALF, :K], lower], axis=0).astype(BF16))
        peak = jnp.max(corr, axis=(0, 1), keepdims=True) * (1.0 / (K * K))
        mean = jnp.sum(corr * corr, axis=(0, 1), keepdims=True) * (1.0 / float(K) ** 6)
        weight = peak / jnp.sqrt(mean + 1e-06)
        weight_ref[pl.ds(first + number, 1), :] = jnp.broadcast_to(weight, (1, 128))


def add_aligned(first, size, scalars_ref, spec_ref, weight_ref, row_ref, total_ref):
    total_re, total_im = total_ref[:ROWS, :], total_ref[ROWS:, :]
    lane = iota((8, K), 1)
    for number in range(size):
        shift_y, shift_x = scalars_ref[2 * (first + number)], scalars_ref[2 * (first + number) + 1]
        weight = weight_ref[pl.ds(first + number, 1), :]
        weight = jnp.concatenate([weight, weight], axis=1)
        turns = column_order(lane) * shift_x
        across_re = weight * cosine(row_ref, turns)[:1]
        across_im = weight * cosine(row_ref, turns + QUARTER)[:1]
        turns = iota((ROWS, HALF), 0) * shift_y
        down_re, down_im = cosine(row_ref, turns), cosine(row_ref, turns + QUARTER)
        down_re = jnp.concatenate([down_re, down_re], axis=1)
        down_im = jnp.concatenate([down_im, down_im], axis=1)
        ramp_re = down_re * across_re - down_im * across_im
        ramp_im = down_re * across_im + down_im * across_re
        spec_re = spec_ref[first + number, :ROWS, :].astype(F32)
        spec_im = spec_ref[first + number, ROWS:, :].astype(F32)
        total_re = total_re + (spec_re * ramp_re - spec_im * ramp_im)
        total_im = total_im + (spec_im * ramp_re + spec_re * ramp_im)
    total_ref[:ROWS, :] = total_re
    total_ref[ROWS:, :] = total_im


def add_bins(first, size, scalars_ref, pattern_ref, weight_ref, bins_ref):
    for number in range(size):
        weight = weight_ref[pl.ds(first + number, 1), :]
        weight = jnp.concatenate([weight, weight], axis=1)
        scaled = (weight * pattern_ref[first + number].astype(F32)).astype(BF16)
        slot = scalars_ref[TARGET + first + number]
        bins_ref[slot] = bins_ref[slot] + scaled


GROUP = 4
COUNT = 16
TARGET = 2 * COUNT
CORE = 3 * COUNT


def first_kernel(
    scalars_ref, row_ref, pattern_hbm, ref_hbm, spec_ref, keep_ref, send_ref, bins_ref,
    pattern_ref, ref_ref, fwd_one_ref, fwd_two_ref, inv_one_ref, inv_two_ref, now_ref, total_ref, cross_ref,
    weight_ref, ref_sem, pattern_sem,
):
    count = pattern_ref.shape[0]
    groups = count // GROUP

    def fetch(number):
        source, target = (ref.at[pl.ds(number * GROUP, GROUP)] for ref in (pattern_hbm, pattern_ref))
        return pltpu.make_async_copy(source, target, pattern_sem.at[number])

    ref_copy = pltpu.make_async_copy(ref_hbm, ref_ref, ref_sem)
    ref_copy.start()
    for number in range(groups):
        fetch(number).start()
    fill_forward(row_ref, fwd_one_ref, fwd_two_ref)
    fill_inverse(row_ref, inv_one_ref, inv_two_ref)
    total_ref[...] = jnp.zeros_like(total_ref)
    bins_ref[...] = jnp.zeros_like(bins_ref)
    weight_ref[...] = jnp.zeros_like(weight_ref)
    spec_ref[:GROUP] = jnp.zeros_like(spec_ref[:GROUP])
    ref_copy.wait()
    hermitian_part(ref_ref, now_ref)

    def finish(first):
        add_aligned(first, GROUP, scalars_ref, spec_ref, weight_ref, row_ref, total_ref)

    def body(number, _):
        first = number * GROUP
        fetch(number).wait()
        finish(jnp.maximum(first - GROUP, 0))
        forward(first, GROUP, pattern_ref, spec_ref, fwd_one_ref, fwd_two_ref)
        correlate(first, GROUP, spec_ref, now_ref, cross_ref, inv_one_ref, inv_two_ref, weight_ref)
        add_bins(first, GROUP, scalars_ref, pattern_ref, weight_ref, bins_ref)
        return 0

    lax.fori_loop(0, groups, body, 0)
    finish(count - GROUP)
    pack(scalars_ref[CORE], total_ref, keep_ref, send_ref)


def second_kernel(
    scalars_ref, row_ref, spec_ref, old_ref, old_other_ref, keep_ref, send_ref, weight_ref,
    inv_one_ref, inv_two_ref, now_ref, total_ref, cross_ref,
):
    count = spec_ref.shape[0]
    fill_inverse(row_ref, inv_one_ref, inv_two_ref)
    total_ref[...] = jnp.zeros_like(total_ref)
    weight_ref[...] = jnp.zeros_like(weight_ref)
    real, imag, last_re, last_im, scale = unpack(scalars_ref[CORE], old_ref, old_other_ref)
    is_first = iota((ROWS - HALF, K), 0) == 0
    now_ref[:HALF, :] = real * scale
    now_ref[HALF:ROWS, :] = jnp.where(is_first, last_re * scale, 0.0)
    now_ref[ROWS : ROWS + HALF, :] = imag * scale
    now_ref[ROWS + HALF :, :] = jnp.where(is_first, last_im * scale, 0.0)

    def finish(first):
        add_aligned(first, GROUP, scalars_ref, spec_ref, weight_ref, row_ref, total_ref)

    def body(number, _):
        first = number * GROUP
        finish(jnp.maximum(first - GROUP, 0))
        correlate(first, GROUP, spec_ref, now_ref, cross_ref, inv_one_ref, inv_two_ref, weight_ref)
        return 0

    lax.fori_loop(0, count // GROUP, body, 0)
    finish(count - GROUP)
    pack(scalars_ref[CORE], total_ref, keep_ref, send_ref)


def last_kernel(scalars_ref, old_ref, old_other_ref, out_ref):
    real, imag, last_re, last_im, scale = unpack(scalars_ref[CORE], old_ref, old_other_ref)
    turn = one_at(HALF - iota((HALF, HALF), 0), iota((HALF, HALF), 1))
    back = one_at(column_order(iota((K, K), 0)) & (K - 1), iota((K, K), 1))
    is_first = iota((HALF, K), 0) == 0
    for part, (body, row_128) in enumerate(((real, last_re), (imag, last_im))):
        turned = negate_columns(dot(turn, body.astype(BF16)))
        turned = jnp.where(is_first, row_128, turned if part == 0 else -turned)
        both = jnp.concatenate([body, turned], axis=0)
        natural = sum(dot(piece, back) for piece in split(both))
        out_ref[part] = natural * scale


def params(mebibytes):
    return pltpu.CompilerParams(vmem_limit_bytes=mebibytes * 1024 * 1024)


SCALARS = pl.BlockSpec(memory_space=pltpu.SMEM)
VMEM = pl.BlockSpec(memory_space=pltpu.VMEM)
HBM = pl.BlockSpec(memory_space=pltpu.HBM)
HALF_SHAPE = (SLICES, 2 * DEEP, 128)
TABLES = [((K, K), BF16), ((2 * ROWS, K), BF16), ((2 * K, 2 * K), BF16), ((K, K), BF16)]
WORK = [((2 * ROWS, K), F32), ((2 * ROWS, K), F32), ((GROUP * ROWS, 2 * K), BF16)]


def scratch(*shapes):
    return [pltpu.VMEM(*shape) for shape in shapes]


def in_hbm(array):
    return pltpu.with_memory_space_constraint(array, pltpu.HBM)


def run_first(patterns, ref_spectrum, scalars, bins):
    count = patterns.shape[0]
    return pl.pallas_call(
        first_kernel,
        out_shape=(
            pltpu.VMEM((count, 2 * ROWS, K), BF16),
            pltpu.VMEM(HALF_SHAPE, F32),
            pltpu.VMEM(HALF_SHAPE, BF16),
            pltpu.VMEM((bins, K, K), BF16),
        ),
        in_specs=[SCALARS, VMEM, HBM, HBM],
        out_specs=(VMEM, VMEM, VMEM, VMEM),
        scratch_shapes=scratch(
            (patterns.shape, BF16), (ref_spectrum.shape, F32), *TABLES, *WORK, ((count, 128), F32)
        )
        + [pltpu.SemaphoreType.DMA, pltpu.SemaphoreType.DMA((count // GROUP,))],
        compiler_params=params(32),
        cost_estimate=pl.CostEstimate(flops=int(4e9), bytes_accessed=int(12e6), transcendentals=0),
        name="forward_and_correlate",
    )(scalars, jnp.asarray(cosine_row()), in_hbm(patterns), in_hbm(ref_spectrum))


def run_second(spectra, keep, other, scalars):
    count = spectra.shape[0]
    return pl.pallas_call(
        second_kernel,
        out_shape=(
            pltpu.VMEM(HALF_SHAPE, F32),
            pltpu.VMEM(HALF_SHAPE, BF16),
            pltpu.VMEM((count, 128), F32),
        ),
        in_specs=[SCALARS, VMEM, VMEM, VMEM, VMEM],
        out_specs=(VMEM, VMEM, VMEM),
        scratch_shapes=scratch(*TABLES[2:], *WORK),
        compiler_params=params(32),
        cost_estimate=pl.CostEstimate(flops=int(3e9), bytes_accessed=int(4e6), transcendentals=0),
        name="correlate_again",
    )(scalars, jnp.asarray(cosine_row()), spectra, keep, other)


def run_last(keep, other, scalars):
    return pl.pallas_call(
        last_kernel,
        out_shape=jax.ShapeDtypeStruct((2, K, K), F32),
        in_specs=[SCALARS, VMEM, VMEM],
        out_specs=VMEM,
        compiler_params=params(16),
        cost_estimate=pl.CostEstimate(flops=int(1e8), bytes_accessed=int(1e6), transcendentals=0),
        name="finish",
    )(scalars, keep, other)


def add_halves(*halves):
    values = [half.astype(F32) for half in halves]
    while len(values) > 1:
        values = [values[i] + values[i + 1] for i in range(0, len(values), 2)]
    return values[0].astype(BF16)


def on_device(patterns, ref_spectrum, shifts, bin_owner, bin_index):
    columns, lines = lax.axis_size("col"), lax.axis_size("row")
    me = lax.axis_index("col")
    owner = bin_owner.reshape(-1)
    chips = columns // 2
    targets = ((owner ^ me) % 2) * (chips * BINS) + ((owner // 2) ^ (me // 2)) * BINS + bin_index
    scalars = jnp.concatenate([shifts.reshape(-1), targets, (me % 2).reshape(1).astype(jnp.int32)])

    def send(array, far, axis="col"):
        return lax.ppermute(array, axis, [(i, i ^ far) for i in range(lax.axis_size(axis))])

    def over_chips(half):
        return [half] + [send(half, 2 * far) for far in range(1, chips)]

    def over_lines(half):
        return [half] + [send(half, far, "row") for far in range(1, lines)]

    spectra, keep, away, bins = run_first(patterns, ref_spectrum, scalars, columns * BINS)
    mine, other, other_far = jnp.split(bins, (chips * BINS, (2 * chips - 1) * BINS))
    half = add_halves(keep, send(away, 1))
    half, other, other_far = lax.optimization_barrier((half, other, other_far))
    half = add_halves(*over_chips(half))
    other, other_far = send(other, 1), send(other_far, 1)
    mine = mine.reshape(chips, BINS, K, K)
    other = other.reshape(chips - 1, BINS, K, K)

    def chip_bins(far, *more, low=0, high=BINS):
        there = other[far] if far < chips - 1 else other_far
        arrays = [array[low:high].astype(F32) for array in (mine[far], there, *more)]
        return sum(arrays[1:], arrays[0])

    binned = chip_bins(0)
    if chips == 4:
        block = chip_bins(3).astype(BF16)
        half, block = lax.optimization_barrier((half, block))
        pairs = lambda hops: [(2 * a + core, 2 * b + core) for a, b in hops for core in range(2)]
        passing = lax.ppermute(block, "col", pairs([(0, 1), (3, 2)]))
        middle = lax.ppermute(block, "col", pairs([(1, 2), (2, 1)]))
        half = add_halves(*over_lines(half))
        other_half = send(half, 1)
        half, passing, middle = lax.optimization_barrier((half, passing, middle))
        cut = BINS // 2
        blocks = [
            (chip_bins(1, low=low, high=high).astype(BF16), chip_bins(2, passing, low=low, high=high).astype(BF16))
            for low, high in ((0, cut), (cut, BINS))
        ]
        half, other_half, blocks = lax.optimization_barrier((half, other_half, blocks))
        lower = (send(blocks[0][0], 2), send(blocks[0][1], 4))
        keep, away, weight = run_second(spectra, half, other_half, scalars)
        away, lower = lax.optimization_barrier((away, lower))
        upper = (send(blocks[1][0], 2), send(blocks[1][1], 4))
        halves = over_lines(add_halves(keep, send(away, 1)))
        halves, upper = lax.optimization_barrier((halves, upper))
        half = add_halves(*halves)
        binned = binned + middle.astype(F32)
        for a, b in zip(lower, upper):
            binned = binned + jnp.concatenate([a, b]).astype(F32)
    else:
        half = add_halves(*over_lines(half))
        for far in range(1, chips):
            binned = binned + send(chip_bins(far).astype(BF16), 2 * far).astype(F32)
        keep, away, weight = run_second(spectra, half, send(half, 1), scalars)
        half = add_halves(*over_lines(add_halves(keep, send(away, 1))))
    half = add_halves(*over_chips(half))
    return (run_last(half, send(half, 1), scalars), weight[:, 0], binned)


def solution(mesh):
    placed = (P(BOTH, None, None), P(), P(BOTH, None), P(BOTH, None), P(BOTH))
    return jax.shard_map(
        on_device,
        mesh=mesh,
        in_specs=placed,
        out_specs=(P(), P(BOTH), P(BOTH, None, None)),
        check_vma=False,
    )
```

time: 95.5 us -> 85 us (0.89)
  Pallas kernels: 23.2 us -> 17.7 us
  other arithmetic: 6.06 us -> 2.79 us
  starting transfers between devices: 37.8 us -> 36.2 us
    pallas_call x2, Pallas kernels: 20.4 us -> 16 us  [the longest x1 9.94 us: run_first(): pl.pallas_call(first_kernel, out_shape=(pltpu.VMEM((count, 2 * ROWS, K),...]
    convert_element_type x6, other arithmetic: 2 us -> 0.19 us  [add_halves(): return values[0].astype(BF16)]
    ppermute x22, starting transfers between devices: 34.3 us -> 32.7 us  [send(): lax.ppermute(array, axis, [(i, i ^ far) for i in range(lax.axis_size(axis...]
    pallas_call x1, Pallas kernels: 2.84 us -> 1.74 us  [run_last(): pl.pallas_call(last_kernel, out_shape=jax.ShapeDtypeStruct((2, K, K), F32...]
    convert_element_type x1, other arithmetic: 1.17 us -> 0.14 us  [on_device(): block = chip_bins(3).astype(BF16)]
  transfers between devices with their start and end apart: 24 -> 24, of which waited for: 14 -> 11; matrix products, arithmetic and copies ran while one was open for 4% -> 3% of each run, Pallas kernels for 9% -> 7%
where the time goes in v3:
time: 85 us; the launch traced here: 84.8 us
  starting transfers between devices  36.2 us (43%)
  waiting for transfers between devices  24.9 us (29%)
  Pallas kernels  17.7 us (21%)
  other arithmetic  2.79 us (3%)
  local copies, waits for them, and re-layouts  2.26 us (3%)
    ppermute x22, starting transfers between devices, send(): lax.ppermute(array, axis, [(i, i ^ far) for i in range(lax.axis_size(axis...  32.7 us
    ppermute x22, waiting for transfers between devices, send(): lax.ppermute(array, axis, [(i, i ^ far) for i in range(lax.axis_size(axis...  24.9 us
    pallas_call x1, Pallas kernels, run_first(): pl.pallas_call(first_kernel, out_shape=(pltpu.VMEM((count, 2 * ROWS, K),...  9.94 us
    pallas_call x1, Pallas kernels, run_second(): pl.pallas_call(second_kernel, out_shape=(pltpu.VMEM(HALF_SHAPE, F32), plt...  6.03 us
    ppermute x1, starting transfers between devices, on_device(): passing = lax.ppermute(block, 'col', pairs([(0, 1), (3, 2)]))  2.88 us
    pallas_call x1, Pallas kernels, run_last(): pl.pallas_call(last_kernel, out_shape=jax.ShapeDtypeStruct((2, K, K), F32...  1.74 us
  transfers between devices with their start and end apart: 24, of which 11 were waited for; matrix products, arithmetic and copies ran while one was open for 3% of the time, Pallas kernels for 7%

profile of v3, /device:TPU:1, one launch (start us, length us, event | category | flops | bytes accessed | tf_op | source)
XLA Modules:
  0.0 84.8 jit_solution(4525649799595521610)
XLA Ops:
  2.9 9.9 %forward_and_correlate.1 = (bf16[16,288,256]{2,1,0:T(8,128)(2,1)S(1)}, f32[16,16,128]{2,1,0:T(8,128)S(1)}, bf16[16,16,128]{2,1,0:T(8,128)(2,1)S(1)}, bf16[32,256,256]{2,1,0:T(8,128)(2,1)S(1)}) custom-call(s32[49]{0:T(128)S(1)} %pad_add_fusion.scalars_ref, f32[8,128]{1,0:T(8,128)S(1)} %jit_solution_.3.row_ref, bf16[16,256,256]{2,1,0:T(8,128)(2,1)} %pattern_hbm.1, ...), custom_call_target="tpu_custom_call" | custom-call | flops 4000000000 | bytes 12000000 | tf_op jit(solution)/shard_map/forward_and_correlate/pallas_call | solution.py:326
  14.8 2.4 %collective-permute-start.1 = (bf16[16,16,128]{2,1,0:T(8,128)(2,1)S(1)}, bf16[16,16,128]{2,1,0:T(8,128)(2,1)S(1)}, u32[]{:S(2)}, u32[]{:S(2)}) collective-permute-start(bf16[16,16,128]{2,1,0:T(8,128)(2,1)S(1)} %add_convert_fusion.10), channel_id=1, source_target_pairs={{0,2},{1,3},{2,0},{3,1},{4,6},{5,7},{6,4},{7,5},{8,10},{9,11},{10,... | collective-permute-start | bytes 196616 | tf_op jit(solution)/shard_map/ppermute | solution.py:392
  17.2 2.3 %collective-permute-start.2 = (bf16[16,16,128]{2,1,0:T(8,128)(2,1)S(1)}, bf16[16,16,128]{2,1,0:T(8,128)(2,1)S(1)}, u32[]{:S(2)}, u32[]{:S(2)}) collective-permute-start(bf16[16,16,128]{2,1,0:T(8,128)(2,1)S(1)} %add_convert_fusion.10), channel_id=1, source_target_pairs={{0,4},{1,5},{2,6},{3,7},{4,0},{5,1},{6,2},{7,3},{8,12},{9,13},{10,... | collective-permute-start | bytes 196616 | tf_op jit(solution)/shard_map/ppermute | solution.py:392
  19.6 1.9 %collective-permute-done.2 = bf16[16,16,128]{2,1,0:T(8,128)(2,1)S(1)} collective-permute-done((bf16[16,16,128]{2,1,0:T(8,128)(2,1)S(1)}, bf16[16,16,128]{2,1,0:T(8,128)(2,1)S(1)}, u32[]{:S(2)}, u32[]{:S(2)}) %collective-permute-start.2) | collective-permute-done | bytes 65568 | tf_op jit(solution)/shard_map/ppermute | solution.py:392
  21.5 3.1 %collective-permute-done.3 = bf16[16,16,128]{2,1,0:T(8,128)(2,1)S(1)} collective-permute-done((bf16[16,16,128]{2,1,0:T(8,128)(2,1)S(1)}, bf16[16,16,128]{2,1,0:T(8,128)(2,1)S(1)}, u32[]{:S(2)}, u32[]{:S(2)}) %collective-permute-start.3) | collective-permute-done | bytes 65568 | tf_op jit(solution)/shard_map/ppermute | solution.py:392
  24.8 2.9 %collective-permute-start.8 = (bf16[4,256,256]{2,1,0:T(8,128)(2,1)S(1)}, bf16[4,256,256]{2,1,0:T(8,128)(2,1)S(1)}, u32[]{:S(2)}, u32[]{:S(2)}) collective-permute-start(bf16[4,256,256]{2,1,0:T(8,128)(2,1)S(1)} %add_convert_fusion), channel_id=1, source_target_pairs={{0,2},{1,3},{6,4},{7,5},{8,10},{9,11},{14,12},{15,13},{16,18},{17,... | collective-permute-start | bytes 1572872 | tf_op jit(solution)/shard_map/ppermute | solution.py:419
  28.4 1.3 %collective-permute-start.5 = (bf16[16,16,128]{2,1,0:T(8,128)(2,1)S(1)}, bf16[16,16,128]{2,1,0:T(8,128)(2,1)S(1)}, u32[]{:S(2)}, u32[]{:S(2)}) collective-permute-start(bf16[16,16,128]{2,1,0:T(8,128)(2,1)S(1)} %add_convert_fusion.9), channel_id=1, source_target_pairs={{0,8},{8,0},{16,24},{24,16},{1,9},{9,1},{17,25},{25,17},{2,10},{10... | collective-permute-start | bytes 196616 | tf_op jit(solution)/shard_map/ppermute | solution.py:392
  29.6 1.2 %collective-permute-start.6 = (bf16[16,16,128]{2,1,0:T(8,128)(2,1)S(1)}, bf16[16,16,128]{2,1,0:T(8,128)(2,1)S(1)}, u32[]{:S(2)}, u32[]{:S(2)}) collective-permute-start(bf16[16,16,128]{2,1,0:T(8,128)(2,1)S(1)} %add_convert_fusion.9), channel_id=1, source_target_pairs={{0,16},{8,24},{16,0},{24,8},{1,17},{9,25},{17,1},{25,9},{2,18},{10... | collective-permute-start | bytes 196616 | tf_op jit(solution)/shard_map/ppermute | solution.py:392
  31.5 2.2 %collective-permute-start.7 = (bf16[16,16,128]{2,1,0:T(8,128)(2,1)S(1)}, bf16[16,16,128]{2,1,0:T(8,128)(2,1)S(1)}, u32[]{:S(2)}, u32[]{:S(2)}) collective-permute-start(bf16[16,16,128]{2,1,0:T(8,128)(2,1)S(1)} %add_convert_fusion.9), channel_id=1, source_target_pairs={{0,24},{8,16},{16,8},{24,0},{1,25},{9,17},{17,9},{25,1},{2,26},{10... | collective-permute-start | bytes 196616 | tf_op jit(solution)/shard_map/ppermute | solution.py:392
  33.7 2.0 %collective-permute-done.7 = bf16[16,16,128]{2,1,0:T(8,128)(2,1)S(1)} collective-permute-done((bf16[16,16,128]{2,1,0:T(8,128)(2,1)S(1)}, bf16[16,16,128]{2,1,0:T(8,128)(2,1)S(1)}, u32[]{:S(2)}, u32[]{:S(2)}) %collective-permute-start.7) | collective-permute-done | bytes 65568 | tf_op jit(solution)/shard_map/ppermute | solution.py:392
  35.7 4.2 %collective-permute-start.10 = (bf16[16,16,128]{2,1,0:T(8,128)(2,1)S(1)}, bf16[16,16,128]{2,1,0:T(8,128)(2,1)S(1)}, u32[]{:S(2)}, u32[]{:S(2)}) collective-permute-start(bf16[16,16,128]{2,1,0:T(8,128)(2,1)S(1)} %add_convert_fusion.8.old_ref), channel_id=1, source_target_pairs={{0,1},{1,0},{2,3},{3,2},{4,5},{5,4},{6,7},{7,6},{8,9},{9,8},{10,11... | collective-permute-start | bytes 196616 | tf_op jit(solution)/shard_map/ppermute | solution.py:392
  40.8 1.8 %collective-permute-start.12 = (bf16[2,256,256]{2,1,0:T(8,128)(2,1)S(1)}, bf16[2,256,256]{2,1,0:T(8,128)(2,1)S(1)}, u32[]{:S(2)}, u32[]{:S(2)}) collective-permute-start(bf16[2,256,256]{2,1,0:T(8,128)(2,1)S(1)} %get-tuple-element.48), channel_id=1, source_target_pairs={{0,2},{1,3},{2,0},{3,1},{4,6},{5,7},{6,4},{7,5},{8,10},{9,11},{10,... | collective-permute-start | bytes 786440 | tf_op jit(solution)/shard_map/ppermute | solution.py:392
  43.3 6.0 %correlate_again.1 = (f32[16,16,128]{2,1,0:T(8,128)S(1)}, bf16[16,16,128]{2,1,0:T(8,128)(2,1)S(1)}, f32[16,128]{1,0:T(8,128)S(1)}) custom-call(s32[49]{0:T(128)S(1)} %pad_add_fusion.scalars_ref, f32[8,128]{1,0:T(8,128)S(1)} %jit_solution_.3.row_ref, bf16[16,288,256]{2,1,0:T(8,128)(2,1)S(1)} %get-tuple-element.33.spec_ref, ...), custom_call_target="tpu_custom_call" | custom-call | flops 3000000000 | bytes 4000000 | tf_op jit(solution)/shard_map/correlate_again/pallas_call | solution.py:348
  49.3 2.7 %collective-permute-done.12 = bf16[2,256,256]{2,1,0:T(8,128)(2,1)S(1)} collective-permute-done((bf16[2,256,256]{2,1,0:T(8,128)(2,1)S(1)}, bf16[2,256,256]{2,1,0:T(8,128)(2,1)S(1)}, u32[]{:S(2)}, u32[]{:S(2)}) %collective-permute-start.12) | collective-permute-done | bytes 262176 | tf_op jit(solution)/shard_map/ppermute | solution.py:392
  52.8 5.1 %collective-permute-start.14 = (bf16[16,16,128]{2,1,0:T(8,128)(2,1)S(1)}, bf16[16,16,128]{2,1,0:T(8,128)(2,1)S(1)}, u32[]{:S(2)}, u32[]{:S(2)}) collective-permute-start(bf16[16,16,128]{2,1,0:T(8,128)(2,1)S(1)} %get-tuple-element.50), channel_id=1, source_target_pairs={{0,1},{1,0},{2,3},{3,2},{4,5},{5,4},{6,7},{7,6},{8,9},{9,8},{10,11... | collective-permute-start | bytes 196616 | tf_op jit(solution)/shard_map/ppermute | solution.py:392
  57.9 1.4 %collective-permute-start.19 = (bf16[2,256,256]{2,1,0:T(8,128)(2,1)S(1)}, bf16[2,256,256]{2,1,0:T(8,128)(2,1)S(1)}, u32[]{:S(2)}, u32[]{:S(2)}) collective-permute-start(bf16[2,256,256]{2,1,0:T(8,128)(2,1)S(1)} %get-tuple-element.52), channel_id=1, source_target_pairs={{0,4},{1,5},{2,6},{3,7},{4,0},{5,1},{6,2},{7,3},{8,12},{9,13},{10,... | collective-permute-start | bytes 786440 | tf_op jit(solution)/shard_map/ppermute | solution.py:392
  59.4 1.3 %collective-permute-start.15 = (bf16[16,16,128]{2,1,0:T(8,128)(2,1)S(1)}, bf16[16,16,128]{2,1,0:T(8,128)(2,1)S(1)}, u32[]{:S(2)}, u32[]{:S(2)}) collective-permute-start(bf16[16,16,128]{2,1,0:T(8,128)(2,1)S(1)} %add_convert_fusion.7), channel_id=1, source_target_pairs={{0,8},{8,0},{16,24},{24,16},{1,9},{9,1},{17,25},{25,17},{2,10},{10... | collective-permute-start | bytes 196616 | tf_op jit(solution)/shard_map/ppermute | solution.py:392
  62.1 8.3 %collective-permute-done.18 = bf16[2,256,256]{2,1,0:T(8,128)(2,1)S(1)} collective-permute-done((bf16[2,256,256]{2,1,0:T(8,128)(2,1)S(1)}, bf16[2,256,256]{2,1,0:T(8,128)(2,1)S(1)}, u32[]{:S(2)}, u32[]{:S(2)}) %collective-permute-start.18) | collective-permute-done | bytes 262176 | tf_op jit(solution)/shard_map/ppermute | solution.py:392
  70.4 2.0 %collective-permute-done.19 = bf16[2,256,256]{2,1,0:T(8,128)(2,1)S(1)} collective-permute-done((bf16[2,256,256]{2,1,0:T(8,128)(2,1)S(1)}, bf16[2,256,256]{2,1,0:T(8,128)(2,1)S(1)}, u32[]{:S(2)}, u32[]{:S(2)}) %collective-permute-start.19) | collective-permute-done | bytes 262176 | tf_op jit(solution)/shard_map/ppermute | solution.py:392
  72.8 3.3 %collective-permute-start.22 = (bf16[16,16,128]{2,1,0:T(8,128)(2,1)S(1)}, bf16[16,16,128]{2,1,0:T(8,128)(2,1)S(1)}, u32[]{:S(2)}, u32[]{:S(2)}) collective-permute-start(bf16[16,16,128]{2,1,0:T(8,128)(2,1)S(1)} %add_convert_fusion.6), channel_id=1, source_target_pairs={{0,6},{1,7},{2,4},{3,5},{4,2},{5,3},{6,0},{7,1},{8,14},{9,15},{10,... | collective-permute-start | bytes 196616 | tf_op jit(solution)/shard_map/ppermute | solution.py:392
  76.7 1.8 %collective-permute-done.22 = bf16[16,16,128]{2,1,0:T(8,128)(2,1)S(1)} collective-permute-done((bf16[16,16,128]{2,1,0:T(8,128)(2,1)S(1)}, bf16[16,16,128]{2,1,0:T(8,128)(2,1)S(1)}, u32[]{:S(2)}, u32[]{:S(2)}) %collective-permute-start.22) | collective-permute-done | bytes 65568 | tf_op jit(solution)/shard_map/ppermute | solution.py:392
  78.6 3.1 %collective-permute-start.23 = (bf16[16,16,128]{2,1,0:T(8,128)(2,1)S(1)}, bf16[16,16,128]{2,1,0:T(8,128)(2,1)S(1)}, u32[]{:S(2)}, u32[]{:S(2)}) collective-permute-start(bf16[16,16,128]{2,1,0:T(8,128)(2,1)S(1)} %add_convert_fusion.5.old_ref), channel_id=1, source_target_pairs={{0,1},{1,0},{2,3},{3,2},{4,5},{5,4},{6,7},{7,6},{8,9},{9,8},{10,11... | collective-permute-start | bytes 196616 | tf_op jit(solution)/shard_map/ppermute | solution.py:392
  81.7 1.3 %convert_add_fusion = f32[4,256,256]{2,1,0:T(8,128)} fusion(bf16[4,256,256]{2,1,0:T(8,128)(2,1)S(1)} %collective-permute-done.9, bf16[12,256,256]{2,1,0:T(8,128)(2,1)S(1)} %collective-permute-done.11, bf16[2,256,256]{2,1,0:T(8,128)(2,1)S(1)} %collective-permute-done.18, bf16[2,256,256]{2,1,0:T(8,128)(2,1)S(1)} %collective-permute-done.12, ...), kind=kLoop, calls=%fused_computation | loop fusion | flops 2883584 | bytes 3670016 | tf_op jit(solution)/shard_map/add | solution.py:439
  83.0 1.7 %finish.1 = f32[2,256,256]{2,1,0:T(8,128)} custom-call(s32[49]{0:T(128)S(1)} %pad_add_fusion.scalars_ref, bf16[16,16,128]{2,1,0:T(8,128)(2,1)S(1)} %add_convert_fusion.5.old_ref, bf16[16,16,128]{2,1,0:T(8,128)(2,1)S(1)} %collective-permute-done.23.old_other_ref), custom_call_target="tpu_custom_call" | custom-call | flops 100000000 | bytes 1000000 | tf_op jit(solution)/shard_map/finish/pallas_call | solution.py:365
  (44 shorter events, 10.6 us)
Async XLA Ops:
  12.9 1.3 %collective-permute-start = (bf16[16,16,128]{2,1,0:T(8,128)(2,1)S(1)}, bf16[16,16,128]{2,1,0:T(8,128)(2,1)S(1)}, u32[]{:S(2)}, u32[]{:S(2)}) collective-permute-start(bf16[16,16,128]{2,1,0:T(8,128)(2,1)S(1)} %get-tuple-element.35), channel_id=1, source_target_pairs={{0,1},{1,0},{2,3},{3,2},{4,5},{5,4},{6,7},{7,6},{8,9},{9,8},{10,11... | collective-permute-start | bytes 196616 | tf_op jit(solution)/shard_map/ppermute | solution.py:392
  14.2 25.7 %collective-permute-start.11 = (bf16[12,256,256]{2,1,0:T(8,128)(2,1)S(1)}, bf16[12,256,256]{2,1,0:T(8,128)(2,1)S(1)}, u32[]{:S(2)}, u32[]{:S(2)}) collective-permute-start(bf16[12,256,256]{2,1,0:T(8,128)(2,1)S(1)} %split.7), channel_id=1, source_target_pairs={{0,1},{1,0},{2,3},{3,2},{4,5},{5,4},{6,7},{7,6},{8,9},{9,8},{10,11... | collective-permute-start | bytes 4718600 | tf_op jit(solution)/shard_map/ppermute | solution.py:392
  14.4 10.2 %collective-permute-start.4 = (bf16[4,256,256]{2,1,0:T(8,128)(2,1)S(1)}, bf16[4,256,256]{2,1,0:T(8,128)(2,1)S(1)}, u32[]{:S(2)}, u32[]{:S(2)}) collective-permute-start(bf16[4,256,256]{2,1,0:T(8,128)(2,1)S(1)} %split.8), channel_id=1, source_target_pairs={{0,1},{1,0},{2,3},{3,2},{4,5},{5,4},{6,7},{7,6},{8,9},{9,8},{10,11... | collective-permute-start | bytes 1572872 | tf_op jit(solution)/shard_map/ppermute | solution.py:392
  14.8 4.8 %collective-permute-start.1 = (bf16[16,16,128]{2,1,0:T(8,128)(2,1)S(1)}, bf16[16,16,128]{2,1,0:T(8,128)(2,1)S(1)}, u32[]{:S(2)}, u32[]{:S(2)}) collective-permute-start(bf16[16,16,128]{2,1,0:T(8,128)(2,1)S(1)} %add_convert_fusion.10), channel_id=1, source_target_pairs={{0,2},{1,3},{2,0},{3,1},{4,6},{5,7},{6,4},{7,5},{8,10},{9,11},{10,... | collective-permute-start | bytes 196616 | tf_op jit(solution)/shard_map/ppermute | solution.py:392
  17.2 4.3 %collective-permute-start.2 = (bf16[16,16,128]{2,1,0:T(8,128)(2,1)S(1)}, bf16[16,16,128]{2,1,0:T(8,128)(2,1)S(1)}, u32[]{:S(2)}, u32[]{:S(2)}) collective-permute-start(bf16[16,16,128]{2,1,0:T(8,128)(2,1)S(1)} %add_convert_fusion.10), channel_id=1, source_target_pairs={{0,4},{1,5},{2,6},{3,7},{4,0},{5,1},{6,2},{7,3},{8,12},{9,13},{10,... | collective-permute-start | bytes 196616 | tf_op jit(solution)/shard_map/ppermute | solution.py:392
  19.6 5.0 %collective-permute-start.3 = (bf16[16,16,128]{2,1,0:T(8,128)(2,1)S(1)}, bf16[16,16,128]{2,1,0:T(8,128)(2,1)S(1)}, u32[]{:S(2)}, u32[]{:S(2)}) collective-permute-start(bf16[16,16,128]{2,1,0:T(8,128)(2,1)S(1)} %add_convert_fusion.10), channel_id=1, source_target_pairs={{0,6},{1,7},{2,4},{3,5},{4,2},{5,3},{6,0},{7,1},{8,14},{9,15},{10,... | collective-permute-start | bytes 196616 | tf_op jit(solution)/shard_map/ppermute | solution.py:392
  24.8 15.2 %collective-permute-start.8 = (bf16[4,256,256]{2,1,0:T(8,128)(2,1)S(1)}, bf16[4,256,256]{2,1,0:T(8,128)(2,1)S(1)}, u32[]{:S(2)}, u32[]{:S(2)}) collective-permute-start(bf16[4,256,256]{2,1,0:T(8,128)(2,1)S(1)} %add_convert_fusion), channel_id=1, source_target_pairs={{0,2},{1,3},{6,4},{7,5},{8,10},{9,11},{14,12},{15,13},{16,18},{17,... | collective-permute-start | bytes 1572872 | tf_op jit(solution)/shard_map/ppermute | solution.py:419
  27.7 12.3 %collective-permute-start.9 = (bf16[4,256,256]{2,1,0:T(8,128)(2,1)S(1)}, bf16[4,256,256]{2,1,0:T(8,128)(2,1)S(1)}, u32[]{:S(2)}, u32[]{:S(2)}) collective-permute-start(bf16[4,256,256]{2,1,0:T(8,128)(2,1)S(1)} %add_convert_fusion), channel_id=1, source_target_pairs={{2,4},{3,5},{4,2},{5,3},{10,12},{11,13},{12,10},{13,11},{18,20},{1... | collective-permute-start | bytes 1572872 | tf_op jit(solution)/shard_map/ppermute | solution.py:420
  28.4 3.2 %collective-permute-start.5 = (bf16[16,16,128]{2,1,0:T(8,128)(2,1)S(1)}, bf16[16,16,128]{2,1,0:T(8,128)(2,1)S(1)}, u32[]{:S(2)}, u32[]{:S(2)}) collective-permute-start(bf16[16,16,128]{2,1,0:T(8,128)(2,1)S(1)} %add_convert_fusion.9), channel_id=1, source_target_pairs={{0,8},{8,0},{16,24},{24,16},{1,9},{9,1},{17,25},{25,17},{2,10},{10... | collective-permute-start | bytes 196616 | tf_op jit(solution)/shard_map/ppermute | solution.py:392
  29.6 4.1 %collective-permute-start.6 = (bf16[16,16,128]{2,1,0:T(8,128)(2,1)S(1)}, bf16[16,16,128]{2,1,0:T(8,128)(2,1)S(1)}, u32[]{:S(2)}, u32[]{:S(2)}) collective-permute-start(bf16[16,16,128]{2,1,0:T(8,128)(2,1)S(1)} %add_convert_fusion.9), channel_id=1, source_target_pairs={{0,16},{8,24},{16,0},{24,8},{1,17},{9,25},{17,1},{25,9},{2,18},{10... | collective-permute-start | bytes 196616 | tf_op jit(solution)/shard_map/ppermute | solution.py:392
  31.5 4.2 %collective-permute-start.7 = (bf16[16,16,128]{2,1,0:T(8,128)(2,1)S(1)}, bf16[16,16,128]{2,1,0:T(8,128)(2,1)S(1)}, u32[]{:S(2)}, u32[]{:S(2)}) collective-permute-start(bf16[16,16,128]{2,1,0:T(8,128)(2,1)S(1)} %add_convert_fusion.9), channel_id=1, source_target_pairs={{0,24},{8,16},{16,8},{24,0},{1,25},{9,17},{17,9},{25,1},{2,26},{10... | collective-permute-start | bytes 196616 | tf_op jit(solution)/shard_map/ppermute | solution.py:392
  35.7 5.1 %collective-permute-start.10 = (bf16[16,16,128]{2,1,0:T(8,128)(2,1)S(1)}, bf16[16,16,128]{2,1,0:T(8,128)(2,1)S(1)}, u32[]{:S(2)}, u32[]{:S(2)}) collective-permute-start(bf16[16,16,128]{2,1,0:T(8,128)(2,1)S(1)} %add_convert_fusion.8.old_ref), channel_id=1, source_target_pairs={{0,1},{1,0},{2,3},{3,2},{4,5},{5,4},{6,7},{7,6},{8,9},{9,8},{10,11... | collective-permute-start | bytes 196616 | tf_op jit(solution)/shard_map/ppermute | solution.py:392
  40.8 11.2 %collective-permute-start.12 = (bf16[2,256,256]{2,1,0:T(8,128)(2,1)S(1)}, bf16[2,256,256]{2,1,0:T(8,128)(2,1)S(1)}, u32[]{:S(2)}, u32[]{:S(2)}) collective-permute-start(bf16[2,256,256]{2,1,0:T(8,128)(2,1)S(1)} %get-tuple-element.48), channel_id=1, source_target_pairs={{0,2},{1,3},{2,0},{3,1},{4,6},{5,7},{6,4},{7,5},{8,10},{9,11},{10,... | collective-permute-start | bytes 786440 | tf_op jit(solution)/shard_map/ppermute | solution.py:392
  42.6 10.2 %collective-permute-start.13 = (bf16[2,256,256]{2,1,0:T(8,128)(2,1)S(1)}, bf16[2,256,256]{2,1,0:T(8,128)(2,1)S(1)}, u32[]{:S(2)}, u32[]{:S(2)}) collective-permute-start(bf16[2,256,256]{2,1,0:T(8,128)(2,1)S(1)} %get-tuple-element.49), channel_id=1, source_target_pairs={{0,4},{1,5},{2,6},{3,7},{4,0},{5,1},{6,2},{7,3},{8,12},{9,13},{10,... | collective-permute-start | bytes 786440 | tf_op jit(solution)/shard_map/ppermute | solution.py:392
  52.8 6.5 %collective-permute-start.14 = (bf16[16,16,128]{2,1,0:T(8,128)(2,1)S(1)}, bf16[16,16,128]{2,1,0:T(8,128)(2,1)S(1)}, u32[]{:S(2)}, u32[]{:S(2)}) collective-permute-start(bf16[16,16,128]{2,1,0:T(8,128)(2,1)S(1)} %get-tuple-element.50), channel_id=1, source_target_pairs={{0,1},{1,0},{2,3},{3,2},{4,5},{5,4},{6,7},{7,6},{8,9},{9,8},{10,11... | collective-permute-start | bytes 196616 | tf_op jit(solution)/shard_map/ppermute | solution.py:392
  57.9 12.5 %collective-permute-start.18 = (bf16[2,256,256]{2,1,0:T(8,128)(2,1)S(1)}, bf16[2,256,256]{2,1,0:T(8,128)(2,1)S(1)}, u32[]{:S(2)}, u32[]{:S(2)}) collective-permute-start(bf16[2,256,256]{2,1,0:T(8,128)(2,1)S(1)} %get-tuple-element.51), channel_id=1, source_target_pairs={{0,2},{1,3},{2,0},{3,1},{4,6},{5,7},{6,4},{7,5},{8,10},{9,11},{10,... | collective-permute-start | bytes 786440 | tf_op jit(solution)/shard_map/ppermute | solution.py:392
  57.9 14.5 %collective-permute-start.19 = (bf16[2,256,256]{2,1,0:T(8,128)(2,1)S(1)}, bf16[2,256,256]{2,1,0:T(8,128)(2,1)S(1)}, u32[]{:S(2)}, u32[]{:S(2)}) collective-permute-start(bf16[2,256,256]{2,1,0:T(8,128)(2,1)S(1)} %get-tuple-element.52), channel_id=1, source_target_pairs={{0,4},{1,5},{2,6},{3,7},{4,0},{5,1},{6,2},{7,3},{8,12},{9,13},{10,... | collective-permute-start | bytes 786440 | tf_op jit(solution)/shard_map/ppermute | solution.py:392
  59.4 13.1 %collective-permute-start.15 = (bf16[16,16,128]{2,1,0:T(8,128)(2,1)S(1)}, bf16[16,16,128]{2,1,0:T(8,128)(2,1)S(1)}, u32[]{:S(2)}, u32[]{:S(2)}) collective-permute-start(bf16[16,16,128]{2,1,0:T(8,128)(2,1)S(1)} %add_convert_fusion.7), channel_id=1, source_target_pairs={{0,8},{8,0},{16,24},{24,16},{1,9},{9,1},{17,25},{25,17},{2,10},{10... | collective-permute-start | bytes 196616 | tf_op jit(solution)/shard_map/ppermute | solution.py:392
  60.7 11.8 %collective-permute-start.16 = (bf16[16,16,128]{2,1,0:T(8,128)(2,1)S(1)}, bf16[16,16,128]{2,1,0:T(8,128)(2,1)S(1)}, u32[]{:S(2)}, u32[]{:S(2)}) collective-permute-start(bf16[16,16,128]{2,1,0:T(8,128)(2,1)S(1)} %add_convert_fusion.7), channel_id=1, source_target_pairs={{0,16},{8,24},{16,0},{24,8},{1,17},{9,25},{17,1},{25,9},{2,18},{10... | collective-permute-start | bytes 196616 | tf_op jit(solution)/shard_map/ppermute | solution.py:392
  61.9 10.5 %collective-permute-start.17 = (bf16[16,16,128]{2,1,0:T(8,128)(2,1)S(1)}, bf16[16,16,128]{2,1,0:T(8,128)(2,1)S(1)}, u32[]{:S(2)}, u32[]{:S(2)}) collective-permute-start(bf16[16,16,128]{2,1,0:T(8,128)(2,1)S(1)} %add_convert_fusion.7), channel_id=1, source_target_pairs={{0,24},{8,16},{16,8},{24,0},{1,25},{9,17},{17,9},{25,1},{2,26},{10... | collective-permute-start | bytes 196616 | tf_op jit(solution)/shard_map/ppermute | solution.py:392
  72.5 4.2 %collective-permute-start.20 = (bf16[16,16,128]{2,1,0:T(8,128)(2,1)S(1)}, bf16[16,16,128]{2,1,0:T(8,128)(2,1)S(1)}, u32[]{:S(2)}, u32[]{:S(2)}) collective-permute-start(bf16[16,16,128]{2,1,0:T(8,128)(2,1)S(1)} %add_convert_fusion.6), channel_id=1, source_target_pairs={{0,2},{1,3},{2,0},{3,1},{4,6},{5,7},{6,4},{7,5},{8,10},{9,11},{10,... | collective-permute-start | bytes 196616 | tf_op jit(solution)/shard_map/ppermute | solution.py:392
  72.6 4.2 %collective-permute-start.21 = (bf16[16,16,128]{2,1,0:T(8,128)(2,1)S(1)}, bf16[16,16,128]{2,1,0:T(8,128)(2,1)S(1)}, u32[]{:S(2)}, u32[]{:S(2)}) collective-permute-start(bf16[16,16,128]{2,1,0:T(8,128)(2,1)S(1)} %add_convert_fusion.6), channel_id=1, source_target_pairs={{0,4},{1,5},{2,6},{3,7},{4,0},{5,1},{6,2},{7,3},{8,12},{9,13},{10,... | collective-permute-start | bytes 196616 | tf_op jit(solution)/shard_map/ppermute | solution.py:392
  72.8 5.7 %collective-permute-start.22 = (bf16[16,16,128]{2,1,0:T(8,128)(2,1)S(1)}, bf16[16,16,128]{2,1,0:T(8,128)(2,1)S(1)}, u32[]{:S(2)}, u32[]{:S(2)}) collective-permute-start(bf16[16,16,128]{2,1,0:T(8,128)(2,1)S(1)} %add_convert_fusion.6), channel_id=1, source_target_pairs={{0,6},{1,7},{2,4},{3,5},{4,2},{5,3},{6,0},{7,1},{8,14},{9,15},{10,... | collective-permute-start | bytes 196616 | tf_op jit(solution)/shard_map/ppermute | solution.py:392
  78.6 4.4 %collective-permute-start.23 = (bf16[16,16,128]{2,1,0:T(8,128)(2,1)S(1)}, bf16[16,16,128]{2,1,0:T(8,128)(2,1)S(1)}, u32[]{:S(2)}, u32[]{:S(2)}) collective-permute-start(bf16[16,16,128]{2,1,0:T(8,128)(2,1)S(1)} %add_convert_fusion.5.old_ref), channel_id=1, source_target_pairs={{0,1},{1,0},{2,3},{3,2},{4,5},{5,4},{6,7},{7,6},{8,9},{9,8},{10,11... | collective-permute-start | bytes 196616 | tf_op jit(solution)/shard_map/ppermute | solution.py:392

commit v4 on v3

--- a/solution.py
+++ b/solution.py
@@ -406,9 +406,9 @@
     mine = mine.reshape(chips, BINS, K, K)
     other = other.reshape(chips - 1, BINS, K, K)
 
-    def chip_bins(far, *more, low=0, high=BINS):
+    def chip_bins(far, *more):
         there = other[far] if far < chips - 1 else other_far
-        arrays = [array[low:high].astype(F32) for array in (mine[far], there, *more)]
+        arrays = [array.astype(F32) for array in (mine[far], there, *more)]
         return sum(arrays[1:], arrays[0])
 
     binned = chip_bins(0)
@@ -420,23 +420,12 @@
         middle = lax.ppermute(block, "col", pairs([(1, 2), (2, 1)]))
         half = add_halves(*over_lines(half))
         other_half = send(half, 1)
-        half, passing, middle = lax.optimization_barrier((half, passing, middle))
-        cut = BINS // 2
-        blocks = [
-            (chip_bins(1, low=low, high=high).astype(BF16), chip_bins(2, passing, low=low, high=high).astype(BF16))
-            for low, high in ((0, cut), (cut, BINS))
-        ]
-        half, other_half, blocks = lax.optimization_barrier((half, other_half, blocks))
-        lower = (send(blocks[0][0], 2), send(blocks[0][1], 4))
-        keep, away, weight = run_second(spectra, half, other_half, scalars)
-        away, lower = lax.optimization_barrier((away, lower))
-        upper = (send(blocks[1][0], 2), send(blocks[1][1], 4))
+        arrived = [middle, send(chip_bins(1).astype(BF16), 2), send(chip_bins(2, passing).astype(BF16), 4)]
+        keep, away, weight = run_second(spectra, half, send(half, 1), scalars)
         halves = over_lines(add_halves(keep, send(away, 1)))
-        halves, upper = lax.optimization_barrier((halves, upper))
+        halves, arrived = lax.optimization_barrier((halves, arrived))
         half = add_halves(*halves)
-        binned = binned + middle.astype(F32)
-        for a, b in zip(lower, upper):
-            binned = binned + jnp.concatenate([a, b]).astype(F32)
+        binned = sum([array.astype(F32) for array in arrived], binned)
     else:
         half = add_halves(*over_lines(half))
         for far in range(1, chips):

time: 85 us -> 81.4 us (0.958)
  starting transfers between devices: 36.2 us -> 33.6 us
  waiting for transfers between devices: 24.9 us -> 24 us
    ppermute x22 -> x20, starting transfers between devices: 32.7 us -> 30.9 us  [send(): lax.ppermute(array, axis, [(i, i ^ far) for i in range(lax.axis_size(axis...]
    ppermute x22 -> x20, waiting for transfers between devices: 24.9 us -> 23.5 us  [send(): lax.ppermute(array, axis, [(i, i ^ far) for i in range(lax.axis_size(axis...]
  transfers between devices with their start and end apart: 24 -> 22, of which waited for: 11 -> 14; matrix products, arithmetic and copies ran while one was open for 3% -> 3% of each run, Pallas kernels for 7% -> 7%
where the time goes in v4:
time: 81.4 us; the launch traced here: 81.1 us
  starting transfers between devices  33.6 us (41%)
  waiting for transfers between devices  24 us (29%)
  Pallas kernels  17.7 us (22%)
  other arithmetic  2.75 us (3%)
  local copies, waits for them, and re-layouts  2.27 us (3%)
    ppermute x20, starting transfers between devices, send(): lax.ppermute(array, axis, [(i, i ^ far) for i in range(lax.axis_size(axis...  30.9 us
    ppermute x20, waiting for transfers between devices, send(): lax.ppermute(array, axis, [(i, i ^ far) for i in range(lax.axis_size(axis...  23.5 us
    pallas_call x1, Pallas kernels, run_first(): pl.pallas_call(first_kernel, out_shape=(pltpu.VMEM((count, 2 * ROWS, K),...  9.94 us
    pallas_call x1, Pallas kernels, run_second(): pl.pallas_call(second_kernel, out_shape=(pltpu.VMEM(HALF_SHAPE, F32), plt...  6.03 us
    ppermute x1, starting transfers between devices, on_device(): passing = lax.ppermute(block, 'col', pairs([(0, 1), (3, 2)]))  2.1 us
    pallas_call x1, Pallas kernels, run_last(): pl.pallas_call(last_kernel, out_shape=jax.ShapeDtypeStruct((2, K, K), F32...  1.74 us
  transfers between devices with their start and end apart: 22, of which 14 were waited for; matrix products, arithmetic and copies ran while one was open for 3% of the time, Pallas kernels for 7%

profile of v4, /device:TPU:1, one launch (start us, length us, event | category | flops | bytes accessed | tf_op | source)
XLA Modules:
  0.0 81.1 jit_solution(1267898359783326441)
XLA Ops:
  2.9 9.9 %forward_and_correlate.1 = (bf16[16,288,256]{2,1,0:T(8,128)(2,1)S(1)}, f32[16,16,128]{2,1,0:T(8,128)S(1)}, bf16[16,16,128]{2,1,0:T(8,128)(2,1)S(1)}, bf16[32,256,256]{2,1,0:T(8,128)(2,1)S(1)}) custom-call(s32[49]{0:T(128)S(1)} %pad_add_fusion.scalars_ref, f32[8,128]{1,0:T(8,128)S(1)} %jit_solution_.3.row_ref, bf16[16,256,256]{2,1,0:T(8,128)(2,1)} %pattern_hbm.1, ...), custom_call_target="tpu_custom_call" | custom-call | flops 4000000000 | bytes 12000000 | tf_op jit(solution)/shard_map/forward_and_correlate/pallas_call | solution.py:326
  13.2 1.0 %collective-permute-done = bf16[16,16,128]{2,1,0:T(8,128)(2,1)S(1)} collective-permute-done((bf16[16,16,128]{2,1,0:T(8,128)(2,1)S(1)}, bf16[16,16,128]{2,1,0:T(8,128)(2,1)S(1)}, u32[]{:S(2)}, u32[]{:S(2)}) %collective-permute-start) | collective-permute-done | bytes 65568 | tf_op jit(solution)/shard_map/ppermute | solution.py:392
  14.8 4.5 %collective-permute-start.3 = (bf16[16,16,128]{2,1,0:T(8,128)(2,1)S(1)}, bf16[16,16,128]{2,1,0:T(8,128)(2,1)S(1)}, u32[]{:S(2)}, u32[]{:S(2)}) collective-permute-start(bf16[16,16,128]{2,1,0:T(8,128)(2,1)S(1)} %add_convert_fusion.8), channel_id=1, source_target_pairs={{0,6},{1,7},{2,4},{3,5},{4,2},{5,3},{6,0},{7,1},{8,14},{9,15},{10,... | collective-permute-start | bytes 196616 | tf_op jit(solution)/shard_map/ppermute | solution.py:392
  19.6 1.9 %collective-permute-done.3 = bf16[16,16,128]{2,1,0:T(8,128)(2,1)S(1)} collective-permute-done((bf16[16,16,128]{2,1,0:T(8,128)(2,1)S(1)}, bf16[16,16,128]{2,1,0:T(8,128)(2,1)S(1)}, u32[]{:S(2)}, u32[]{:S(2)}) %collective-permute-start.3) | collective-permute-done | bytes 65568 | tf_op jit(solution)/shard_map/ppermute | solution.py:392
  21.4 3.5 %collective-permute-done.2 = bf16[16,16,128]{2,1,0:T(8,128)(2,1)S(1)} collective-permute-done((bf16[16,16,128]{2,1,0:T(8,128)(2,1)S(1)}, bf16[16,16,128]{2,1,0:T(8,128)(2,1)S(1)}, u32[]{:S(2)}, u32[]{:S(2)}) %collective-permute-start.2) | collective-permute-done | bytes 65568 | tf_op jit(solution)/shard_map/ppermute | solution.py:392
  25.2 2.1 %collective-permute-start.16 = (bf16[4,256,256]{2,1,0:T(8,128)(2,1)S(1)}, bf16[4,256,256]{2,1,0:T(8,128)(2,1)S(1)}, u32[]{:S(2)}, u32[]{:S(2)}) collective-permute-start(bf16[4,256,256]{2,1,0:T(8,128)(2,1)S(1)} %add_convert_fusion.2), channel_id=1, source_target_pairs={{0,2},{1,3},{6,4},{7,5},{8,10},{9,11},{14,12},{15,13},{16,18},{17,... | collective-permute-start | bytes 1572872 | tf_op jit(solution)/shard_map/ppermute | solution.py:419
  27.3 2.2 %collective-permute-start.7 = (bf16[16,16,128]{2,1,0:T(8,128)(2,1)S(1)}, bf16[16,16,128]{2,1,0:T(8,128)(2,1)S(1)}, u32[]{:S(2)}, u32[]{:S(2)}) collective-permute-start(bf16[16,16,128]{2,1,0:T(8,128)(2,1)S(1)} %add_convert_fusion.7), channel_id=1, source_target_pairs={{0,24},{8,16},{16,8},{24,0},{1,25},{9,17},{17,9},{25,1},{2,26},{10... | collective-permute-start | bytes 196616 | tf_op jit(solution)/shard_map/ppermute | solution.py:392
  30.0 1.4 %collective-permute-done.7 = bf16[16,16,128]{2,1,0:T(8,128)(2,1)S(1)} collective-permute-done((bf16[16,16,128]{2,1,0:T(8,128)(2,1)S(1)}, bf16[16,16,128]{2,1,0:T(8,128)(2,1)S(1)}, u32[]{:S(2)}, u32[]{:S(2)}) %collective-permute-start.7) | collective-permute-done | bytes 65568 | tf_op jit(solution)/shard_map/ppermute | solution.py:392
  32.9 3.5 %collective-permute-start.8 = (bf16[16,16,128]{2,1,0:T(8,128)(2,1)S(1)}, bf16[16,16,128]{2,1,0:T(8,128)(2,1)S(1)}, u32[]{:S(2)}, u32[]{:S(2)}) collective-permute-start(bf16[16,16,128]{2,1,0:T(8,128)(2,1)S(1)} %add_convert_fusion.6.old_ref), channel_id=1, source_target_pairs={{0,1},{1,0},{2,3},{3,2},{4,5},{5,4},{6,7},{7,6},{8,9},{9,8},{10,11... | collective-permute-start | bytes 196616 | tf_op jit(solution)/shard_map/ppermute | solution.py:392
  37.3 1.9 %collective-permute-start.17 = (bf16[4,256,256]{2,1,0:T(8,128)(2,1)S(1)}, bf16[4,256,256]{2,1,0:T(8,128)(2,1)S(1)}, u32[]{:S(2)}, u32[]{:S(2)}) collective-permute-start(bf16[4,256,256]{2,1,0:T(8,128)(2,1)S(1)} %get-tuple-element.41), channel_id=1, source_target_pairs={{0,4},{1,5},{2,6},{3,7},{4,0},{5,1},{6,2},{7,3},{8,12},{9,13},{10,... | collective-permute-start | bytes 1572872 | tf_op jit(solution)/shard_map/ppermute | solution.py:392
  39.7 6.0 %correlate_again.1 = (f32[16,16,128]{2,1,0:T(8,128)S(1)}, bf16[16,16,128]{2,1,0:T(8,128)(2,1)S(1)}, f32[16,128]{1,0:T(8,128)S(1)}) custom-call(s32[49]{0:T(128)S(1)} %pad_add_fusion.scalars_ref, f32[8,128]{1,0:T(8,128)S(1)} %jit_solution_.3.row_ref, bf16[16,288,256]{2,1,0:T(8,128)(2,1)S(1)} %get-tuple-element.22.spec_ref, ...), custom_call_target="tpu_custom_call" | custom-call | flops 3000000000 | bytes 4000000 | tf_op jit(solution)/shard_map/correlate_again/pallas_call | solution.py:348
  45.7 2.8 %collective-permute-start.9 = (bf16[16,16,128]{2,1,0:T(8,128)(2,1)S(1)}, bf16[16,16,128]{2,1,0:T(8,128)(2,1)S(1)}, u32[]{:S(2)}, u32[]{:S(2)}) collective-permute-start(bf16[16,16,128]{2,1,0:T(8,128)(2,1)S(1)} %get-tuple-element.30), channel_id=1, source_target_pairs={{0,1},{1,0},{2,3},{3,2},{4,5},{5,4},{6,7},{7,6},{8,9},{9,8},{10,11... | collective-permute-start | bytes 196616 | tf_op jit(solution)/shard_map/ppermute | solution.py:392
  48.5 0.9 %collective-permute-done.9 = bf16[16,16,128]{2,1,0:T(8,128)(2,1)S(1)} collective-permute-done((bf16[16,16,128]{2,1,0:T(8,128)(2,1)S(1)}, bf16[16,16,128]{2,1,0:T(8,128)(2,1)S(1)}, u32[]{:S(2)}, u32[]{:S(2)}) %collective-permute-start.9) | collective-permute-done | bytes 65568 | tf_op jit(solution)/shard_map/ppermute | solution.py:392
  49.4 2.2 %collective-permute-start.12 = (bf16[16,16,128]{2,1,0:T(8,128)(2,1)S(1)}, bf16[16,16,128]{2,1,0:T(8,128)(2,1)S(1)}, u32[]{:S(2)}, u32[]{:S(2)}) collective-permute-start(bf16[16,16,128]{2,1,0:T(8,128)(2,1)S(1)} %add_convert_fusion.5), channel_id=1, source_target_pairs={{0,24},{8,16},{16,8},{24,0},{1,25},{9,17},{17,9},{25,1},{2,26},{10... | collective-permute-start | bytes 196616 | tf_op jit(solution)/shard_map/ppermute | solution.py:392
  51.9 1.6 %collective-permute-done.12 = bf16[16,16,128]{2,1,0:T(8,128)(2,1)S(1)} collective-permute-done((bf16[16,16,128]{2,1,0:T(8,128)(2,1)S(1)}, bf16[16,16,128]{2,1,0:T(8,128)(2,1)S(1)}, u32[]{:S(2)}, u32[]{:S(2)}) %collective-permute-start.12) | collective-permute-done | bytes 65568 | tf_op jit(solution)/shard_map/ppermute | solution.py:392
  53.5 1.2 %collective-permute-start.10 = (bf16[16,16,128]{2,1,0:T(8,128)(2,1)S(1)}, bf16[16,16,128]{2,1,0:T(8,128)(2,1)S(1)}, u32[]{:S(2)}, u32[]{:S(2)}) collective-permute-start(bf16[16,16,128]{2,1,0:T(8,128)(2,1)S(1)} %add_convert_fusion.5), channel_id=1, source_target_pairs={{0,8},{8,0},{16,24},{24,16},{1,9},{9,1},{17,25},{25,17},{2,10},{10... | collective-permute-start | bytes 196616 | tf_op jit(solution)/shard_map/ppermute | solution.py:392
  55.0 1.6 %collective-permute-done.10 = bf16[16,16,128]{2,1,0:T(8,128)(2,1)S(1)} collective-permute-done((bf16[16,16,128]{2,1,0:T(8,128)(2,1)S(1)}, bf16[16,16,128]{2,1,0:T(8,128)(2,1)S(1)}, u32[]{:S(2)}, u32[]{:S(2)}) %collective-permute-start.10) | collective-permute-done | bytes 65568 | tf_op jit(solution)/shard_map/ppermute | solution.py:392
  56.6 8.7 %collective-permute-done.17 = bf16[4,256,256]{2,1,0:T(8,128)(2,1)S(1)} collective-permute-done((bf16[4,256,256]{2,1,0:T(8,128)(2,1)S(1)}, bf16[4,256,256]{2,1,0:T(8,128)(2,1)S(1)}, u32[]{:S(2)}, u32[]{:S(2)}) %collective-permute-start.17) | collective-permute-done | bytes 524320 | tf_op jit(solution)/shard_map/ppermute | solution.py:392
  65.8 3.1 %collective-permute-start.18 = (bf16[16,16,128]{2,1,0:T(8,128)(2,1)S(1)}, bf16[16,16,128]{2,1,0:T(8,128)(2,1)S(1)}, u32[]{:S(2)}, u32[]{:S(2)}) collective-permute-start(bf16[16,16,128]{2,1,0:T(8,128)(2,1)S(1)} %add_convert_fusion.4), channel_id=1, source_target_pairs={{0,2},{1,3},{2,0},{3,1},{4,6},{5,7},{6,4},{7,5},{8,10},{9,11},{10,... | collective-permute-start | bytes 196616 | tf_op jit(solution)/shard_map/ppermute | solution.py:392
  69.6 0.9 %collective-permute-done.20 = bf16[16,16,128]{2,1,0:T(8,128)(2,1)S(1)} collective-permute-done((bf16[16,16,128]{2,1,0:T(8,128)(2,1)S(1)}, bf16[16,16,128]{2,1,0:T(8,128)(2,1)S(1)}, u32[]{:S(2)}, u32[]{:S(2)}) %collective-permute-start.20) | collective-permute-done | bytes 65568 | tf_op jit(solution)/shard_map/ppermute | solution.py:392
  70.5 0.8 collective-permute-done.19
  71.4 6.7 %collective-permute-start.21 = (bf16[16,16,128]{2,1,0:T(8,128)(2,1)S(1)}, bf16[16,16,128]{2,1,0:T(8,128)(2,1)S(1)}, u32[]{:S(2)}, u32[]{:S(2)}) collective-permute-start(bf16[16,16,128]{2,1,0:T(8,128)(2,1)S(1)} %add_convert_fusion.3.old_ref), channel_id=1, source_target_pairs={{0,1},{1,0},{2,3},{3,2},{4,5},{5,4},{6,7},{7,6},{8,9},{9,8},{10,11... | collective-permute-start | bytes 196616 | tf_op jit(solution)/shard_map/ppermute | solution.py:392
  78.1 1.3 %convert_add_fusion = f32[4,256,256]{2,1,0:T(8,128)} fusion(bf16[4,256,256]{2,1,0:T(8,128)(2,1)S(1)} %collective-permute-done.17, bf16[4,256,256]{2,1,0:T(8,128)(2,1)S(1)} %collective-permute-done.15, bf16[4,256,256]{2,1,0:T(8,128)(2,1)S(1)} %collective-permute-done.13, bf16[12,256,256]{2,1,0:T(8,128)(2,1)S(1)} %collective-permute-done.14, ...), kind=kLoop, calls=%fused_computation | loop fusion | flops 2359296 | bytes 3670016 | tf_op jit(solution)/shard_map/add | solution.py:428
  79.4 1.7 %finish.1 = f32[2,256,256]{2,1,0:T(8,128)} custom-call(s32[49]{0:T(128)S(1)} %pad_add_fusion.scalars_ref, bf16[16,16,128]{2,1,0:T(8,128)(2,1)S(1)} %add_convert_fusion.3.old_ref, bf16[16,16,128]{2,1,0:T(8,128)(2,1)S(1)} %collective-permute-done.21.old_other_ref), custom_call_target="tpu_custom_call" | custom-call | flops 100000000 | bytes 1000000 | tf_op jit(solution)/shard_map/finish/pallas_call | solution.py:365
  (40 shorter events, 8.7 us)
Async XLA Ops:
  12.9 1.3 %collective-permute-start = (bf16[16,16,128]{2,1,0:T(8,128)(2,1)S(1)}, bf16[16,16,128]{2,1,0:T(8,128)(2,1)S(1)}, u32[]{:S(2)}, u32[]{:S(2)}) collective-permute-start(bf16[16,16,128]{2,1,0:T(8,128)(2,1)S(1)} %get-tuple-element.24), channel_id=1, source_target_pairs={{0,1},{1,0},{2,3},{3,2},{4,5},{5,4},{6,7},{7,6},{8,9},{9,8},{10,11... | collective-permute-start | bytes 196616 | tf_op jit(solution)/shard_map/ppermute | solution.py:392
  14.2 22.8 %collective-permute-start.14 = (bf16[12,256,256]{2,1,0:T(8,128)(2,1)S(1)}, bf16[12,256,256]{2,1,0:T(8,128)(2,1)S(1)}, u32[]{:S(2)}, u32[]{:S(2)}) collective-permute-start(bf16[12,256,256]{2,1,0:T(8,128)(2,1)S(1)} %split.7), channel_id=1, source_target_pairs={{0,1},{1,0},{2,3},{3,2},{4,5},{5,4},{6,7},{7,6},{8,9},{9,8},{10,11... | collective-permute-start | bytes 4718600 | tf_op jit(solution)/shard_map/ppermute | solution.py:392
  14.4 10.6 %collective-permute-start.4 = (bf16[4,256,256]{2,1,0:T(8,128)(2,1)S(1)}, bf16[4,256,256]{2,1,0:T(8,128)(2,1)S(1)}, u32[]{:S(2)}, u32[]{:S(2)}) collective-permute-start(bf16[4,256,256]{2,1,0:T(8,128)(2,1)S(1)} %split.8), channel_id=1, source_target_pairs={{0,1},{1,0},{2,3},{3,2},{4,5},{5,4},{6,7},{7,6},{8,9},{9,8},{10,11... | collective-permute-start | bytes 1572872 | tf_op jit(solution)/shard_map/ppermute | solution.py:392
  14.8 6.6 %collective-permute-start.3 = (bf16[16,16,128]{2,1,0:T(8,128)(2,1)S(1)}, bf16[16,16,128]{2,1,0:T(8,128)(2,1)S(1)}, u32[]{:S(2)}, u32[]{:S(2)}) collective-permute-start(bf16[16,16,128]{2,1,0:T(8,128)(2,1)S(1)} %add_convert_fusion.8), channel_id=1, source_target_pairs={{0,6},{1,7},{2,4},{3,5},{4,2},{5,3},{6,0},{7,1},{8,14},{9,15},{10,... | collective-permute-start | bytes 196616 | tf_op jit(solution)/shard_map/ppermute | solution.py:392
  19.3 5.7 %collective-permute-start.2 = (bf16[16,16,128]{2,1,0:T(8,128)(2,1)S(1)}, bf16[16,16,128]{2,1,0:T(8,128)(2,1)S(1)}, u32[]{:S(2)}, u32[]{:S(2)}) collective-permute-start(bf16[16,16,128]{2,1,0:T(8,128)(2,1)S(1)} %add_convert_fusion.8), channel_id=1, source_target_pairs={{0,4},{1,5},{2,6},{3,7},{4,0},{5,1},{6,2},{7,3},{8,12},{9,13},{10,... | collective-permute-start | bytes 196616 | tf_op jit(solution)/shard_map/ppermute | solution.py:392
  19.3 5.7 %collective-permute-start.1 = (bf16[16,16,128]{2,1,0:T(8,128)(2,1)S(1)}, bf16[16,16,128]{2,1,0:T(8,128)(2,1)S(1)}, u32[]{:S(2)}, u32[]{:S(2)}) collective-permute-start(bf16[16,16,128]{2,1,0:T(8,128)(2,1)S(1)} %add_convert_fusion.8), channel_id=1, source_target_pairs={{0,2},{1,3},{2,0},{3,1},{4,6},{5,7},{6,4},{7,5},{8,10},{9,11},{10,... | collective-permute-start | bytes 196616 | tf_op jit(solution)/shard_map/ppermute | solution.py:392
  25.2 11.8 %collective-permute-start.16 = (bf16[4,256,256]{2,1,0:T(8,128)(2,1)S(1)}, bf16[4,256,256]{2,1,0:T(8,128)(2,1)S(1)}, u32[]{:S(2)}, u32[]{:S(2)}) collective-permute-start(bf16[4,256,256]{2,1,0:T(8,128)(2,1)S(1)} %add_convert_fusion.2), channel_id=1, source_target_pairs={{0,2},{1,3},{6,4},{7,5},{8,10},{9,11},{14,12},{15,13},{16,18},{17,... | collective-permute-start | bytes 1572872 | tf_op jit(solution)/shard_map/ppermute | solution.py:419
  27.3 4.1 %collective-permute-start.7 = (bf16[16,16,128]{2,1,0:T(8,128)(2,1)S(1)}, bf16[16,16,128]{2,1,0:T(8,128)(2,1)S(1)}, u32[]{:S(2)}, u32[]{:S(2)}) collective-permute-start(bf16[16,16,128]{2,1,0:T(8,128)(2,1)S(1)} %add_convert_fusion.7), channel_id=1, source_target_pairs={{0,24},{8,16},{16,8},{24,0},{1,25},{9,17},{17,9},{25,1},{2,26},{10... | collective-permute-start | bytes 196616 | tf_op jit(solution)/shard_map/ppermute | solution.py:392
  29.5 3.1 %collective-permute-start.6 = (bf16[16,16,128]{2,1,0:T(8,128)(2,1)S(1)}, bf16[16,16,128]{2,1,0:T(8,128)(2,1)S(1)}, u32[]{:S(2)}, u32[]{:S(2)}) collective-permute-start(bf16[16,16,128]{2,1,0:T(8,128)(2,1)S(1)} %add_convert_fusion.7), channel_id=1, source_target_pairs={{0,16},{8,24},{16,0},{24,8},{1,17},{9,25},{17,1},{25,9},{2,18},{10... | collective-permute-start | bytes 196616 | tf_op jit(solution)/shard_map/ppermute | solution.py:392
  29.8 3.1 %collective-permute-start.5 = (bf16[16,16,128]{2,1,0:T(8,128)(2,1)S(1)}, bf16[16,16,128]{2,1,0:T(8,128)(2,1)S(1)}, u32[]{:S(2)}, u32[]{:S(2)}) collective-permute-start(bf16[16,16,128]{2,1,0:T(8,128)(2,1)S(1)} %add_convert_fusion.7), channel_id=1, source_target_pairs={{0,8},{8,0},{16,24},{24,16},{1,9},{9,1},{17,25},{25,17},{2,10},{10... | collective-permute-start | bytes 196616 | tf_op jit(solution)/shard_map/ppermute | solution.py:392
  31.4 25.2 %collective-permute-start.13 = (bf16[4,256,256]{2,1,0:T(8,128)(2,1)S(1)}, bf16[4,256,256]{2,1,0:T(8,128)(2,1)S(1)}, u32[]{:S(2)}, u32[]{:S(2)}) collective-permute-start(bf16[4,256,256]{2,1,0:T(8,128)(2,1)S(1)} %add_convert_fusion.2), channel_id=1, source_target_pairs={{2,4},{3,5},{4,2},{5,3},{10,12},{11,13},{12,10},{13,11},{18,20},{1... | collective-permute-start | bytes 1572872 | tf_op jit(solution)/shard_map/ppermute | solution.py:420
  32.9 6.8 %collective-permute-start.8 = (bf16[16,16,128]{2,1,0:T(8,128)(2,1)S(1)}, bf16[16,16,128]{2,1,0:T(8,128)(2,1)S(1)}, u32[]{:S(2)}, u32[]{:S(2)}) collective-permute-start(bf16[16,16,128]{2,1,0:T(8,128)(2,1)S(1)} %add_convert_fusion.6.old_ref), channel_id=1, source_target_pairs={{0,1},{1,0},{2,3},{3,2},{4,5},{5,4},{6,7},{7,6},{8,9},{9,8},{10,11... | collective-permute-start | bytes 196616 | tf_op jit(solution)/shard_map/ppermute | solution.py:392
  37.3 28.0 %collective-permute-start.17 = (bf16[4,256,256]{2,1,0:T(8,128)(2,1)S(1)}, bf16[4,256,256]{2,1,0:T(8,128)(2,1)S(1)}, u32[]{:S(2)}, u32[]{:S(2)}) collective-permute-start(bf16[4,256,256]{2,1,0:T(8,128)(2,1)S(1)} %get-tuple-element.41), channel_id=1, source_target_pairs={{0,4},{1,5},{2,6},{3,7},{4,0},{5,1},{6,2},{7,3},{8,12},{9,13},{10,... | collective-permute-start | bytes 1572872 | tf_op jit(solution)/shard_map/ppermute | solution.py:392
  39.2 26.1 %collective-permute-start.15 = (bf16[4,256,256]{2,1,0:T(8,128)(2,1)S(1)}, bf16[4,256,256]{2,1,0:T(8,128)(2,1)S(1)}, u32[]{:S(2)}, u32[]{:S(2)}) collective-permute-start(bf16[4,256,256]{2,1,0:T(8,128)(2,1)S(1)} %get-tuple-element.42), channel_id=1, source_target_pairs={{0,2},{1,3},{2,0},{3,1},{4,6},{5,7},{6,4},{7,5},{8,10},{9,11},{10,... | collective-permute-start | bytes 1572872 | tf_op jit(solution)/shard_map/ppermute | solution.py:392
  45.7 3.7 %collective-permute-start.9 = (bf16[16,16,128]{2,1,0:T(8,128)(2,1)S(1)}, bf16[16,16,128]{2,1,0:T(8,128)(2,1)S(1)}, u32[]{:S(2)}, u32[]{:S(2)}) collective-permute-start(bf16[16,16,128]{2,1,0:T(8,128)(2,1)S(1)} %get-tuple-element.30), channel_id=1, source_target_pairs={{0,1},{1,0},{2,3},{3,2},{4,5},{5,4},{6,7},{7,6},{8,9},{9,8},{10,11... | collective-permute-start | bytes 196616 | tf_op jit(solution)/shard_map/ppermute | solution.py:392
  49.4 4.1 %collective-permute-start.12 = (bf16[16,16,128]{2,1,0:T(8,128)(2,1)S(1)}, bf16[16,16,128]{2,1,0:T(8,128)(2,1)S(1)}, u32[]{:S(2)}, u32[]{:S(2)}) collective-permute-start(bf16[16,16,128]{2,1,0:T(8,128)(2,1)S(1)} %add_convert_fusion.5), channel_id=1, source_target_pairs={{0,24},{8,16},{16,8},{24,0},{1,25},{9,17},{17,9},{25,1},{2,26},{10... | collective-permute-start | bytes 196616 | tf_op jit(solution)/shard_map/ppermute | solution.py:392
  51.6 3.4 %collective-permute-start.11 = (bf16[16,16,128]{2,1,0:T(8,128)(2,1)S(1)}, bf16[16,16,128]{2,1,0:T(8,128)(2,1)S(1)}, u32[]{:S(2)}, u32[]{:S(2)}) collective-permute-start(bf16[16,16,128]{2,1,0:T(8,128)(2,1)S(1)} %add_convert_fusion.5), channel_id=1, source_target_pairs={{0,16},{8,24},{16,0},{24,8},{1,17},{9,25},{17,1},{25,9},{2,18},{10... | collective-permute-start | bytes 196616 | tf_op jit(solution)/shard_map/ppermute | solution.py:392
  53.5 3.1 %collective-permute-start.10 = (bf16[16,16,128]{2,1,0:T(8,128)(2,1)S(1)}, bf16[16,16,128]{2,1,0:T(8,128)(2,1)S(1)}, u32[]{:S(2)}, u32[]{:S(2)}) collective-permute-start(bf16[16,16,128]{2,1,0:T(8,128)(2,1)S(1)} %add_convert_fusion.5), channel_id=1, source_target_pairs={{0,8},{8,0},{16,24},{24,16},{1,9},{9,1},{17,25},{25,17},{2,10},{10... | collective-permute-start | bytes 196616 | tf_op jit(solution)/shard_map/ppermute | solution.py:392
  65.4 5.1 %collective-permute-start.20 = (bf16[16,16,128]{2,1,0:T(8,128)(2,1)S(1)}, bf16[16,16,128]{2,1,0:T(8,128)(2,1)S(1)}, u32[]{:S(2)}, u32[]{:S(2)}) collective-permute-start(bf16[16,16,128]{2,1,0:T(8,128)(2,1)S(1)} %add_convert_fusion.4), channel_id=1, source_target_pairs={{0,6},{1,7},{2,4},{3,5},{4,2},{5,3},{6,0},{7,1},{8,14},{9,15},{10,... | collective-permute-start | bytes 196616 | tf_op jit(solution)/shard_map/ppermute | solution.py:392
  65.8 5.5 %collective-permute-start.19 = (bf16[16,16,128]{2,1,0:T(8,128)(2,1)S(1)}, bf16[16,16,128]{2,1,0:T(8,128)(2,1)S(1)}, u32[]{:S(2)}, u32[]{:S(2)}) collective-permute-start(bf16[16,16,128]{2,1,0:T(8,128)(2,1)S(1)} %add_convert_fusion.4), channel_id=1, source_target_pairs={{0,4},{1,5},{2,6},{3,7},{4,0},{5,1},{6,2},{7,3},{8,12},{9,13},{10,... | collective-permute-start | bytes 196616 | tf_op jit(solution)/shard_map/ppermute | solution.py:392
  65.8 5.5 %collective-permute-start.18 = (bf16[16,16,128]{2,1,0:T(8,128)(2,1)S(1)}, bf16[16,16,128]{2,1,0:T(8,128)(2,1)S(1)}, u32[]{:S(2)}, u32[]{:S(2)}) collective-permute-start(bf16[16,16,128]{2,1,0:T(8,128)(2,1)S(1)} %add_convert_fusion.4), channel_id=1, source_target_pairs={{0,2},{1,3},{2,0},{3,1},{4,6},{5,7},{6,4},{7,5},{8,10},{9,11},{10,... | collective-permute-start | bytes 196616 | tf_op jit(solution)/shard_map/ppermute | solution.py:392
  71.4 8.0 %collective-permute-start.21 = (bf16[16,16,128]{2,1,0:T(8,128)(2,1)S(1)}, bf16[16,16,128]{2,1,0:T(8,128)(2,1)S(1)}, u32[]{:S(2)}, u32[]{:S(2)}) collective-permute-start(bf16[16,16,128]{2,1,0:T(8,128)(2,1)S(1)} %add_convert_fusion.3.old_ref), channel_id=1, source_target_pairs={{0,1},{1,0},{2,3},{3,2},{4,5},{5,4},{6,7},{7,6},{8,9},{9,8},{10,11... | collective-permute-start | bytes 196616 | tf_op jit(solution)/shard_map/ppermute | solution.py:392

commit v5 on v4

--- a/solution.py
+++ b/solution.py
@@ -182,7 +182,7 @@
     total_re, total_im = total_ref[:ROWS, :], total_ref[ROWS:, :]
     lane = iota((8, K), 1)
     for number in range(size):
-        shift_y, shift_x = scalars_ref[2 * (first + number)], scalars_ref[2 * (first + number) + 1]
+        shift_y, shift_x = scalars_ref[first + number], scalars_ref[COUNT + first + number]
         weight = weight_ref[pl.ds(first + number, 1), :]
         weight = jnp.concatenate([weight, weight], axis=1)
         turns = column_order(lane) * shift_x
@@ -386,7 +386,7 @@
     owner = bin_owner.reshape(-1)
     chips = columns // 2
     targets = ((owner ^ me) % 2) * (chips * BINS) + ((owner // 2) ^ (me // 2)) * BINS + bin_index
-    scalars = jnp.concatenate([shifts.reshape(-1), targets, (me % 2).reshape(1).astype(jnp.int32)])
+    scalars = jnp.concatenate([shifts[:, 0], shifts[:, 1], targets, (me % 2).reshape(1).astype(jnp.int32)])
 
     def send(array, far, axis="col"):
         return lax.ppermute(array, axis, [(i, i ^ far) for i in range(lax.axis_size(axis))])
@@ -401,7 +401,7 @@
     mine, other, other_far = jnp.split(bins, (chips * BINS, (2 * chips - 1) * BINS))
     half = add_halves(keep, send(away, 1))
     half, other, other_far = lax.optimization_barrier((half, other, other_far))
-    half = add_halves(*over_chips(half))
+    halves = over_chips(half)
     other, other_far = send(other, 1), send(other_far, 1)
     mine = mine.reshape(chips, BINS, K, K)
     other = other.reshape(chips - 1, BINS, K, K)
@@ -414,20 +414,24 @@
     binned = chip_bins(0)
     if chips == 4:
         block = chip_bins(3).astype(BF16)
-        half, block = lax.optimization_barrier((half, block))
+        second, first = chip_bins(2).astype(BF16), chip_bins(1).astype(BF16)
+        halves[3], block, second, first = lax.optimization_barrier((halves[3], block, second, first))
+        half = add_halves(*halves)
         pairs = lambda hops: [(2 * a + core, 2 * b + core) for a, b in hops for core in range(2)]
         passing = lax.ppermute(block, "col", pairs([(0, 1), (3, 2)]))
         middle = lax.ppermute(block, "col", pairs([(1, 2), (2, 1)]))
+        ends = lax.ppermute(second, "col", pairs([(0, 2), (3, 1)]))
         half = add_halves(*over_lines(half))
-        other_half = send(half, 1)
-        arrived = [middle, send(chip_bins(1).astype(BF16), 2), send(chip_bins(2, passing).astype(BF16), 4)]
+        near = send(first, 2)
+        inner = lax.ppermute(chip_bins(2, passing).astype(BF16), "col", pairs([(1, 3), (2, 0)]))
         keep, away, weight = run_second(spectra, half, send(half, 1), scalars)
+        away, middle, ends = lax.optimization_barrier((away, middle, ends))
         halves = over_lines(add_halves(keep, send(away, 1)))
-        halves, arrived = lax.optimization_barrier((halves, arrived))
+        halves, near, inner = lax.optimization_barrier((halves, near, inner))
         half = add_halves(*halves)
-        binned = sum([array.astype(F32) for array in arrived], binned)
+        binned = sum([array.astype(F32) for array in (middle, ends, near, inner)], binned)
     else:
-        half = add_halves(*over_lines(half))
+        half = add_halves(*over_lines(add_halves(*halves)))
         for far in range(1, chips):
             binned = binned + send(chip_bins(far).astype(BF16), 2 * far).astype(F32)
         keep, away, weight = run_second(spectra, half, send(half, 1), scalars)

time: 81.4 us -> 78.1 us (0.959)
  waiting for transfers between devices: 24 us -> 19.7 us
    ppermute x20 -> x19, waiting for transfers between devices: 23.5 us -> 12.1 us  [send(): lax.ppermute(array, axis, [(i, i ^ far) for i in range(lax.axis_size(axis...]
    ppermute x0 -> x2, waiting for transfers between devices: none -> 7.61 us  [the longest x1 6.69 us: on_device(): lax.ppermute(chip_bins(2, passing).astype(BF16), 'col', pairs([(1, 3), (2...]
    ppermute x0 -> x2, starting transfers between devices: none -> 5.12 us  [the longest x1 3.83 us: on_device(): ends = lax.ppermute(second, 'col', pairs([(0, 2), (3, 1)]))]
    ppermute x20 -> x19, starting transfers between devices: 30.9 us -> 26.7 us  [send(): lax.ppermute(array, axis, [(i, i ^ far) for i in range(lax.axis_size(axis...]
  transfers between devices with their start and end apart: 22 -> 23, of which waited for: 14 -> 12; matrix products, arithmetic and copies ran while one was open for 3% -> 4% of each run, Pallas kernels for 7% -> 8%
where the time goes in v5:
time: 78.1 us; the launch traced here: 77.8 us
  starting transfers between devices  34.3 us (44%)
  waiting for transfers between devices  19.7 us (25%)
  Pallas kernels  17.7 us (23%)
  other arithmetic  3.01 us (4%)
  local copies, waits for them, and re-layouts  2.18 us (3%)
  between operations  0.8 us (1%)
    ppermute x19, starting transfers between devices, send(): lax.ppermute(array, axis, [(i, i ^ far) for i in range(lax.axis_size(axis...  26.7 us
    ppermute x19, waiting for transfers between devices, send(): lax.ppermute(array, axis, [(i, i ^ far) for i in range(lax.axis_size(axis...  12.1 us
    pallas_call x1, Pallas kernels, run_first(): pl.pallas_call(first_kernel, out_shape=(pltpu.VMEM((count, 2 * ROWS, K),...  9.94 us
    ppermute x1, waiting for transfers between devices, on_device(): lax.ppermute(chip_bins(2, passing).astype(BF16), 'col', pairs([(1, 3), (2...  6.69 us
    pallas_call x1, Pallas kernels, run_second(): pl.pallas_call(second_kernel, out_shape=(pltpu.VMEM(HALF_SHAPE, F32), plt...  6.06 us
    ppermute x1, starting transfers between devices, on_device(): ends = lax.ppermute(second, 'col', pairs([(0, 2), (3, 1)]))  3.83 us
    ppermute x1, starting transfers between devices, on_device(): passing = lax.ppermute(block, 'col', pairs([(0, 1), (3, 2)]))  1.87 us
    pallas_call x1, Pallas kernels, run_last(): pl.pallas_call(last_kernel, out_shape=jax.ShapeDtypeStruct((2, K, K), F32...  1.74 us
  transfers between devices with their start and end apart: 23, of which 12 were waited for; matrix products, arithmetic and copies ran while one was open for 4% of the time, Pallas kernels for 8%

profile of v5, /device:TPU:1, one launch (start us, length us, event | category | flops | bytes accessed | tf_op | source)
XLA Modules:
  0.0 77.8 jit_solution(7276839143480667674)
XLA Ops:
  0.6 0.8 slice_bitcast_fusion.1
  2.8 9.9 %forward_and_correlate.1 = (bf16[16,288,256]{2,1,0:T(8,128)(2,1)S(1)}, f32[16,16,128]{2,1,0:T(8,128)S(1)}, bf16[16,16,128]{2,1,0:T(8,128)(2,1)S(1)}, bf16[32,256,256]{2,1,0:T(8,128)(2,1)S(1)}) custom-call(s32[49]{0:T(128)S(1)} %pad_add_fusion.scalars_ref, f32[8,128]{1,0:T(8,128)S(1)} %jit_solution_.3.row_ref, bf16[16,256,256]{2,1,0:T(8,128)(2,1)} %pattern_hbm.1, ...), custom_call_target="tpu_custom_call" | custom-call | flops 4000000000 | bytes 12000000 | tf_op jit(solution)/shard_map/forward_and_correlate/pallas_call | solution.py:326
  13.1 1.0 %collective-permute-done = bf16[16,16,128]{2,1,0:T(8,128)(2,1)S(1)} collective-permute-done((bf16[16,16,128]{2,1,0:T(8,128)(2,1)S(1)}, bf16[16,16,128]{2,1,0:T(8,128)(2,1)S(1)}, u32[]{:S(2)}, u32[]{:S(2)}) %collective-permute-start) | collective-permute-done | bytes 65568 | tf_op jit(solution)/shard_map/ppermute | solution.py:392
  14.7 4.5 %collective-permute-start.3 = (bf16[16,16,128]{2,1,0:T(8,128)(2,1)S(1)}, bf16[16,16,128]{2,1,0:T(8,128)(2,1)S(1)}, u32[]{:S(2)}, u32[]{:S(2)}) collective-permute-start(bf16[16,16,128]{2,1,0:T(8,128)(2,1)S(1)} %add_convert_fusion.8), channel_id=1, source_target_pairs={{0,6},{1,7},{2,4},{3,5},{4,2},{5,3},{6,0},{7,1},{8,14},{9,15},{10,... | collective-permute-start | bytes 196616 | tf_op jit(solution)/shard_map/ppermute | solution.py:392
  19.9 1.4 %collective-permute-done.3 = bf16[16,16,128]{2,1,0:T(8,128)(2,1)S(1)} collective-permute-done((bf16[16,16,128]{2,1,0:T(8,128)(2,1)S(1)}, bf16[16,16,128]{2,1,0:T(8,128)(2,1)S(1)}, u32[]{:S(2)}, u32[]{:S(2)}) %collective-permute-start.3) | collective-permute-done | bytes 65568 | tf_op jit(solution)/shard_map/ppermute | solution.py:392
  21.3 1.9 %collective-permute-start.17 = (bf16[4,256,256]{2,1,0:T(8,128)(2,1)S(1)}, bf16[4,256,256]{2,1,0:T(8,128)(2,1)S(1)}, u32[]{:S(2)}, u32[]{:S(2)}) collective-permute-start(bf16[4,256,256]{2,1,0:T(8,128)(2,1)S(1)} %get-tuple-element.36), channel_id=1, source_target_pairs={{0,2},{1,3},{6,4},{7,5},{8,10},{9,11},{14,12},{15,13},{16,18},{17,... | collective-permute-start | bytes 1572872 | tf_op jit(solution)/shard_map/ppermute | solution.py:421
  23.2 1.7 %collective-permute-done.2 = bf16[16,16,128]{2,1,0:T(8,128)(2,1)S(1)} collective-permute-done((bf16[16,16,128]{2,1,0:T(8,128)(2,1)S(1)}, bf16[16,16,128]{2,1,0:T(8,128)(2,1)S(1)}, u32[]{:S(2)}, u32[]{:S(2)}) %collective-permute-start.2) | collective-permute-done | bytes 65568 | tf_op jit(solution)/shard_map/ppermute | solution.py:392
  24.9 2.2 %collective-permute-start.8 = (bf16[16,16,128]{2,1,0:T(8,128)(2,1)S(1)}, bf16[16,16,128]{2,1,0:T(8,128)(2,1)S(1)}, u32[]{:S(2)}, u32[]{:S(2)}) collective-permute-start(bf16[16,16,128]{2,1,0:T(8,128)(2,1)S(1)} %add_convert_fusion.7), channel_id=1, source_target_pairs={{0,24},{8,16},{16,8},{24,0},{1,25},{9,17},{17,9},{25,1},{2,26},{10... | collective-permute-start | bytes 196616 | tf_op jit(solution)/shard_map/ppermute | solution.py:392
  29.0 3.8 %collective-permute-start.11 = (bf16[4,256,256]{2,1,0:T(8,128)(2,1)S(1)}, bf16[4,256,256]{2,1,0:T(8,128)(2,1)S(1)}, u32[]{:S(2)}, u32[]{:S(2)}) collective-permute-start(bf16[4,256,256]{2,1,0:T(8,128)(2,1)S(1)} %get-tuple-element.37), channel_id=1, source_target_pairs={{0,4},{1,5},{6,2},{7,3},{8,12},{9,13},{14,10},{15,11},{16,20},{17,... | collective-permute-start | bytes 1572872 | tf_op jit(solution)/shard_map/ppermute | solution.py:423
  33.0 3.1 %collective-permute-start.9 = (bf16[16,16,128]{2,1,0:T(8,128)(2,1)S(1)}, bf16[16,16,128]{2,1,0:T(8,128)(2,1)S(1)}, u32[]{:S(2)}, u32[]{:S(2)}) collective-permute-start(bf16[16,16,128]{2,1,0:T(8,128)(2,1)S(1)} %add_convert_fusion.6.old_ref), channel_id=1, source_target_pairs={{0,1},{1,0},{2,3},{3,2},{4,5},{5,4},{6,7},{7,6},{8,9},{9,8},{10,11... | collective-permute-start | bytes 196616 | tf_op jit(solution)/shard_map/ppermute | solution.py:392
  36.3 1.3 %collective-permute-start.18 = (bf16[4,256,256]{2,1,0:T(8,128)(2,1)S(1)}, bf16[4,256,256]{2,1,0:T(8,128)(2,1)S(1)}, u32[]{:S(2)}, u32[]{:S(2)}) collective-permute-start(bf16[4,256,256]{2,1,0:T(8,128)(2,1)S(1)} %add_convert_fusion), channel_id=1, source_target_pairs={{2,6},{3,7},{4,0},{5,1},{10,14},{11,15},{12,8},{13,9},{18,22},{19,... | collective-permute-start | bytes 1572872 | tf_op jit(solution)/shard_map/ppermute | solution.py:426
  37.7 6.1 %correlate_again.1 = (f32[16,16,128]{2,1,0:T(8,128)S(1)}, bf16[16,16,128]{2,1,0:T(8,128)(2,1)S(1)}, f32[16,128]{1,0:T(8,128)S(1)}) custom-call(s32[49]{0:T(128)S(1)} %pad_add_fusion.scalars_ref, f32[8,128]{1,0:T(8,128)S(1)} %jit_solution_.3.row_ref, bf16[16,288,256]{2,1,0:T(8,128)(2,1)S(1)} %get-tuple-element.26.spec_ref, ...), custom_call_target="tpu_custom_call" | custom-call | flops 3000000000 | bytes 4000000 | tf_op jit(solution)/shard_map/correlate_again/pallas_call | solution.py:348
  43.7 0.9 %collective-permute-done.11 = bf16[4,256,256]{2,1,0:T(8,128)(2,1)S(1)} collective-permute-done((bf16[4,256,256]{2,1,0:T(8,128)(2,1)S(1)}, bf16[4,256,256]{2,1,0:T(8,128)(2,1)S(1)}, u32[]{:S(2)}, u32[]{:S(2)}) %collective-permute-start.11) | collective-permute-done | bytes 524320 | tf_op jit(solution)/shard_map/ppermute | solution.py:423
  44.7 4.0 %collective-permute-start.12 = (bf16[16,16,128]{2,1,0:T(8,128)(2,1)S(1)}, bf16[16,16,128]{2,1,0:T(8,128)(2,1)S(1)}, u32[]{:S(2)}, u32[]{:S(2)}) collective-permute-start(bf16[16,16,128]{2,1,0:T(8,128)(2,1)S(1)} %get-tuple-element.38), channel_id=1, source_target_pairs={{0,1},{1,0},{2,3},{3,2},{4,5},{5,4},{6,7},{7,6},{8,9},{9,8},{10,11... | collective-permute-start | bytes 196616 | tf_op jit(solution)/shard_map/ppermute | solution.py:392
  48.6 0.9 %collective-permute-done.12 = bf16[16,16,128]{2,1,0:T(8,128)(2,1)S(1)} collective-permute-done((bf16[16,16,128]{2,1,0:T(8,128)(2,1)S(1)}, bf16[16,16,128]{2,1,0:T(8,128)(2,1)S(1)}, u32[]{:S(2)}, u32[]{:S(2)}) %collective-permute-start.12) | collective-permute-done | bytes 65568 | tf_op jit(solution)/shard_map/ppermute | solution.py:392
  49.6 1.3 %collective-permute-start.13 = (bf16[16,16,128]{2,1,0:T(8,128)(2,1)S(1)}, bf16[16,16,128]{2,1,0:T(8,128)(2,1)S(1)}, u32[]{:S(2)}, u32[]{:S(2)}) collective-permute-start(bf16[16,16,128]{2,1,0:T(8,128)(2,1)S(1)} %add_convert_fusion.5), channel_id=1, source_target_pairs={{0,8},{8,0},{16,24},{24,16},{1,9},{9,1},{17,25},{25,17},{2,10},{10... | collective-permute-start | bytes 196616 | tf_op jit(solution)/shard_map/ppermute | solution.py:392
  50.8 1.2 %collective-permute-start.14 = (bf16[16,16,128]{2,1,0:T(8,128)(2,1)S(1)}, bf16[16,16,128]{2,1,0:T(8,128)(2,1)S(1)}, u32[]{:S(2)}, u32[]{:S(2)}) collective-permute-start(bf16[16,16,128]{2,1,0:T(8,128)(2,1)S(1)} %add_convert_fusion.5), channel_id=1, source_target_pairs={{0,16},{8,24},{16,0},{24,8},{1,17},{9,25},{17,1},{25,9},{2,18},{10... | collective-permute-start | bytes 196616 | tf_op jit(solution)/shard_map/ppermute | solution.py:392
  52.3 3.6 %collective-permute-done.16 = bf16[4,256,256]{2,1,0:T(8,128)(2,1)S(1)} collective-permute-done((bf16[4,256,256]{2,1,0:T(8,128)(2,1)S(1)}, bf16[4,256,256]{2,1,0:T(8,128)(2,1)S(1)}, u32[]{:S(2)}, u32[]{:S(2)}) %collective-permute-start.16) | collective-permute-done | bytes 524320 | tf_op jit(solution)/shard_map/ppermute | solution.py:392
  56.1 6.7 %collective-permute-done.18 = bf16[4,256,256]{2,1,0:T(8,128)(2,1)S(1)} collective-permute-done((bf16[4,256,256]{2,1,0:T(8,128)(2,1)S(1)}, bf16[4,256,256]{2,1,0:T(8,128)(2,1)S(1)}, u32[]{:S(2)}, u32[]{:S(2)}) %collective-permute-start.18) | collective-permute-done | bytes 524320 | tf_op jit(solution)/shard_map/ppermute | solution.py:426
  63.5 3.5 %collective-permute-start.20 = (bf16[16,16,128]{2,1,0:T(8,128)(2,1)S(1)}, bf16[16,16,128]{2,1,0:T(8,128)(2,1)S(1)}, u32[]{:S(2)}, u32[]{:S(2)}) collective-permute-start(bf16[16,16,128]{2,1,0:T(8,128)(2,1)S(1)} %add_convert_fusion.4), channel_id=1, source_target_pairs={{0,4},{1,5},{2,6},{3,7},{4,0},{5,1},{6,2},{7,3},{8,12},{9,13},{10,... | collective-permute-start | bytes 196616 | tf_op jit(solution)/shard_map/ppermute | solution.py:392
  67.8 2.4 %collective-permute-done.20 = bf16[16,16,128]{2,1,0:T(8,128)(2,1)S(1)} collective-permute-done((bf16[16,16,128]{2,1,0:T(8,128)(2,1)S(1)}, bf16[16,16,128]{2,1,0:T(8,128)(2,1)S(1)}, u32[]{:S(2)}, u32[]{:S(2)}) %collective-permute-start.20) | collective-permute-done | bytes 65568 | tf_op jit(solution)/shard_map/ppermute | solution.py:392
  70.3 4.4 %collective-permute-start.22 = (bf16[16,16,128]{2,1,0:T(8,128)(2,1)S(1)}, bf16[16,16,128]{2,1,0:T(8,128)(2,1)S(1)}, u32[]{:S(2)}, u32[]{:S(2)}) collective-permute-start(bf16[16,16,128]{2,1,0:T(8,128)(2,1)S(1)} %add_convert_fusion.3.old_ref), channel_id=1, source_target_pairs={{0,1},{1,0},{2,3},{3,2},{4,5},{5,4},{6,7},{7,6},{8,9},{9,8},{10,11... | collective-permute-start | bytes 196616 | tf_op jit(solution)/shard_map/ppermute | solution.py:392
  74.7 1.4 %convert_add_fusion = f32[4,256,256]{2,1,0:T(8,128)} fusion(bf16[4,256,256]{2,1,0:T(8,128)(2,1)S(1)} %collective-permute-done.18, bf16[4,256,256]{2,1,0:T(8,128)(2,1)S(1)} %collective-permute-done.16, bf16[4,256,256]{2,1,0:T(8,128)(2,1)S(1)} %collective-permute-done.11, bf16[4,256,256]{2,1,0:T(8,128)(2,1)S(1)} %collective-permute-done.10, ...), kind=kLoop, calls=%fused_computation | loop fusion | flops 2883584 | bytes 4194304 | tf_op jit(solution)/shard_map/add | solution.py:432
  76.1 1.7 %finish.1 = f32[2,256,256]{2,1,0:T(8,128)} custom-call(s32[49]{0:T(128)S(1)} %pad_add_fusion.scalars_ref, bf16[16,16,128]{2,1,0:T(8,128)(2,1)S(1)} %add_convert_fusion.3.old_ref, bf16[16,16,128]{2,1,0:T(8,128)(2,1)S(1)} %collective-permute-done.22.old_other_ref), custom_call_target="tpu_custom_call" | custom-call | flops 100000000 | bytes 1000000 | tf_op jit(solution)/shard_map/finish/pallas_call | solution.py:365
  (41 shorter events, 7.3 us)
Async XLA Ops:
  12.8 1.3 %collective-permute-start = (bf16[16,16,128]{2,1,0:T(8,128)(2,1)S(1)}, bf16[16,16,128]{2,1,0:T(8,128)(2,1)S(1)}, u32[]{:S(2)}, u32[]{:S(2)}) collective-permute-start(bf16[16,16,128]{2,1,0:T(8,128)(2,1)S(1)} %get-tuple-element.28), channel_id=1, source_target_pairs={{0,1},{1,0},{2,3},{3,2},{4,5},{5,4},{6,7},{7,6},{8,9},{9,8},{10,11... | collective-permute-start | bytes 196616 | tf_op jit(solution)/shard_map/ppermute | solution.py:392
  14.1 5.3 %collective-permute-start.5 = (bf16[12,256,256]{2,1,0:T(8,128)(2,1)S(1)}, bf16[12,256,256]{2,1,0:T(8,128)(2,1)S(1)}, u32[]{:S(2)}, u32[]{:S(2)}) collective-permute-start(bf16[12,256,256]{2,1,0:T(8,128)(2,1)S(1)} %split.7), channel_id=1, source_target_pairs={{0,1},{1,0},{2,3},{3,2},{4,5},{5,4},{6,7},{7,6},{8,9},{9,8},{10,11... | collective-permute-start | bytes 4718600 | tf_op jit(solution)/shard_map/ppermute | solution.py:392
  14.3 5.1 %collective-permute-start.4 = (bf16[4,256,256]{2,1,0:T(8,128)(2,1)S(1)}, bf16[4,256,256]{2,1,0:T(8,128)(2,1)S(1)}, u32[]{:S(2)}, u32[]{:S(2)}) collective-permute-start(bf16[4,256,256]{2,1,0:T(8,128)(2,1)S(1)} %split.8), channel_id=1, source_target_pairs={{0,1},{1,0},{2,3},{3,2},{4,5},{5,4},{6,7},{7,6},{8,9},{9,8},{10,11... | collective-permute-start | bytes 1572872 | tf_op jit(solution)/shard_map/ppermute | solution.py:392
  14.7 6.7 %collective-permute-start.3 = (bf16[16,16,128]{2,1,0:T(8,128)(2,1)S(1)}, bf16[16,16,128]{2,1,0:T(8,128)(2,1)S(1)}, u32[]{:S(2)}, u32[]{:S(2)}) collective-permute-start(bf16[16,16,128]{2,1,0:T(8,128)(2,1)S(1)} %add_convert_fusion.8), channel_id=1, source_target_pairs={{0,6},{1,7},{2,4},{3,5},{4,2},{5,3},{6,0},{7,1},{8,14},{9,15},{10,... | collective-permute-start | bytes 196616 | tf_op jit(solution)/shard_map/ppermute | solution.py:392
  19.2 5.7 %collective-permute-start.2 = (bf16[16,16,128]{2,1,0:T(8,128)(2,1)S(1)}, bf16[16,16,128]{2,1,0:T(8,128)(2,1)S(1)}, u32[]{:S(2)}, u32[]{:S(2)}) collective-permute-start(bf16[16,16,128]{2,1,0:T(8,128)(2,1)S(1)} %add_convert_fusion.8), channel_id=1, source_target_pairs={{0,4},{1,5},{2,6},{3,7},{4,0},{5,1},{6,2},{7,3},{8,12},{9,13},{10,... | collective-permute-start | bytes 196616 | tf_op jit(solution)/shard_map/ppermute | solution.py:392
  19.2 5.7 %collective-permute-start.1 = (bf16[16,16,128]{2,1,0:T(8,128)(2,1)S(1)}, bf16[16,16,128]{2,1,0:T(8,128)(2,1)S(1)}, u32[]{:S(2)}, u32[]{:S(2)}) collective-permute-start(bf16[16,16,128]{2,1,0:T(8,128)(2,1)S(1)} %add_convert_fusion.8), channel_id=1, source_target_pairs={{0,2},{1,3},{2,0},{3,1},{4,6},{5,7},{6,4},{7,5},{8,10},{9,11},{10,... | collective-permute-start | bytes 196616 | tf_op jit(solution)/shard_map/ppermute | solution.py:392
  21.3 14.8 %collective-permute-start.17 = (bf16[4,256,256]{2,1,0:T(8,128)(2,1)S(1)}, bf16[4,256,256]{2,1,0:T(8,128)(2,1)S(1)}, u32[]{:S(2)}, u32[]{:S(2)}) collective-permute-start(bf16[4,256,256]{2,1,0:T(8,128)(2,1)S(1)} %get-tuple-element.36), channel_id=1, source_target_pairs={{0,2},{1,3},{6,4},{7,5},{8,10},{9,11},{14,12},{15,13},{16,18},{17,... | collective-permute-start | bytes 1572872 | tf_op jit(solution)/shard_map/ppermute | solution.py:421
  24.9 4.1 %collective-permute-start.8 = (bf16[16,16,128]{2,1,0:T(8,128)(2,1)S(1)}, bf16[16,16,128]{2,1,0:T(8,128)(2,1)S(1)}, u32[]{:S(2)}, u32[]{:S(2)}) collective-permute-start(bf16[16,16,128]{2,1,0:T(8,128)(2,1)S(1)} %add_convert_fusion.7), channel_id=1, source_target_pairs={{0,24},{8,16},{16,8},{24,0},{1,25},{9,17},{17,9},{25,1},{2,26},{10... | collective-permute-start | bytes 196616 | tf_op jit(solution)/shard_map/ppermute | solution.py:392
  27.2 5.7 %collective-permute-start.7 = (bf16[16,16,128]{2,1,0:T(8,128)(2,1)S(1)}, bf16[16,16,128]{2,1,0:T(8,128)(2,1)S(1)}, u32[]{:S(2)}, u32[]{:S(2)}) collective-permute-start(bf16[16,16,128]{2,1,0:T(8,128)(2,1)S(1)} %add_convert_fusion.7), channel_id=1, source_target_pairs={{0,16},{8,24},{16,0},{24,8},{1,17},{9,25},{17,1},{25,9},{2,18},{10... | collective-permute-start | bytes 196616 | tf_op jit(solution)/shard_map/ppermute | solution.py:392
  27.4 5.6 %collective-permute-start.6 = (bf16[16,16,128]{2,1,0:T(8,128)(2,1)S(1)}, bf16[16,16,128]{2,1,0:T(8,128)(2,1)S(1)}, u32[]{:S(2)}, u32[]{:S(2)}) collective-permute-start(bf16[16,16,128]{2,1,0:T(8,128)(2,1)S(1)} %add_convert_fusion.7), channel_id=1, source_target_pairs={{0,8},{8,0},{16,24},{24,16},{1,9},{9,1},{17,25},{25,17},{2,10},{10... | collective-permute-start | bytes 196616 | tf_op jit(solution)/shard_map/ppermute | solution.py:392
  27.6 16.1 %collective-permute-start.10 = (bf16[4,256,256]{2,1,0:T(8,128)(2,1)S(1)}, bf16[4,256,256]{2,1,0:T(8,128)(2,1)S(1)}, u32[]{:S(2)}, u32[]{:S(2)}) collective-permute-start(bf16[4,256,256]{2,1,0:T(8,128)(2,1)S(1)} %get-tuple-element.36), channel_id=1, source_target_pairs={{2,4},{3,5},{4,2},{5,3},{10,12},{11,13},{12,10},{13,11},{18,20},{1... | collective-permute-start | bytes 1572872 | tf_op jit(solution)/shard_map/ppermute | solution.py:422
  29.0 15.6 %collective-permute-start.11 = (bf16[4,256,256]{2,1,0:T(8,128)(2,1)S(1)}, bf16[4,256,256]{2,1,0:T(8,128)(2,1)S(1)}, u32[]{:S(2)}, u32[]{:S(2)}) collective-permute-start(bf16[4,256,256]{2,1,0:T(8,128)(2,1)S(1)} %get-tuple-element.37), channel_id=1, source_target_pairs={{0,4},{1,5},{6,2},{7,3},{8,12},{9,13},{14,10},{15,11},{16,20},{17,... | collective-permute-start | bytes 1572872 | tf_op jit(solution)/shard_map/ppermute | solution.py:423
  32.9 23.0 %collective-permute-start.16 = (bf16[4,256,256]{2,1,0:T(8,128)(2,1)S(1)}, bf16[4,256,256]{2,1,0:T(8,128)(2,1)S(1)}, u32[]{:S(2)}, u32[]{:S(2)}) collective-permute-start(bf16[4,256,256]{2,1,0:T(8,128)(2,1)S(1)} %get-tuple-element.39), channel_id=1, source_target_pairs={{0,2},{1,3},{2,0},{3,1},{4,6},{5,7},{6,4},{7,5},{8,10},{9,11},{10,... | collective-permute-start | bytes 1572872 | tf_op jit(solution)/shard_map/ppermute | solution.py:392
  33.0 4.6 %collective-permute-start.9 = (bf16[16,16,128]{2,1,0:T(8,128)(2,1)S(1)}, bf16[16,16,128]{2,1,0:T(8,128)(2,1)S(1)}, u32[]{:S(2)}, u32[]{:S(2)}) collective-permute-start(bf16[16,16,128]{2,1,0:T(8,128)(2,1)S(1)} %add_convert_fusion.6.old_ref), channel_id=1, source_target_pairs={{0,1},{1,0},{2,3},{3,2},{4,5},{5,4},{6,7},{7,6},{8,9},{9,8},{10,11... | collective-permute-start | bytes 196616 | tf_op jit(solution)/shard_map/ppermute | solution.py:392
  36.3 26.4 %collective-permute-start.18 = (bf16[4,256,256]{2,1,0:T(8,128)(2,1)S(1)}, bf16[4,256,256]{2,1,0:T(8,128)(2,1)S(1)}, u32[]{:S(2)}, u32[]{:S(2)}) collective-permute-start(bf16[4,256,256]{2,1,0:T(8,128)(2,1)S(1)} %add_convert_fusion), channel_id=1, source_target_pairs={{2,6},{3,7},{4,0},{5,1},{10,14},{11,15},{12,8},{13,9},{18,22},{19,... | collective-permute-start | bytes 1572872 | tf_op jit(solution)/shard_map/ppermute | solution.py:426
  44.7 4.9 %collective-permute-start.12 = (bf16[16,16,128]{2,1,0:T(8,128)(2,1)S(1)}, bf16[16,16,128]{2,1,0:T(8,128)(2,1)S(1)}, u32[]{:S(2)}, u32[]{:S(2)}) collective-permute-start(bf16[16,16,128]{2,1,0:T(8,128)(2,1)S(1)} %get-tuple-element.38), channel_id=1, source_target_pairs={{0,1},{1,0},{2,3},{3,2},{4,5},{5,4},{6,7},{7,6},{8,9},{9,8},{10,11... | collective-permute-start | bytes 196616 | tf_op jit(solution)/shard_map/ppermute | solution.py:392
  49.6 6.3 %collective-permute-start.13 = (bf16[16,16,128]{2,1,0:T(8,128)(2,1)S(1)}, bf16[16,16,128]{2,1,0:T(8,128)(2,1)S(1)}, u32[]{:S(2)}, u32[]{:S(2)}) collective-permute-start(bf16[16,16,128]{2,1,0:T(8,128)(2,1)S(1)} %add_convert_fusion.5), channel_id=1, source_target_pairs={{0,8},{8,0},{16,24},{24,16},{1,9},{9,1},{17,25},{25,17},{2,10},{10... | collective-permute-start | bytes 196616 | tf_op jit(solution)/shard_map/ppermute | solution.py:392
  50.8 5.1 %collective-permute-start.14 = (bf16[16,16,128]{2,1,0:T(8,128)(2,1)S(1)}, bf16[16,16,128]{2,1,0:T(8,128)(2,1)S(1)}, u32[]{:S(2)}, u32[]{:S(2)}) collective-permute-start(bf16[16,16,128]{2,1,0:T(8,128)(2,1)S(1)} %add_convert_fusion.5), channel_id=1, source_target_pairs={{0,16},{8,24},{16,0},{24,8},{1,17},{9,25},{17,1},{25,9},{2,18},{10... | collective-permute-start | bytes 196616 | tf_op jit(solution)/shard_map/ppermute | solution.py:392
  52.1 4.0 %collective-permute-start.15 = (bf16[16,16,128]{2,1,0:T(8,128)(2,1)S(1)}, bf16[16,16,128]{2,1,0:T(8,128)(2,1)S(1)}, u32[]{:S(2)}, u32[]{:S(2)}) collective-permute-start(bf16[16,16,128]{2,1,0:T(8,128)(2,1)S(1)} %add_convert_fusion.5), channel_id=1, source_target_pairs={{0,24},{8,16},{16,8},{24,0},{1,25},{9,17},{17,9},{25,1},{2,26},{10... | collective-permute-start | bytes 196616 | tf_op jit(solution)/shard_map/ppermute | solution.py:392
  62.8 5.0 %collective-permute-start.21 = (bf16[16,16,128]{2,1,0:T(8,128)(2,1)S(1)}, bf16[16,16,128]{2,1,0:T(8,128)(2,1)S(1)}, u32[]{:S(2)}, u32[]{:S(2)}) collective-permute-start(bf16[16,16,128]{2,1,0:T(8,128)(2,1)S(1)} %add_convert_fusion.4), channel_id=1, source_target_pairs={{0,6},{1,7},{2,4},{3,5},{4,2},{5,3},{6,0},{7,1},{8,14},{9,15},{10,... | collective-permute-start | bytes 196616 | tf_op jit(solution)/shard_map/ppermute | solution.py:392
  63.5 6.7 %collective-permute-start.20 = (bf16[16,16,128]{2,1,0:T(8,128)(2,1)S(1)}, bf16[16,16,128]{2,1,0:T(8,128)(2,1)S(1)}, u32[]{:S(2)}, u32[]{:S(2)}) collective-permute-start(bf16[16,16,128]{2,1,0:T(8,128)(2,1)S(1)} %add_convert_fusion.4), channel_id=1, source_target_pairs={{0,4},{1,5},{2,6},{3,7},{4,0},{5,1},{6,2},{7,3},{8,12},{9,13},{10,... | collective-permute-start | bytes 196616 | tf_op jit(solution)/shard_map/ppermute | solution.py:392
  67.0 3.2 %collective-permute-start.19 = (bf16[16,16,128]{2,1,0:T(8,128)(2,1)S(1)}, bf16[16,16,128]{2,1,0:T(8,128)(2,1)S(1)}, u32[]{:S(2)}, u32[]{:S(2)}) collective-permute-start(bf16[16,16,128]{2,1,0:T(8,128)(2,1)S(1)} %add_convert_fusion.4), channel_id=1, source_target_pairs={{0,2},{1,3},{2,0},{3,1},{4,6},{5,7},{6,4},{7,5},{8,10},{9,11},{10,... | collective-permute-start | bytes 196616 | tf_op jit(solution)/shard_map/ppermute | solution.py:392
  70.3 5.7 %collective-permute-start.22 = (bf16[16,16,128]{2,1,0:T(8,128)(2,1)S(1)}, bf16[16,16,128]{2,1,0:T(8,128)(2,1)S(1)}, u32[]{:S(2)}, u32[]{:S(2)}) collective-permute-start(bf16[16,16,128]{2,1,0:T(8,128)(2,1)S(1)} %add_convert_fusion.3.old_ref), channel_id=1, source_target_pairs={{0,1},{1,0},{2,3},{3,2},{4,5},{5,4},{6,7},{7,6},{8,9},{9,8},{10,11... | collective-permute-start | bytes 196616 | tf_op jit(solution)/shard_map/ppermute | solution.py:392

commit v6 on v5

--- a/solution.py
+++ b/solution.py
@@ -1,10 +1,7 @@
-import functools
 import math
 
 import jax
 import jax.numpy as jnp
-import ml_dtypes
-import numpy as np
 from jax import lax
 from jax.experimental import pallas as pl
 from jax.experimental.pallas import tpu as pltpu
@@ -23,12 +20,6 @@
 BF16 = jnp.bfloat16
 
 
-@functools.cache
-def cosine_row():
-    angle = np.arange(HALF).astype(np.float32) * np.float32(2.0 * math.pi / K)
-    return np.broadcast_to(np.cos(angle).astype(np.float32), (8, HALF))
-
-
 def iota(shape, axis):
     return lax.broadcasted_iota(jnp.int32, shape, axis)
 
@@ -51,28 +42,44 @@
     return jnp.where(index <= HALF, index, HALF - index)
 
 
+def quarter_tables(row_ref):
+    row, lane = iota((HALF, HALF), 0), iota((HALF, HALF), 1)
+    turns = row * lane
+    by_row, by_lane = (jnp.where((index & 1) == 0, 1.0, -1.0) for index in (row, lane))
+    return cosine(row_ref, turns), cosine(row_ref, turns - QUARTER), by_row, by_lane, lane == 0
+
+
+def beside(a, b):
+    return jnp.concatenate([a, b], axis=1)
+
+
 def fill_forward(row_ref, fwd_one_ref, fwd_two_ref):
-    lane = iota((K, K), 1)
-    turns = iota((K, K), 0) * jnp.where(lane <= HALF, lane, lane - HALF)
-    fwd_one_ref[...] = cosine(row_ref, turns - jnp.where(lane <= HALF, 0, QUARTER)).astype(BF16)
-    row = iota((ROWS, K), 0)
-    turns = row * iota((ROWS, K), 1)
-    for part in range(2):
-        table = jnp.where(row <= HALF, cosine(row_ref, turns + part * QUARTER), 0.0)
-        fwd_two_ref[part * ROWS : (part + 1) * ROWS, :] = table.astype(BF16)
+    even, odd, by_row, by_lane, at_zero = quarter_tables(row_ref)
+    fwd_one_ref[:HALF, :] = beside(even, jnp.where(at_zero, by_row, odd)).astype(BF16)
+    fwd_one_ref[HALF:, :] = beside(even * by_lane, jnp.where(at_zero, by_row, odd * by_lane)).astype(BF16)
+    pad = iota((ROWS - HALF, K), 0)
+    last = jnp.where((iota((ROWS - HALF, K), 1) & 1) == 0, 1.0, -1.0)
+    fwd_two_ref[:HALF, :] = beside(even, even * by_row).astype(BF16)
+    fwd_two_ref[HALF:ROWS, :] = jnp.where(pad == 0, last, 0.0).astype(BF16)
+    fwd_two_ref[ROWS : ROWS + HALF, :] = beside(-odd, -odd * by_row).astype(BF16)
+    fwd_two_ref[ROWS + HALF :, :] = jnp.zeros((ROWS - HALF, K), BF16)
 
 
 def fill_inverse(row_ref, inv_one_ref, inv_two_ref):
-    row, lane = iota((K, K), 0), iota((K, K), 1)
-    turns = column_order(row) * lane
-    even, odd = cosine(row_ref, turns).astype(BF16), cosine(row_ref, turns - QUARTER).astype(BF16)
-    inv_one_ref[:K, :K] = even
-    inv_one_ref[:K, K:] = odd
-    inv_one_ref[K:, :K] = -odd
-    inv_one_ref[K:, K:] = even
-    turns = row * jnp.where(lane <= HALF, lane, lane - HALF) + jnp.where(lane <= HALF, 0, QUARTER)
-    scale = jnp.where((lane == 0) | (lane == HALF), 1.0, 2.0)
-    inv_two_ref[...] = (scale * cosine(row_ref, turns).astype(BF16).astype(F32)).astype(BF16)
+    even, odd, by_row, by_lane, at_zero = quarter_tables(row_ref)
+    real, imag = beside(even, even * by_row), beside(odd, odd * by_row)
+    is_first = iota((HALF, K), 0) == 0
+    parity = jnp.where((iota((HALF, K), 1) & 1) == 0, 1.0, -1.0)
+    real_back, imag_back = jnp.where(is_first, parity, real), jnp.where(is_first, 0.0, -imag)
+    for first, re, im in ((0, real, imag), (HALF, real_back, imag_back)):
+        inv_one_ref[first : first + HALF, :K] = re.astype(BF16)
+        inv_one_ref[first : first + HALF, K:] = im.astype(BF16)
+        inv_one_ref[K + first : K + first + HALF, :K] = (-im).astype(BF16)
+        inv_one_ref[K + first : K + first + HALF, K:] = re.astype(BF16)
+    for first, sign in ((0, 1.0), (HALF, by_lane)):
+        left = jnp.where(at_zero, 1.0, 2.0 * sign * even)
+        right = jnp.where(at_zero, by_row, -2.0 * sign * odd)
+        inv_two_ref[first : first + HALF, :] = beside(left, right).astype(BF16)
 
 
 def one_at(rows, lanes):
@@ -218,7 +225,7 @@
 
 
 def first_kernel(
-    scalars_ref, row_ref, pattern_hbm, ref_hbm, spec_ref, keep_ref, send_ref, bins_ref,
+    scalars_ref, pattern_hbm, ref_hbm, spec_ref, keep_ref, send_ref, bins_ref, row_ref,
     pattern_ref, ref_ref, fwd_one_ref, fwd_two_ref, inv_one_ref, inv_two_ref, now_ref, total_ref, cross_ref,
     weight_ref, ref_sem, pattern_sem,
 ):
@@ -233,12 +240,13 @@
     ref_copy.start()
     for number in range(groups):
         fetch(number).start()
-    fill_forward(row_ref, fwd_one_ref, fwd_two_ref)
-    fill_inverse(row_ref, inv_one_ref, inv_two_ref)
     total_ref[...] = jnp.zeros_like(total_ref)
     bins_ref[...] = jnp.zeros_like(bins_ref)
     weight_ref[...] = jnp.zeros_like(weight_ref)
     spec_ref[:GROUP] = jnp.zeros_like(spec_ref[:GROUP])
+    row_ref[...] = jnp.cos(iota((8, HALF), 1).astype(F32) * (2.0 * math.pi / K))
+    fill_forward(row_ref, fwd_one_ref, fwd_two_ref)
+    fill_inverse(row_ref, inv_one_ref, inv_two_ref)
     ref_copy.wait()
     hermitian_part(ref_ref, now_ref)
 
@@ -330,9 +338,10 @@
             pltpu.VMEM(HALF_SHAPE, F32),
             pltpu.VMEM(HALF_SHAPE, BF16),
             pltpu.VMEM((bins, K, K), BF16),
+            pltpu.VMEM((8, HALF), F32),
         ),
-        in_specs=[SCALARS, VMEM, HBM, HBM],
-        out_specs=(VMEM, VMEM, VMEM, VMEM),
+        in_specs=[SCALARS, HBM, HBM],
+        out_specs=(VMEM, VMEM, VMEM, VMEM, VMEM),
         scratch_shapes=scratch(
             (patterns.shape, BF16), (ref_spectrum.shape, F32), *TABLES, *WORK, ((count, 128), F32)
         )
@@ -340,10 +349,10 @@
         compiler_params=params(32),
         cost_estimate=pl.CostEstimate(flops=int(4e9), bytes_accessed=int(12e6), transcendentals=0),
         name="forward_and_correlate",
-    )(scalars, jnp.asarray(cosine_row()), in_hbm(patterns), in_hbm(ref_spectrum))
-
-
-def run_second(spectra, keep, other, scalars):
+    )(scalars, in_hbm(patterns), in_hbm(ref_spectrum))
+
+
+def run_second(spectra, keep, other, row, scalars):
     count = spectra.shape[0]
     return pl.pallas_call(
         second_kernel,
@@ -358,7 +367,7 @@
         compiler_params=params(32),
         cost_estimate=pl.CostEstimate(flops=int(3e9), bytes_accessed=int(4e6), transcendentals=0),
         name="correlate_again",
-    )(scalars, jnp.asarray(cosine_row()), spectra, keep, other)
+    )(scalars, row, spectra, keep, other)
 
 
 def run_last(keep, other, scalars):
@@ -397,7 +406,7 @@
     def over_lines(half):
         return [half] + [send(half, far, "row") for far in range(1, lines)]
 
-    spectra, keep, away, bins = run_first(patterns, ref_spectrum, scalars, columns * BINS)
+    spectra, keep, away, bins, row = run_first(patterns, ref_spectrum, scalars, columns * BINS)
     mine, other, other_far = jnp.split(bins, (chips * BINS, (2 * chips - 1) * BINS))
     half = add_halves(keep, send(away, 1))
     half, other, other_far = lax.optimization_barrier((half, other, other_far))
@@ -424,7 +433,7 @@
         half = add_halves(*over_lines(half))
         near = send(first, 2)
         inner = lax.ppermute(chip_bins(2, passing).astype(BF16), "col", pairs([(1, 3), (2, 0)]))
-        keep, away, weight = run_second(spectra, half, send(half, 1), scalars)
+        keep, away, weight = run_second(spectra, half, send(half, 1), row, scalars)
         away, middle, ends = lax.optimization_barrier((away, middle, ends))
         halves = over_lines(add_halves(keep, send(away, 1)))
         halves, near, inner = lax.optimization_barrier((halves, near, inner))
@@ -434,7 +443,7 @@
         half = add_halves(*over_lines(add_halves(*halves)))
         for far in range(1, chips):
             binned = binned + send(chip_bins(far).astype(BF16), 2 * far).astype(F32)
-        keep, away, weight = run_second(spectra, half, send(half, 1), scalars)
+        keep, away, weight = run_second(spectra, half, send(half, 1), row, scalars)
         half = add_halves(*over_lines(add_halves(keep, send(away, 1))))
     half = add_halves(*over_chips(half))
     return (run_last(half, send(half, 1), scalars), weight[:, 0], binned)

time: 78.1 us -> 77.3 us (0.990)
  transfers between devices with their start and end apart: 23 -> 23, of which waited for: 12 -> 11; matrix products, arithmetic and copies ran while one was open for 4% -> 4% of each run, Pallas kernels for 8% -> 7%
where the time goes in v6:
time: 77.3 us; the launch traced here: 77 us
  starting transfers between devices  34.3 us (44%)
  waiting for transfers between devices  20.2 us (26%)
  Pallas kernels  17.2 us (22%)
  other arithmetic  3.03 us (4%)
  local copies, waits for them, and re-layouts  1.52 us (2%)
  between operations  0.8 us (1%)
    ppermute x19, starting transfers between devices, send(): lax.ppermute(array, axis, [(i, i ^ far) for i in range(lax.axis_size(axis...  26.5 us
    ppermute x19, waiting for transfers between devices, send(): lax.ppermute(array, axis, [(i, i ^ far) for i in range(lax.axis_size(axis...  12 us
    pallas_call x1, Pallas kernels, run_first(): pl.pallas_call(first_kernel, out_shape=(pltpu.VMEM((count, 2 * ROWS, K),...  9.93 us
    ppermute x1, waiting for transfers between devices, on_device(): lax.ppermute(chip_bins(2, passing).astype(BF16), 'col', pairs([(1, 3), (2...  6.72 us
    pallas_call x1, Pallas kernels, run_second(): pl.pallas_call(second_kernel, out_shape=(pltpu.VMEM(HALF_SHAPE, F32), plt...  5.53 us
    ppermute x1, starting transfers between devices, on_device(): ends = lax.ppermute(second, 'col', pairs([(0, 2), (3, 1)]))  3.84 us
    ppermute x1, starting transfers between devices, on_device(): passing = lax.ppermute(block, 'col', pairs([(0, 1), (3, 2)]))  1.91 us
    pallas_call x1, Pallas kernels, run_last(): pl.pallas_call(last_kernel, out_shape=jax.ShapeDtypeStruct((2, K, K), F32...  1.74 us
  transfers between devices with their start and end apart: 23, of which 11 were waited for; matrix products, arithmetic and copies ran while one was open for 4% of the time, Pallas kernels for 7%

profile of v6, /device:TPU:1, one launch (start us, length us, event | category | flops | bytes accessed | tf_op | source)
XLA Modules:
  0.0 77.0 jit_solution(4533249029685377658)
XLA Ops:
  0.6 0.8 slice_bitcast_fusion.1
  2.2 9.9 %forward_and_correlate.1 = (bf16[16,288,256]{2,1,0:T(8,128)(2,1)S(1)}, f32[16,16,128]{2,1,0:T(8,128)S(1)}, bf16[16,16,128]{2,1,0:T(8,128)(2,1)S(1)}, bf16[32,256,256]{2,1,0:T(8,128)(2,1)S(1)}, f32[8,128]{1,0:T(8,128)S(1)}) custom-call(s32[49]{0:T(128)S(1)} %pad_add_fusion.scalars_ref, bf16[16,256,256]{2,1,0:T(8,128)(2,1)} %pattern_hbm.1, f32[2,256,256]{2,1,0:T(8,128)} %ref_hbm.1), custom_call_target="tpu_custom_call" | custom-call | flops 4000000000 | bytes 12000000 | tf_op jit(solution)/shard_map/forward_and_correlate/pallas_call | solution.py:334
  12.4 1.0 %collective-permute-done = bf16[16,16,128]{2,1,0:T(8,128)(2,1)S(1)} collective-permute-done((bf16[16,16,128]{2,1,0:T(8,128)(2,1)S(1)}, bf16[16,16,128]{2,1,0:T(8,128)(2,1)S(1)}, u32[]{:S(2)}, u32[]{:S(2)}) %collective-permute-start) | collective-permute-done | bytes 65568 | tf_op jit(solution)/shard_map/ppermute | solution.py:401
  14.0 4.5 %collective-permute-start.3 = (bf16[16,16,128]{2,1,0:T(8,128)(2,1)S(1)}, bf16[16,16,128]{2,1,0:T(8,128)(2,1)S(1)}, u32[]{:S(2)}, u32[]{:S(2)}) collective-permute-start(bf16[16,16,128]{2,1,0:T(8,128)(2,1)S(1)} %add_convert_fusion.8), channel_id=1, source_target_pairs={{0,6},{1,7},{2,4},{3,5},{4,2},{5,3},{6,0},{7,1},{8,14},{9,15},{10,... | collective-permute-start | bytes 196616 | tf_op jit(solution)/shard_map/ppermute | solution.py:401
  19.3 1.4 %collective-permute-done.3 = bf16[16,16,128]{2,1,0:T(8,128)(2,1)S(1)} collective-permute-done((bf16[16,16,128]{2,1,0:T(8,128)(2,1)S(1)}, bf16[16,16,128]{2,1,0:T(8,128)(2,1)S(1)}, u32[]{:S(2)}, u32[]{:S(2)}) %collective-permute-start.3) | collective-permute-done | bytes 65568 | tf_op jit(solution)/shard_map/ppermute | solution.py:401
  20.7 1.9 %collective-permute-start.17 = (bf16[4,256,256]{2,1,0:T(8,128)(2,1)S(1)}, bf16[4,256,256]{2,1,0:T(8,128)(2,1)S(1)}, u32[]{:S(2)}, u32[]{:S(2)}) collective-permute-start(bf16[4,256,256]{2,1,0:T(8,128)(2,1)S(1)} %get-tuple-element.38), channel_id=1, source_target_pairs={{0,2},{1,3},{6,4},{7,5},{8,10},{9,11},{14,12},{15,13},{16,18},{17,... | collective-permute-start | bytes 1572872 | tf_op jit(solution)/shard_map/ppermute | solution.py:430
  22.6 1.6 %collective-permute-done.2 = bf16[16,16,128]{2,1,0:T(8,128)(2,1)S(1)} collective-permute-done((bf16[16,16,128]{2,1,0:T(8,128)(2,1)S(1)}, bf16[16,16,128]{2,1,0:T(8,128)(2,1)S(1)}, u32[]{:S(2)}, u32[]{:S(2)}) %collective-permute-start.2) | collective-permute-done | bytes 65568 | tf_op jit(solution)/shard_map/ppermute | solution.py:401
  24.3 2.2 %collective-permute-start.8 = (bf16[16,16,128]{2,1,0:T(8,128)(2,1)S(1)}, bf16[16,16,128]{2,1,0:T(8,128)(2,1)S(1)}, u32[]{:S(2)}, u32[]{:S(2)}) collective-permute-start(bf16[16,16,128]{2,1,0:T(8,128)(2,1)S(1)} %add_convert_fusion.7), channel_id=1, source_target_pairs={{0,24},{8,16},{16,8},{24,0},{1,25},{9,17},{17,9},{25,1},{2,26},{10... | collective-permute-start | bytes 196616 | tf_op jit(solution)/shard_map/ppermute | solution.py:401
  28.3 3.8 %collective-permute-start.11 = (bf16[4,256,256]{2,1,0:T(8,128)(2,1)S(1)}, bf16[4,256,256]{2,1,0:T(8,128)(2,1)S(1)}, u32[]{:S(2)}, u32[]{:S(2)}) collective-permute-start(bf16[4,256,256]{2,1,0:T(8,128)(2,1)S(1)} %get-tuple-element.39), channel_id=1, source_target_pairs={{0,4},{1,5},{6,2},{7,3},{8,12},{9,13},{14,10},{15,11},{16,20},{17,... | collective-permute-start | bytes 1572872 | tf_op jit(solution)/shard_map/ppermute | solution.py:432
  32.3 3.1 %collective-permute-start.9 = (bf16[16,16,128]{2,1,0:T(8,128)(2,1)S(1)}, bf16[16,16,128]{2,1,0:T(8,128)(2,1)S(1)}, u32[]{:S(2)}, u32[]{:S(2)}) collective-permute-start(bf16[16,16,128]{2,1,0:T(8,128)(2,1)S(1)} %add_convert_fusion.6.old_ref), channel_id=1, source_target_pairs={{0,1},{1,0},{2,3},{3,2},{4,5},{5,4},{6,7},{7,6},{8,9},{9,8},{10,11... | collective-permute-start | bytes 196616 | tf_op jit(solution)/shard_map/ppermute | solution.py:401
  35.6 1.3 %collective-permute-start.18 = (bf16[4,256,256]{2,1,0:T(8,128)(2,1)S(1)}, bf16[4,256,256]{2,1,0:T(8,128)(2,1)S(1)}, u32[]{:S(2)}, u32[]{:S(2)}) collective-permute-start(bf16[4,256,256]{2,1,0:T(8,128)(2,1)S(1)} %add_convert_fusion), channel_id=1, source_target_pairs={{2,6},{3,7},{4,0},{5,1},{10,14},{11,15},{12,8},{13,9},{18,22},{19,... | collective-permute-start | bytes 1572872 | tf_op jit(solution)/shard_map/ppermute | solution.py:435
  37.0 5.5 %correlate_again.1 = (f32[16,16,128]{2,1,0:T(8,128)S(1)}, bf16[16,16,128]{2,1,0:T(8,128)(2,1)S(1)}, f32[16,128]{1,0:T(8,128)S(1)}) custom-call(s32[49]{0:T(128)S(1)} %pad_add_fusion.scalars_ref, f32[8,128]{1,0:T(8,128)S(1)} %get-tuple-element.27.row_ref, bf16[16,288,256]{2,1,0:T(8,128)(2,1)S(1)} %get-tuple-element.28.spec_ref, ...), custom_call_target="tpu_custom_call" | custom-call | flops 3000000000 | bytes 4000000 | tf_op jit(solution)/shard_map/correlate_again/pallas_call | solution.py:357
  42.5 1.5 %collective-permute-done.11 = bf16[4,256,256]{2,1,0:T(8,128)(2,1)S(1)} collective-permute-done((bf16[4,256,256]{2,1,0:T(8,128)(2,1)S(1)}, bf16[4,256,256]{2,1,0:T(8,128)(2,1)S(1)}, u32[]{:S(2)}, u32[]{:S(2)}) %collective-permute-start.11) | collective-permute-done | bytes 524320 | tf_op jit(solution)/shard_map/ppermute | solution.py:432
  44.0 4.0 %collective-permute-start.12 = (bf16[16,16,128]{2,1,0:T(8,128)(2,1)S(1)}, bf16[16,16,128]{2,1,0:T(8,128)(2,1)S(1)}, u32[]{:S(2)}, u32[]{:S(2)}) collective-permute-start(bf16[16,16,128]{2,1,0:T(8,128)(2,1)S(1)} %get-tuple-element.40), channel_id=1, source_target_pairs={{0,1},{1,0},{2,3},{3,2},{4,5},{5,4},{6,7},{7,6},{8,9},{9,8},{10,11... | collective-permute-start | bytes 196616 | tf_op jit(solution)/shard_map/ppermute | solution.py:401
  48.0 0.9 %collective-permute-done.12 = bf16[16,16,128]{2,1,0:T(8,128)(2,1)S(1)} collective-permute-done((bf16[16,16,128]{2,1,0:T(8,128)(2,1)S(1)}, bf16[16,16,128]{2,1,0:T(8,128)(2,1)S(1)}, u32[]{:S(2)}, u32[]{:S(2)}) %collective-permute-start.12) | collective-permute-done | bytes 65568 | tf_op jit(solution)/shard_map/ppermute | solution.py:401
  48.9 1.3 %collective-permute-start.13 = (bf16[16,16,128]{2,1,0:T(8,128)(2,1)S(1)}, bf16[16,16,128]{2,1,0:T(8,128)(2,1)S(1)}, u32[]{:S(2)}, u32[]{:S(2)}) collective-permute-start(bf16[16,16,128]{2,1,0:T(8,128)(2,1)S(1)} %add_convert_fusion.5), channel_id=1, source_target_pairs={{0,8},{8,0},{16,24},{24,16},{1,9},{9,1},{17,25},{25,17},{2,10},{10... | collective-permute-start | bytes 196616 | tf_op jit(solution)/shard_map/ppermute | solution.py:401
  50.2 1.2 %collective-permute-start.14 = (bf16[16,16,128]{2,1,0:T(8,128)(2,1)S(1)}, bf16[16,16,128]{2,1,0:T(8,128)(2,1)S(1)}, u32[]{:S(2)}, u32[]{:S(2)}) collective-permute-start(bf16[16,16,128]{2,1,0:T(8,128)(2,1)S(1)} %add_convert_fusion.5), channel_id=1, source_target_pairs={{0,16},{8,24},{16,0},{24,8},{1,17},{9,25},{17,1},{25,9},{2,18},{10... | collective-permute-start | bytes 196616 | tf_op jit(solution)/shard_map/ppermute | solution.py:401
  51.6 3.6 %collective-permute-done.16 = bf16[4,256,256]{2,1,0:T(8,128)(2,1)S(1)} collective-permute-done((bf16[4,256,256]{2,1,0:T(8,128)(2,1)S(1)}, bf16[4,256,256]{2,1,0:T(8,128)(2,1)S(1)}, u32[]{:S(2)}, u32[]{:S(2)}) %collective-permute-start.16) | collective-permute-done | bytes 524320 | tf_op jit(solution)/shard_map/ppermute | solution.py:401
  55.4 6.7 %collective-permute-done.18 = bf16[4,256,256]{2,1,0:T(8,128)(2,1)S(1)} collective-permute-done((bf16[4,256,256]{2,1,0:T(8,128)(2,1)S(1)}, bf16[4,256,256]{2,1,0:T(8,128)(2,1)S(1)}, u32[]{:S(2)}, u32[]{:S(2)}) %collective-permute-start.18) | collective-permute-done | bytes 524320 | tf_op jit(solution)/shard_map/ppermute | solution.py:435
  62.8 3.5 %collective-permute-start.20 = (bf16[16,16,128]{2,1,0:T(8,128)(2,1)S(1)}, bf16[16,16,128]{2,1,0:T(8,128)(2,1)S(1)}, u32[]{:S(2)}, u32[]{:S(2)}) collective-permute-start(bf16[16,16,128]{2,1,0:T(8,128)(2,1)S(1)} %add_convert_fusion.4), channel_id=1, source_target_pairs={{0,4},{1,5},{2,6},{3,7},{4,0},{5,1},{6,2},{7,3},{8,12},{9,13},{10,... | collective-permute-start | bytes 196616 | tf_op jit(solution)/shard_map/ppermute | solution.py:401
  67.2 2.3 %collective-permute-done.20 = bf16[16,16,128]{2,1,0:T(8,128)(2,1)S(1)} collective-permute-done((bf16[16,16,128]{2,1,0:T(8,128)(2,1)S(1)}, bf16[16,16,128]{2,1,0:T(8,128)(2,1)S(1)}, u32[]{:S(2)}, u32[]{:S(2)}) %collective-permute-start.20) | collective-permute-done | bytes 65568 | tf_op jit(solution)/shard_map/ppermute | solution.py:401
  69.6 4.4 %collective-permute-start.22 = (bf16[16,16,128]{2,1,0:T(8,128)(2,1)S(1)}, bf16[16,16,128]{2,1,0:T(8,128)(2,1)S(1)}, u32[]{:S(2)}, u32[]{:S(2)}) collective-permute-start(bf16[16,16,128]{2,1,0:T(8,128)(2,1)S(1)} %add_convert_fusion.3.old_ref), channel_id=1, source_target_pairs={{0,1},{1,0},{2,3},{3,2},{4,5},{5,4},{6,7},{7,6},{8,9},{9,8},{10,11... | collective-permute-start | bytes 196616 | tf_op jit(solution)/shard_map/ppermute | solution.py:401
  73.9 1.3 %convert_add_fusion = f32[4,256,256]{2,1,0:T(8,128)} fusion(bf16[4,256,256]{2,1,0:T(8,128)(2,1)S(1)} %collective-permute-done.18, bf16[4,256,256]{2,1,0:T(8,128)(2,1)S(1)} %collective-permute-done.16, bf16[4,256,256]{2,1,0:T(8,128)(2,1)S(1)} %collective-permute-done.11, bf16[4,256,256]{2,1,0:T(8,128)(2,1)S(1)} %collective-permute-done.10, ...), kind=kLoop, calls=%fused_computation | loop fusion | flops 2883584 | bytes 4194304 | tf_op jit(solution)/shard_map/add | solution.py:441
  75.3 1.7 %finish.1 = f32[2,256,256]{2,1,0:T(8,128)} custom-call(s32[49]{0:T(128)S(1)} %pad_add_fusion.scalars_ref, bf16[16,16,128]{2,1,0:T(8,128)(2,1)S(1)} %add_convert_fusion.3.old_ref, bf16[16,16,128]{2,1,0:T(8,128)(2,1)S(1)} %collective-permute-done.22.old_other_ref), custom_call_target="tpu_custom_call" | custom-call | flops 100000000 | bytes 1000000 | tf_op jit(solution)/shard_map/finish/pallas_call | solution.py:374
  (40 shorter events, 6.6 us)
Async XLA Ops:
  12.1 1.3 %collective-permute-start = (bf16[16,16,128]{2,1,0:T(8,128)(2,1)S(1)}, bf16[16,16,128]{2,1,0:T(8,128)(2,1)S(1)}, u32[]{:S(2)}, u32[]{:S(2)}) collective-permute-start(bf16[16,16,128]{2,1,0:T(8,128)(2,1)S(1)} %get-tuple-element.30), channel_id=1, source_target_pairs={{0,1},{1,0},{2,3},{3,2},{4,5},{5,4},{6,7},{7,6},{8,9},{9,8},{10,11... | collective-permute-start | bytes 196616 | tf_op jit(solution)/shard_map/ppermute | solution.py:401
  13.4 5.3 %collective-permute-start.5 = (bf16[12,256,256]{2,1,0:T(8,128)(2,1)S(1)}, bf16[12,256,256]{2,1,0:T(8,128)(2,1)S(1)}, u32[]{:S(2)}, u32[]{:S(2)}) collective-permute-start(bf16[12,256,256]{2,1,0:T(8,128)(2,1)S(1)} %split.7), channel_id=1, source_target_pairs={{0,1},{1,0},{2,3},{3,2},{4,5},{5,4},{6,7},{7,6},{8,9},{9,8},{10,11... | collective-permute-start | bytes 4718600 | tf_op jit(solution)/shard_map/ppermute | solution.py:401
  13.7 5.1 %collective-permute-start.4 = (bf16[4,256,256]{2,1,0:T(8,128)(2,1)S(1)}, bf16[4,256,256]{2,1,0:T(8,128)(2,1)S(1)}, u32[]{:S(2)}, u32[]{:S(2)}) collective-permute-start(bf16[4,256,256]{2,1,0:T(8,128)(2,1)S(1)} %split.8), channel_id=1, source_target_pairs={{0,1},{1,0},{2,3},{3,2},{4,5},{5,4},{6,7},{7,6},{8,9},{9,8},{10,11... | collective-permute-start | bytes 1572872 | tf_op jit(solution)/shard_map/ppermute | solution.py:401
  14.0 6.6 %collective-permute-start.3 = (bf16[16,16,128]{2,1,0:T(8,128)(2,1)S(1)}, bf16[16,16,128]{2,1,0:T(8,128)(2,1)S(1)}, u32[]{:S(2)}, u32[]{:S(2)}) collective-permute-start(bf16[16,16,128]{2,1,0:T(8,128)(2,1)S(1)} %add_convert_fusion.8), channel_id=1, source_target_pairs={{0,6},{1,7},{2,4},{3,5},{4,2},{5,3},{6,0},{7,1},{8,14},{9,15},{10,... | collective-permute-start | bytes 196616 | tf_op jit(solution)/shard_map/ppermute | solution.py:401
  18.5 5.7 %collective-permute-start.2 = (bf16[16,16,128]{2,1,0:T(8,128)(2,1)S(1)}, bf16[16,16,128]{2,1,0:T(8,128)(2,1)S(1)}, u32[]{:S(2)}, u32[]{:S(2)}) collective-permute-start(bf16[16,16,128]{2,1,0:T(8,128)(2,1)S(1)} %add_convert_fusion.8), channel_id=1, source_target_pairs={{0,4},{1,5},{2,6},{3,7},{4,0},{5,1},{6,2},{7,3},{8,12},{9,13},{10,... | collective-permute-start | bytes 196616 | tf_op jit(solution)/shard_map/ppermute | solution.py:401
  18.5 5.7 %collective-permute-start.1 = (bf16[16,16,128]{2,1,0:T(8,128)(2,1)S(1)}, bf16[16,16,128]{2,1,0:T(8,128)(2,1)S(1)}, u32[]{:S(2)}, u32[]{:S(2)}) collective-permute-start(bf16[16,16,128]{2,1,0:T(8,128)(2,1)S(1)} %add_convert_fusion.8), channel_id=1, source_target_pairs={{0,2},{1,3},{2,0},{3,1},{4,6},{5,7},{6,4},{7,5},{8,10},{9,11},{10,... | collective-permute-start | bytes 196616 | tf_op jit(solution)/shard_map/ppermute | solution.py:401
  20.7 14.7 %collective-permute-start.17 = (bf16[4,256,256]{2,1,0:T(8,128)(2,1)S(1)}, bf16[4,256,256]{2,1,0:T(8,128)(2,1)S(1)}, u32[]{:S(2)}, u32[]{:S(2)}) collective-permute-start(bf16[4,256,256]{2,1,0:T(8,128)(2,1)S(1)} %get-tuple-element.38), channel_id=1, source_target_pairs={{0,2},{1,3},{6,4},{7,5},{8,10},{9,11},{14,12},{15,13},{16,18},{17,... | collective-permute-start | bytes 1572872 | tf_op jit(solution)/shard_map/ppermute | solution.py:430
  24.3 4.1 %collective-permute-start.8 = (bf16[16,16,128]{2,1,0:T(8,128)(2,1)S(1)}, bf16[16,16,128]{2,1,0:T(8,128)(2,1)S(1)}, u32[]{:S(2)}, u32[]{:S(2)}) collective-permute-start(bf16[16,16,128]{2,1,0:T(8,128)(2,1)S(1)} %add_convert_fusion.7), channel_id=1, source_target_pairs={{0,24},{8,16},{16,8},{24,0},{1,25},{9,17},{17,9},{25,1},{2,26},{10... | collective-permute-start | bytes 196616 | tf_op jit(solution)/shard_map/ppermute | solution.py:401
  26.5 5.7 %collective-permute-start.7 = (bf16[16,16,128]{2,1,0:T(8,128)(2,1)S(1)}, bf16[16,16,128]{2,1,0:T(8,128)(2,1)S(1)}, u32[]{:S(2)}, u32[]{:S(2)}) collective-permute-start(bf16[16,16,128]{2,1,0:T(8,128)(2,1)S(1)} %add_convert_fusion.7), channel_id=1, source_target_pairs={{0,16},{8,24},{16,0},{24,8},{1,17},{9,25},{17,1},{25,9},{2,18},{10... | collective-permute-start | bytes 196616 | tf_op jit(solution)/shard_map/ppermute | solution.py:401
  26.7 5.5 %collective-permute-start.6 = (bf16[16,16,128]{2,1,0:T(8,128)(2,1)S(1)}, bf16[16,16,128]{2,1,0:T(8,128)(2,1)S(1)}, u32[]{:S(2)}, u32[]{:S(2)}) collective-permute-start(bf16[16,16,128]{2,1,0:T(8,128)(2,1)S(1)} %add_convert_fusion.7), channel_id=1, source_target_pairs={{0,8},{8,0},{16,24},{24,16},{1,9},{9,1},{17,25},{25,17},{2,10},{10... | collective-permute-start | bytes 196616 | tf_op jit(solution)/shard_map/ppermute | solution.py:401
  27.0 15.5 %collective-permute-start.10 = (bf16[4,256,256]{2,1,0:T(8,128)(2,1)S(1)}, bf16[4,256,256]{2,1,0:T(8,128)(2,1)S(1)}, u32[]{:S(2)}, u32[]{:S(2)}) collective-permute-start(bf16[4,256,256]{2,1,0:T(8,128)(2,1)S(1)} %get-tuple-element.38), channel_id=1, source_target_pairs={{2,4},{3,5},{4,2},{5,3},{10,12},{11,13},{12,10},{13,11},{18,20},{1... | collective-permute-start | bytes 1572872 | tf_op jit(solution)/shard_map/ppermute | solution.py:431
  28.3 15.6 %collective-permute-start.11 = (bf16[4,256,256]{2,1,0:T(8,128)(2,1)S(1)}, bf16[4,256,256]{2,1,0:T(8,128)(2,1)S(1)}, u32[]{:S(2)}, u32[]{:S(2)}) collective-permute-start(bf16[4,256,256]{2,1,0:T(8,128)(2,1)S(1)} %get-tuple-element.39), channel_id=1, source_target_pairs={{0,4},{1,5},{6,2},{7,3},{8,12},{9,13},{14,10},{15,11},{16,20},{17,... | collective-permute-start | bytes 1572872 | tf_op jit(solution)/shard_map/ppermute | solution.py:432
  32.2 23.0 %collective-permute-start.16 = (bf16[4,256,256]{2,1,0:T(8,128)(2,1)S(1)}, bf16[4,256,256]{2,1,0:T(8,128)(2,1)S(1)}, u32[]{:S(2)}, u32[]{:S(2)}) collective-permute-start(bf16[4,256,256]{2,1,0:T(8,128)(2,1)S(1)} %get-tuple-element.41), channel_id=1, source_target_pairs={{0,2},{1,3},{2,0},{3,1},{4,6},{5,7},{6,4},{7,5},{8,10},{9,11},{10,... | collective-permute-start | bytes 1572872 | tf_op jit(solution)/shard_map/ppermute | solution.py:401
  32.3 4.6 %collective-permute-start.9 = (bf16[16,16,128]{2,1,0:T(8,128)(2,1)S(1)}, bf16[16,16,128]{2,1,0:T(8,128)(2,1)S(1)}, u32[]{:S(2)}, u32[]{:S(2)}) collective-permute-start(bf16[16,16,128]{2,1,0:T(8,128)(2,1)S(1)} %add_convert_fusion.6.old_ref), channel_id=1, source_target_pairs={{0,1},{1,0},{2,3},{3,2},{4,5},{5,4},{6,7},{7,6},{8,9},{9,8},{10,11... | collective-permute-start | bytes 196616 | tf_op jit(solution)/shard_map/ppermute | solution.py:401
  35.6 26.5 %collective-permute-start.18 = (bf16[4,256,256]{2,1,0:T(8,128)(2,1)S(1)}, bf16[4,256,256]{2,1,0:T(8,128)(2,1)S(1)}, u32[]{:S(2)}, u32[]{:S(2)}) collective-permute-start(bf16[4,256,256]{2,1,0:T(8,128)(2,1)S(1)} %add_convert_fusion), channel_id=1, source_target_pairs={{2,6},{3,7},{4,0},{5,1},{10,14},{11,15},{12,8},{13,9},{18,22},{19,... | collective-permute-start | bytes 1572872 | tf_op jit(solution)/shard_map/ppermute | solution.py:435
  44.0 4.9 %collective-permute-start.12 = (bf16[16,16,128]{2,1,0:T(8,128)(2,1)S(1)}, bf16[16,16,128]{2,1,0:T(8,128)(2,1)S(1)}, u32[]{:S(2)}, u32[]{:S(2)}) collective-permute-start(bf16[16,16,128]{2,1,0:T(8,128)(2,1)S(1)} %get-tuple-element.40), channel_id=1, source_target_pairs={{0,1},{1,0},{2,3},{3,2},{4,5},{5,4},{6,7},{7,6},{8,9},{9,8},{10,11... | collective-permute-start | bytes 196616 | tf_op jit(solution)/shard_map/ppermute | solution.py:401
  48.9 6.3 %collective-permute-start.13 = (bf16[16,16,128]{2,1,0:T(8,128)(2,1)S(1)}, bf16[16,16,128]{2,1,0:T(8,128)(2,1)S(1)}, u32[]{:S(2)}, u32[]{:S(2)}) collective-permute-start(bf16[16,16,128]{2,1,0:T(8,128)(2,1)S(1)} %add_convert_fusion.5), channel_id=1, source_target_pairs={{0,8},{8,0},{16,24},{24,16},{1,9},{9,1},{17,25},{25,17},{2,10},{10... | collective-permute-start | bytes 196616 | tf_op jit(solution)/shard_map/ppermute | solution.py:401
  50.2 5.0 %collective-permute-start.14 = (bf16[16,16,128]{2,1,0:T(8,128)(2,1)S(1)}, bf16[16,16,128]{2,1,0:T(8,128)(2,1)S(1)}, u32[]{:S(2)}, u32[]{:S(2)}) collective-permute-start(bf16[16,16,128]{2,1,0:T(8,128)(2,1)S(1)} %add_convert_fusion.5), channel_id=1, source_target_pairs={{0,16},{8,24},{16,0},{24,8},{1,17},{9,25},{17,1},{25,9},{2,18},{10... | collective-permute-start | bytes 196616 | tf_op jit(solution)/shard_map/ppermute | solution.py:401
  51.4 4.0 %collective-permute-start.15 = (bf16[16,16,128]{2,1,0:T(8,128)(2,1)S(1)}, bf16[16,16,128]{2,1,0:T(8,128)(2,1)S(1)}, u32[]{:S(2)}, u32[]{:S(2)}) collective-permute-start(bf16[16,16,128]{2,1,0:T(8,128)(2,1)S(1)} %add_convert_fusion.5), channel_id=1, source_target_pairs={{0,24},{8,16},{16,8},{24,0},{1,25},{9,17},{17,9},{25,1},{2,26},{10... | collective-permute-start | bytes 196616 | tf_op jit(solution)/shard_map/ppermute | solution.py:401
  62.2 5.0 %collective-permute-start.21 = (bf16[16,16,128]{2,1,0:T(8,128)(2,1)S(1)}, bf16[16,16,128]{2,1,0:T(8,128)(2,1)S(1)}, u32[]{:S(2)}, u32[]{:S(2)}) collective-permute-start(bf16[16,16,128]{2,1,0:T(8,128)(2,1)S(1)} %add_convert_fusion.4), channel_id=1, source_target_pairs={{0,6},{1,7},{2,4},{3,5},{4,2},{5,3},{6,0},{7,1},{8,14},{9,15},{10,... | collective-permute-start | bytes 196616 | tf_op jit(solution)/shard_map/ppermute | solution.py:401
  62.8 6.7 %collective-permute-start.20 = (bf16[16,16,128]{2,1,0:T(8,128)(2,1)S(1)}, bf16[16,16,128]{2,1,0:T(8,128)(2,1)S(1)}, u32[]{:S(2)}, u32[]{:S(2)}) collective-permute-start(bf16[16,16,128]{2,1,0:T(8,128)(2,1)S(1)} %add_convert_fusion.4), channel_id=1, source_target_pairs={{0,4},{1,5},{2,6},{3,7},{4,0},{5,1},{6,2},{7,3},{8,12},{9,13},{10,... | collective-permute-start | bytes 196616 | tf_op jit(solution)/shard_map/ppermute | solution.py:401
  66.3 3.2 %collective-permute-start.19 = (bf16[16,16,128]{2,1,0:T(8,128)(2,1)S(1)}, bf16[16,16,128]{2,1,0:T(8,128)(2,1)S(1)}, u32[]{:S(2)}, u32[]{:S(2)}) collective-permute-start(bf16[16,16,128]{2,1,0:T(8,128)(2,1)S(1)} %add_convert_fusion.4), channel_id=1, source_target_pairs={{0,2},{1,3},{2,0},{3,1},{4,6},{5,7},{6,4},{7,5},{8,10},{9,11},{10,... | collective-permute-start | bytes 196616 | tf_op jit(solution)/shard_map/ppermute | solution.py:401
  69.6 5.7 %collective-permute-start.22 = (bf16[16,16,128]{2,1,0:T(8,128)(2,1)S(1)}, bf16[16,16,128]{2,1,0:T(8,128)(2,1)S(1)}, u32[]{:S(2)}, u32[]{:S(2)}) collective-permute-start(bf16[16,16,128]{2,1,0:T(8,128)(2,1)S(1)} %add_convert_fusion.3.old_ref), channel_id=1, source_target_pairs={{0,1},{1,0},{2,3},{3,2},{4,5},{5,4},{6,7},{7,6},{8,9},{9,8},{10,11... | collective-permute-start | bytes 196616 | tf_op jit(solution)/shard_map/ppermute | solution.py:401

commit v7 on v6

--- a/solution.py
+++ b/solution.py
@@ -8,7 +8,6 @@
 from jax.sharding import PartitionSpec as P
 
 BINS = 4
-ITERS = 2
 K = 256
 HALF = K // 2
 ROWS = HALF + 16
@@ -238,8 +237,7 @@
 
     ref_copy = pltpu.make_async_copy(ref_hbm, ref_ref, ref_sem)
     ref_copy.start()
-    for number in range(groups):
-        fetch(number).start()
+    fetch(0).start()
     total_ref[...] = jnp.zeros_like(total_ref)
     bins_ref[...] = jnp.zeros_like(bins_ref)
     weight_ref[...] = jnp.zeros_like(weight_ref)
@@ -248,6 +246,8 @@
     fill_forward(row_ref, fwd_one_ref, fwd_two_ref)
     fill_inverse(row_ref, inv_one_ref, inv_two_ref)
     ref_copy.wait()
+    for number in range(1, groups):
+        fetch(number).start()
     hermitian_part(ref_ref, now_ref)
 
     def finish(first):
@@ -445,7 +445,8 @@
             binned = binned + send(chip_bins(far).astype(BF16), 2 * far).astype(F32)
         keep, away, weight = run_second(spectra, half, send(half, 1), row, scalars)
         half = add_halves(*over_lines(add_halves(keep, send(away, 1))))
-    half = add_halves(*over_chips(half))
+    halves, binned = lax.optimization_barrier((over_chips(half), binned))
+    half = add_halves(*halves)
     return (run_last(half, send(half, 1), scalars), weight[:, 0], binned)
 
 

time: 77.3 us -> 76.7 us (level)
  transfers between devices with their start and end apart: 23 -> 23, of which waited for: 11 -> 12; matrix products, arithmetic and copies ran while one was open for 4% -> 4% of each run, Pallas kernels for 7% -> 7%
where the time goes in v7:
time: 76.7 us; the launch traced here: 76.2 us
  starting transfers between devices  34.2 us (45%)
  waiting for transfers between devices  19.9 us (26%)
  Pallas kernels  16.7 us (22%)
  other arithmetic  3.03 us (4%)
  local copies, waits for them, and re-layouts  1.52 us (2%)
  between operations  0.8 us (1%)
    ppermute x19, starting transfers between devices, send(): lax.ppermute(array, axis, [(i, i ^ far) for i in range(lax.axis_size(axis...  26.5 us
    ppermute x19, waiting for transfers between devices, send(): lax.ppermute(array, axis, [(i, i ^ far) for i in range(lax.axis_size(axis...  11.7 us
    pallas_call x1, Pallas kernels, run_first(): pl.pallas_call(first_kernel, out_shape=(pltpu.VMEM((count, 2 * ROWS, K),...  9.46 us
    ppermute x1, waiting for transfers between devices, on_device(): lax.ppermute(chip_bins(2, passing).astype(BF16), 'col', pairs([(1, 3), (2...  6.72 us
    pallas_call x1, Pallas kernels, run_second(): pl.pallas_call(second_kernel, out_shape=(pltpu.VMEM(HALF_SHAPE, F32), plt...  5.53 us
    ppermute x1, starting transfers between devices, on_device(): ends = lax.ppermute(second, 'col', pairs([(0, 2), (3, 1)]))  3.83 us
    ppermute x1, starting transfers between devices, on_device(): passing = lax.ppermute(block, 'col', pairs([(0, 1), (3, 2)]))  1.9 us
    pallas_call x1, Pallas kernels, run_last(): pl.pallas_call(last_kernel, out_shape=jax.ShapeDtypeStruct((2, K, K), F32...  1.74 us
  transfers between devices with their start and end apart: 23, of which 12 were waited for; matrix products, arithmetic and copies ran while one was open for 4% of the time, Pallas kernels for 7%

profile of v7, /device:TPU:1, one launch (start us, length us, event | category | flops | bytes accessed | tf_op | source)
XLA Modules:
  0.0 76.2 jit_solution(1786464006365050482)
XLA Ops:
  2.2 9.5 %forward_and_correlate.1 = (bf16[16,288,256]{2,1,0:T(8,128)(2,1)S(1)}, f32[16,16,128]{2,1,0:T(8,128)S(1)}, bf16[16,16,128]{2,1,0:T(8,128)(2,1)S(1)}, bf16[32,256,256]{2,1,0:T(8,128)(2,1)S(1)}, f32[8,128]{1,0:T(8,128)S(1)}) custom-call(s32[49]{0:T(128)S(1)} %pad_add_fusion.scalars_ref, bf16[16,256,256]{2,1,0:T(8,128)(2,1)} %pattern_hbm.1, f32[2,256,256]{2,1,0:T(8,128)} %ref_hbm.1), custom_call_target="tpu_custom_call" | custom-call | flops 4000000000 | bytes 12000000 | tf_op jit(solution)/shard_map/forward_and_correlate/pallas_call | solution.py:334
  11.9 1.0 %collective-permute-done = bf16[16,16,128]{2,1,0:T(8,128)(2,1)S(1)} collective-permute-done((bf16[16,16,128]{2,1,0:T(8,128)(2,1)S(1)}, bf16[16,16,128]{2,1,0:T(8,128)(2,1)S(1)}, u32[]{:S(2)}, u32[]{:S(2)}) %collective-permute-start) | collective-permute-done | bytes 65568 | tf_op jit(solution)/shard_map/ppermute | solution.py:401
  13.6 4.5 %collective-permute-start.3 = (bf16[16,16,128]{2,1,0:T(8,128)(2,1)S(1)}, bf16[16,16,128]{2,1,0:T(8,128)(2,1)S(1)}, u32[]{:S(2)}, u32[]{:S(2)}) collective-permute-start(bf16[16,16,128]{2,1,0:T(8,128)(2,1)S(1)} %add_convert_fusion.8), channel_id=1, source_target_pairs={{0,6},{1,7},{2,4},{3,5},{4,2},{5,3},{6,0},{7,1},{8,14},{9,15},{10,... | collective-permute-start | bytes 196616 | tf_op jit(solution)/shard_map/ppermute | solution.py:401
  18.8 1.4 %collective-permute-done.3 = bf16[16,16,128]{2,1,0:T(8,128)(2,1)S(1)} collective-permute-done((bf16[16,16,128]{2,1,0:T(8,128)(2,1)S(1)}, bf16[16,16,128]{2,1,0:T(8,128)(2,1)S(1)}, u32[]{:S(2)}, u32[]{:S(2)}) %collective-permute-start.3) | collective-permute-done | bytes 65568 | tf_op jit(solution)/shard_map/ppermute | solution.py:401
  20.2 1.9 %collective-permute-start.17 = (bf16[4,256,256]{2,1,0:T(8,128)(2,1)S(1)}, bf16[4,256,256]{2,1,0:T(8,128)(2,1)S(1)}, u32[]{:S(2)}, u32[]{:S(2)}) collective-permute-start(bf16[4,256,256]{2,1,0:T(8,128)(2,1)S(1)} %get-tuple-element.43), channel_id=1, source_target_pairs={{0,2},{1,3},{6,4},{7,5},{8,10},{9,11},{14,12},{15,13},{16,18},{17,... | collective-permute-start | bytes 1572872 | tf_op jit(solution)/shard_map/ppermute | solution.py:430
  22.1 1.6 %collective-permute-done.2 = bf16[16,16,128]{2,1,0:T(8,128)(2,1)S(1)} collective-permute-done((bf16[16,16,128]{2,1,0:T(8,128)(2,1)S(1)}, bf16[16,16,128]{2,1,0:T(8,128)(2,1)S(1)}, u32[]{:S(2)}, u32[]{:S(2)}) %collective-permute-start.2) | collective-permute-done | bytes 65568 | tf_op jit(solution)/shard_map/ppermute | solution.py:401
  23.8 2.2 %collective-permute-start.8 = (bf16[16,16,128]{2,1,0:T(8,128)(2,1)S(1)}, bf16[16,16,128]{2,1,0:T(8,128)(2,1)S(1)}, u32[]{:S(2)}, u32[]{:S(2)}) collective-permute-start(bf16[16,16,128]{2,1,0:T(8,128)(2,1)S(1)} %add_convert_fusion.7), channel_id=1, source_target_pairs={{0,24},{8,16},{16,8},{24,0},{1,25},{9,17},{17,9},{25,1},{2,26},{10... | collective-permute-start | bytes 196616 | tf_op jit(solution)/shard_map/ppermute | solution.py:401
  27.9 3.8 %collective-permute-start.11 = (bf16[4,256,256]{2,1,0:T(8,128)(2,1)S(1)}, bf16[4,256,256]{2,1,0:T(8,128)(2,1)S(1)}, u32[]{:S(2)}, u32[]{:S(2)}) collective-permute-start(bf16[4,256,256]{2,1,0:T(8,128)(2,1)S(1)} %get-tuple-element.44), channel_id=1, source_target_pairs={{0,4},{1,5},{6,2},{7,3},{8,12},{9,13},{14,10},{15,11},{16,20},{17,... | collective-permute-start | bytes 1572872 | tf_op jit(solution)/shard_map/ppermute | solution.py:432
  31.9 3.1 %collective-permute-start.9 = (bf16[16,16,128]{2,1,0:T(8,128)(2,1)S(1)}, bf16[16,16,128]{2,1,0:T(8,128)(2,1)S(1)}, u32[]{:S(2)}, u32[]{:S(2)}) collective-permute-start(bf16[16,16,128]{2,1,0:T(8,128)(2,1)S(1)} %add_convert_fusion.6.old_ref), channel_id=1, source_target_pairs={{0,1},{1,0},{2,3},{3,2},{4,5},{5,4},{6,7},{7,6},{8,9},{9,8},{10,11... | collective-permute-start | bytes 196616 | tf_op jit(solution)/shard_map/ppermute | solution.py:401
  35.2 1.3 %collective-permute-start.18 = (bf16[4,256,256]{2,1,0:T(8,128)(2,1)S(1)}, bf16[4,256,256]{2,1,0:T(8,128)(2,1)S(1)}, u32[]{:S(2)}, u32[]{:S(2)}) collective-permute-start(bf16[4,256,256]{2,1,0:T(8,128)(2,1)S(1)} %add_convert_fusion), channel_id=1, source_target_pairs={{2,6},{3,7},{4,0},{5,1},{10,14},{11,15},{12,8},{13,9},{18,22},{19,... | collective-permute-start | bytes 1572872 | tf_op jit(solution)/shard_map/ppermute | solution.py:435
  36.5 5.5 %correlate_again.1 = (f32[16,16,128]{2,1,0:T(8,128)S(1)}, bf16[16,16,128]{2,1,0:T(8,128)(2,1)S(1)}, f32[16,128]{1,0:T(8,128)S(1)}) custom-call(s32[49]{0:T(128)S(1)} %pad_add_fusion.scalars_ref, f32[8,128]{1,0:T(8,128)S(1)} %get-tuple-element.32.row_ref, bf16[16,288,256]{2,1,0:T(8,128)(2,1)S(1)} %get-tuple-element.33.spec_ref, ...), custom_call_target="tpu_custom_call" | custom-call | flops 3000000000 | bytes 4000000 | tf_op jit(solution)/shard_map/correlate_again/pallas_call | solution.py:357
  42.0 1.5 %collective-permute-done.11 = bf16[4,256,256]{2,1,0:T(8,128)(2,1)S(1)} collective-permute-done((bf16[4,256,256]{2,1,0:T(8,128)(2,1)S(1)}, bf16[4,256,256]{2,1,0:T(8,128)(2,1)S(1)}, u32[]{:S(2)}, u32[]{:S(2)}) %collective-permute-start.11) | collective-permute-done | bytes 524320 | tf_op jit(solution)/shard_map/ppermute | solution.py:432
  43.5 4.0 %collective-permute-start.12 = (bf16[16,16,128]{2,1,0:T(8,128)(2,1)S(1)}, bf16[16,16,128]{2,1,0:T(8,128)(2,1)S(1)}, u32[]{:S(2)}, u32[]{:S(2)}) collective-permute-start(bf16[16,16,128]{2,1,0:T(8,128)(2,1)S(1)} %get-tuple-element.45), channel_id=1, source_target_pairs={{0,1},{1,0},{2,3},{3,2},{4,5},{5,4},{6,7},{7,6},{8,9},{9,8},{10,11... | collective-permute-start | bytes 196616 | tf_op jit(solution)/shard_map/ppermute | solution.py:401
  47.5 0.9 %collective-permute-done.12 = bf16[16,16,128]{2,1,0:T(8,128)(2,1)S(1)} collective-permute-done((bf16[16,16,128]{2,1,0:T(8,128)(2,1)S(1)}, bf16[16,16,128]{2,1,0:T(8,128)(2,1)S(1)}, u32[]{:S(2)}, u32[]{:S(2)}) %collective-permute-start.12) | collective-permute-done | bytes 65568 | tf_op jit(solution)/shard_map/ppermute | solution.py:401
  48.4 1.3 %collective-permute-start.13 = (bf16[16,16,128]{2,1,0:T(8,128)(2,1)S(1)}, bf16[16,16,128]{2,1,0:T(8,128)(2,1)S(1)}, u32[]{:S(2)}, u32[]{:S(2)}) collective-permute-start(bf16[16,16,128]{2,1,0:T(8,128)(2,1)S(1)} %add_convert_fusion.5), channel_id=1, source_target_pairs={{0,8},{8,0},{16,24},{24,16},{1,9},{9,1},{17,25},{25,17},{2,10},{10... | collective-permute-start | bytes 196616 | tf_op jit(solution)/shard_map/ppermute | solution.py:401
  49.7 1.2 %collective-permute-start.14 = (bf16[16,16,128]{2,1,0:T(8,128)(2,1)S(1)}, bf16[16,16,128]{2,1,0:T(8,128)(2,1)S(1)}, u32[]{:S(2)}, u32[]{:S(2)}) collective-permute-start(bf16[16,16,128]{2,1,0:T(8,128)(2,1)S(1)} %add_convert_fusion.5), channel_id=1, source_target_pairs={{0,16},{8,24},{16,0},{24,8},{1,17},{9,25},{17,1},{25,9},{2,18},{10... | collective-permute-start | bytes 196616 | tf_op jit(solution)/shard_map/ppermute | solution.py:401
  51.1 3.6 %collective-permute-done.16 = bf16[4,256,256]{2,1,0:T(8,128)(2,1)S(1)} collective-permute-done((bf16[4,256,256]{2,1,0:T(8,128)(2,1)S(1)}, bf16[4,256,256]{2,1,0:T(8,128)(2,1)S(1)}, u32[]{:S(2)}, u32[]{:S(2)}) %collective-permute-start.16) | collective-permute-done | bytes 524320 | tf_op jit(solution)/shard_map/ppermute | solution.py:401
  55.0 6.7 %collective-permute-done.18 = bf16[4,256,256]{2,1,0:T(8,128)(2,1)S(1)} collective-permute-done((bf16[4,256,256]{2,1,0:T(8,128)(2,1)S(1)}, bf16[4,256,256]{2,1,0:T(8,128)(2,1)S(1)}, u32[]{:S(2)}, u32[]{:S(2)}) %collective-permute-start.18) | collective-permute-done | bytes 524320 | tf_op jit(solution)/shard_map/ppermute | solution.py:435
  61.7 3.0 %collective-permute-start.19 = (bf16[16,16,128]{2,1,0:T(8,128)(2,1)S(1)}, bf16[16,16,128]{2,1,0:T(8,128)(2,1)S(1)}, u32[]{:S(2)}, u32[]{:S(2)}) collective-permute-start(bf16[16,16,128]{2,1,0:T(8,128)(2,1)S(1)} %add_convert_fusion.4), channel_id=1, source_target_pairs={{0,2},{1,3},{2,0},{3,1},{4,6},{5,7},{6,4},{7,5},{8,10},{9,11},{10,... | collective-permute-start | bytes 196616 | tf_op jit(solution)/shard_map/ppermute | solution.py:401
  64.8 2.0 %collective-permute-start.21 = (bf16[16,16,128]{2,1,0:T(8,128)(2,1)S(1)}, bf16[16,16,128]{2,1,0:T(8,128)(2,1)S(1)}, u32[]{:S(2)}, u32[]{:S(2)}) collective-permute-start(bf16[16,16,128]{2,1,0:T(8,128)(2,1)S(1)} %add_convert_fusion.4), channel_id=1, source_target_pairs={{0,6},{1,7},{2,4},{3,5},{4,2},{5,3},{6,0},{7,1},{8,14},{9,15},{10,... | collective-permute-start | bytes 196616 | tf_op jit(solution)/shard_map/ppermute | solution.py:401
  66.9 1.3 %convert_add_fusion = f32[4,256,256]{2,1,0:T(8,128)} fusion(bf16[4,256,256]{2,1,0:T(8,128)(2,1)S(1)} %collective-permute-done.18, bf16[4,256,256]{2,1,0:T(8,128)(2,1)S(1)} %collective-permute-done.16, bf16[4,256,256]{2,1,0:T(8,128)(2,1)S(1)} %collective-permute-done.11, bf16[4,256,256]{2,1,0:T(8,128)(2,1)S(1)} %collective-permute-done.10, ...), kind=kLoop, calls=%fused_computation | loop fusion | flops 2883584 | bytes 4194304 | tf_op jit(solution)/shard_map/add | solution.py:441
  68.2 1.6 %collective-permute-done.20 = bf16[16,16,128]{2,1,0:T(8,128)(2,1)S(1)} collective-permute-done((bf16[16,16,128]{2,1,0:T(8,128)(2,1)S(1)}, bf16[16,16,128]{2,1,0:T(8,128)(2,1)S(1)}, u32[]{:S(2)}, u32[]{:S(2)}) %collective-permute-start.20) | collective-permute-done | bytes 65568 | tf_op jit(solution)/shard_map/ppermute | solution.py:401
  70.2 3.4 %collective-permute-start.22 = (bf16[16,16,128]{2,1,0:T(8,128)(2,1)S(1)}, bf16[16,16,128]{2,1,0:T(8,128)(2,1)S(1)}, u32[]{:S(2)}, u32[]{:S(2)}) collective-permute-start(bf16[16,16,128]{2,1,0:T(8,128)(2,1)S(1)} %add_convert_fusion.3.old_ref), channel_id=1, source_target_pairs={{0,1},{1,0},{2,3},{3,2},{4,5},{5,4},{6,7},{7,6},{8,9},{9,8},{10,11... | collective-permute-start | bytes 196616 | tf_op jit(solution)/shard_map/ppermute | solution.py:401
  74.5 1.7 %finish.1 = f32[2,256,256]{2,1,0:T(8,128)} custom-call(s32[49]{0:T(128)S(1)} %pad_add_fusion.scalars_ref, bf16[16,16,128]{2,1,0:T(8,128)(2,1)S(1)} %add_convert_fusion.3.old_ref, bf16[16,16,128]{2,1,0:T(8,128)(2,1)S(1)} %collective-permute-done.22.old_other_ref), custom_call_target="tpu_custom_call" | custom-call | flops 100000000 | bytes 1000000 | tf_op jit(solution)/shard_map/finish/pallas_call | solution.py:374
  (40 shorter events, 7.3 us)
Async XLA Ops:
  11.6 1.3 %collective-permute-start = (bf16[16,16,128]{2,1,0:T(8,128)(2,1)S(1)}, bf16[16,16,128]{2,1,0:T(8,128)(2,1)S(1)}, u32[]{:S(2)}, u32[]{:S(2)}) collective-permute-start(bf16[16,16,128]{2,1,0:T(8,128)(2,1)S(1)} %get-tuple-element.35), channel_id=1, source_target_pairs={{0,1},{1,0},{2,3},{3,2},{4,5},{5,4},{6,7},{7,6},{8,9},{9,8},{10,11... | collective-permute-start | bytes 196616 | tf_op jit(solution)/shard_map/ppermute | solution.py:401
  13.0 5.3 %collective-permute-start.5 = (bf16[12,256,256]{2,1,0:T(8,128)(2,1)S(1)}, bf16[12,256,256]{2,1,0:T(8,128)(2,1)S(1)}, u32[]{:S(2)}, u32[]{:S(2)}) collective-permute-start(bf16[12,256,256]{2,1,0:T(8,128)(2,1)S(1)} %split.7), channel_id=1, source_target_pairs={{0,1},{1,0},{2,3},{3,2},{4,5},{5,4},{6,7},{7,6},{8,9},{9,8},{10,11... | collective-permute-start | bytes 4718600 | tf_op jit(solution)/shard_map/ppermute | solution.py:401
  13.2 5.1 %collective-permute-start.4 = (bf16[4,256,256]{2,1,0:T(8,128)(2,1)S(1)}, bf16[4,256,256]{2,1,0:T(8,128)(2,1)S(1)}, u32[]{:S(2)}, u32[]{:S(2)}) collective-permute-start(bf16[4,256,256]{2,1,0:T(8,128)(2,1)S(1)} %split.8), channel_id=1, source_target_pairs={{0,1},{1,0},{2,3},{3,2},{4,5},{5,4},{6,7},{7,6},{8,9},{9,8},{10,11... | collective-permute-start | bytes 1572872 | tf_op jit(solution)/shard_map/ppermute | solution.py:401
  13.6 6.6 %collective-permute-start.3 = (bf16[16,16,128]{2,1,0:T(8,128)(2,1)S(1)}, bf16[16,16,128]{2,1,0:T(8,128)(2,1)S(1)}, u32[]{:S(2)}, u32[]{:S(2)}) collective-permute-start(bf16[16,16,128]{2,1,0:T(8,128)(2,1)S(1)} %add_convert_fusion.8), channel_id=1, source_target_pairs={{0,6},{1,7},{2,4},{3,5},{4,2},{5,3},{6,0},{7,1},{8,14},{9,15},{10,... | collective-permute-start | bytes 196616 | tf_op jit(solution)/shard_map/ppermute | solution.py:401
  18.0 5.7 %collective-permute-start.2 = (bf16[16,16,128]{2,1,0:T(8,128)(2,1)S(1)}, bf16[16,16,128]{2,1,0:T(8,128)(2,1)S(1)}, u32[]{:S(2)}, u32[]{:S(2)}) collective-permute-start(bf16[16,16,128]{2,1,0:T(8,128)(2,1)S(1)} %add_convert_fusion.8), channel_id=1, source_target_pairs={{0,4},{1,5},{2,6},{3,7},{4,0},{5,1},{6,2},{7,3},{8,12},{9,13},{10,... | collective-permute-start | bytes 196616 | tf_op jit(solution)/shard_map/ppermute | solution.py:401
  18.0 5.7 %collective-permute-start.1 = (bf16[16,16,128]{2,1,0:T(8,128)(2,1)S(1)}, bf16[16,16,128]{2,1,0:T(8,128)(2,1)S(1)}, u32[]{:S(2)}, u32[]{:S(2)}) collective-permute-start(bf16[16,16,128]{2,1,0:T(8,128)(2,1)S(1)} %add_convert_fusion.8), channel_id=1, source_target_pairs={{0,2},{1,3},{2,0},{3,1},{4,6},{5,7},{6,4},{7,5},{8,10},{9,11},{10,... | collective-permute-start | bytes 196616 | tf_op jit(solution)/shard_map/ppermute | solution.py:401
  20.2 14.8 %collective-permute-start.17 = (bf16[4,256,256]{2,1,0:T(8,128)(2,1)S(1)}, bf16[4,256,256]{2,1,0:T(8,128)(2,1)S(1)}, u32[]{:S(2)}, u32[]{:S(2)}) collective-permute-start(bf16[4,256,256]{2,1,0:T(8,128)(2,1)S(1)} %get-tuple-element.43), channel_id=1, source_target_pairs={{0,2},{1,3},{6,4},{7,5},{8,10},{9,11},{14,12},{15,13},{16,18},{17,... | collective-permute-start | bytes 1572872 | tf_op jit(solution)/shard_map/ppermute | solution.py:430
  23.8 4.1 %collective-permute-start.8 = (bf16[16,16,128]{2,1,0:T(8,128)(2,1)S(1)}, bf16[16,16,128]{2,1,0:T(8,128)(2,1)S(1)}, u32[]{:S(2)}, u32[]{:S(2)}) collective-permute-start(bf16[16,16,128]{2,1,0:T(8,128)(2,1)S(1)} %add_convert_fusion.7), channel_id=1, source_target_pairs={{0,24},{8,16},{16,8},{24,0},{1,25},{9,17},{17,9},{25,1},{2,26},{10... | collective-permute-start | bytes 196616 | tf_op jit(solution)/shard_map/ppermute | solution.py:401
  26.0 5.7 %collective-permute-start.7 = (bf16[16,16,128]{2,1,0:T(8,128)(2,1)S(1)}, bf16[16,16,128]{2,1,0:T(8,128)(2,1)S(1)}, u32[]{:S(2)}, u32[]{:S(2)}) collective-permute-start(bf16[16,16,128]{2,1,0:T(8,128)(2,1)S(1)} %add_convert_fusion.7), channel_id=1, source_target_pairs={{0,16},{8,24},{16,0},{24,8},{1,17},{9,25},{17,1},{25,9},{2,18},{10... | collective-permute-start | bytes 196616 | tf_op jit(solution)/shard_map/ppermute | solution.py:401
  26.2 5.6 %collective-permute-start.6 = (bf16[16,16,128]{2,1,0:T(8,128)(2,1)S(1)}, bf16[16,16,128]{2,1,0:T(8,128)(2,1)S(1)}, u32[]{:S(2)}, u32[]{:S(2)}) collective-permute-start(bf16[16,16,128]{2,1,0:T(8,128)(2,1)S(1)} %add_convert_fusion.7), channel_id=1, source_target_pairs={{0,8},{8,0},{16,24},{24,16},{1,9},{9,1},{17,25},{25,17},{2,10},{10... | collective-permute-start | bytes 196616 | tf_op jit(solution)/shard_map/ppermute | solution.py:401
  26.5 15.5 %collective-permute-start.10 = (bf16[4,256,256]{2,1,0:T(8,128)(2,1)S(1)}, bf16[4,256,256]{2,1,0:T(8,128)(2,1)S(1)}, u32[]{:S(2)}, u32[]{:S(2)}) collective-permute-start(bf16[4,256,256]{2,1,0:T(8,128)(2,1)S(1)} %get-tuple-element.43), channel_id=1, source_target_pairs={{2,4},{3,5},{4,2},{5,3},{10,12},{11,13},{12,10},{13,11},{18,20},{1... | collective-permute-start | bytes 1572872 | tf_op jit(solution)/shard_map/ppermute | solution.py:431
  27.9 15.6 %collective-permute-start.11 = (bf16[4,256,256]{2,1,0:T(8,128)(2,1)S(1)}, bf16[4,256,256]{2,1,0:T(8,128)(2,1)S(1)}, u32[]{:S(2)}, u32[]{:S(2)}) collective-permute-start(bf16[4,256,256]{2,1,0:T(8,128)(2,1)S(1)} %get-tuple-element.44), channel_id=1, source_target_pairs={{0,4},{1,5},{6,2},{7,3},{8,12},{9,13},{14,10},{15,11},{16,20},{17,... | collective-permute-start | bytes 1572872 | tf_op jit(solution)/shard_map/ppermute | solution.py:432
  31.7 23.0 %collective-permute-start.16 = (bf16[4,256,256]{2,1,0:T(8,128)(2,1)S(1)}, bf16[4,256,256]{2,1,0:T(8,128)(2,1)S(1)}, u32[]{:S(2)}, u32[]{:S(2)}) collective-permute-start(bf16[4,256,256]{2,1,0:T(8,128)(2,1)S(1)} %get-tuple-element.46), channel_id=1, source_target_pairs={{0,2},{1,3},{2,0},{3,1},{4,6},{5,7},{6,4},{7,5},{8,10},{9,11},{10,... | collective-permute-start | bytes 1572872 | tf_op jit(solution)/shard_map/ppermute | solution.py:401
  31.9 4.6 %collective-permute-start.9 = (bf16[16,16,128]{2,1,0:T(8,128)(2,1)S(1)}, bf16[16,16,128]{2,1,0:T(8,128)(2,1)S(1)}, u32[]{:S(2)}, u32[]{:S(2)}) collective-permute-start(bf16[16,16,128]{2,1,0:T(8,128)(2,1)S(1)} %add_convert_fusion.6.old_ref), channel_id=1, source_target_pairs={{0,1},{1,0},{2,3},{3,2},{4,5},{5,4},{6,7},{7,6},{8,9},{9,8},{10,11... | collective-permute-start | bytes 196616 | tf_op jit(solution)/shard_map/ppermute | solution.py:401
  35.2 26.5 %collective-permute-start.18 = (bf16[4,256,256]{2,1,0:T(8,128)(2,1)S(1)}, bf16[4,256,256]{2,1,0:T(8,128)(2,1)S(1)}, u32[]{:S(2)}, u32[]{:S(2)}) collective-permute-start(bf16[4,256,256]{2,1,0:T(8,128)(2,1)S(1)} %add_convert_fusion), channel_id=1, source_target_pairs={{2,6},{3,7},{4,0},{5,1},{10,14},{11,15},{12,8},{13,9},{18,22},{19,... | collective-permute-start | bytes 1572872 | tf_op jit(solution)/shard_map/ppermute | solution.py:435
  43.5 4.9 %collective-permute-start.12 = (bf16[16,16,128]{2,1,0:T(8,128)(2,1)S(1)}, bf16[16,16,128]{2,1,0:T(8,128)(2,1)S(1)}, u32[]{:S(2)}, u32[]{:S(2)}) collective-permute-start(bf16[16,16,128]{2,1,0:T(8,128)(2,1)S(1)} %get-tuple-element.45), channel_id=1, source_target_pairs={{0,1},{1,0},{2,3},{3,2},{4,5},{5,4},{6,7},{7,6},{8,9},{9,8},{10,11... | collective-permute-start | bytes 196616 | tf_op jit(solution)/shard_map/ppermute | solution.py:401
  48.4 6.3 %collective-permute-start.13 = (bf16[16,16,128]{2,1,0:T(8,128)(2,1)S(1)}, bf16[16,16,128]{2,1,0:T(8,128)(2,1)S(1)}, u32[]{:S(2)}, u32[]{:S(2)}) collective-permute-start(bf16[16,16,128]{2,1,0:T(8,128)(2,1)S(1)} %add_convert_fusion.5), channel_id=1, source_target_pairs={{0,8},{8,0},{16,24},{24,16},{1,9},{9,1},{17,25},{25,17},{2,10},{10... | collective-permute-start | bytes 196616 | tf_op jit(solution)/shard_map/ppermute | solution.py:401
  49.7 5.1 %collective-permute-start.14 = (bf16[16,16,128]{2,1,0:T(8,128)(2,1)S(1)}, bf16[16,16,128]{2,1,0:T(8,128)(2,1)S(1)}, u32[]{:S(2)}, u32[]{:S(2)}) collective-permute-start(bf16[16,16,128]{2,1,0:T(8,128)(2,1)S(1)} %add_convert_fusion.5), channel_id=1, source_target_pairs={{0,16},{8,24},{16,0},{24,8},{1,17},{9,25},{17,1},{25,9},{2,18},{10... | collective-permute-start | bytes 196616 | tf_op jit(solution)/shard_map/ppermute | solution.py:401
  50.9 4.0 %collective-permute-start.15 = (bf16[16,16,128]{2,1,0:T(8,128)(2,1)S(1)}, bf16[16,16,128]{2,1,0:T(8,128)(2,1)S(1)}, u32[]{:S(2)}, u32[]{:S(2)}) collective-permute-start(bf16[16,16,128]{2,1,0:T(8,128)(2,1)S(1)} %add_convert_fusion.5), channel_id=1, source_target_pairs={{0,24},{8,16},{16,8},{24,0},{1,25},{9,17},{17,9},{25,1},{2,26},{10... | collective-permute-start | bytes 196616 | tf_op jit(solution)/shard_map/ppermute | solution.py:401
  61.7 6.5 %collective-permute-start.19 = (bf16[16,16,128]{2,1,0:T(8,128)(2,1)S(1)}, bf16[16,16,128]{2,1,0:T(8,128)(2,1)S(1)}, u32[]{:S(2)}, u32[]{:S(2)}) collective-permute-start(bf16[16,16,128]{2,1,0:T(8,128)(2,1)S(1)} %add_convert_fusion.4), channel_id=1, source_target_pairs={{0,2},{1,3},{2,0},{3,1},{4,6},{5,7},{6,4},{7,5},{8,10},{9,11},{10,... | collective-permute-start | bytes 196616 | tf_op jit(solution)/shard_map/ppermute | solution.py:401
  64.7 5.1 %collective-permute-start.20 = (bf16[16,16,128]{2,1,0:T(8,128)(2,1)S(1)}, bf16[16,16,128]{2,1,0:T(8,128)(2,1)S(1)}, u32[]{:S(2)}, u32[]{:S(2)}) collective-permute-start(bf16[16,16,128]{2,1,0:T(8,128)(2,1)S(1)} %add_convert_fusion.4), channel_id=1, source_target_pairs={{0,4},{1,5},{2,6},{3,7},{4,0},{5,1},{6,2},{7,3},{8,12},{9,13},{10,... | collective-permute-start | bytes 196616 | tf_op jit(solution)/shard_map/ppermute | solution.py:401
  64.8 5.3 %collective-permute-start.21 = (bf16[16,16,128]{2,1,0:T(8,128)(2,1)S(1)}, bf16[16,16,128]{2,1,0:T(8,128)(2,1)S(1)}, u32[]{:S(2)}, u32[]{:S(2)}) collective-permute-start(bf16[16,16,128]{2,1,0:T(8,128)(2,1)S(1)} %add_convert_fusion.4), channel_id=1, source_target_pairs={{0,6},{1,7},{2,4},{3,5},{4,2},{5,3},{6,0},{7,1},{8,14},{9,15},{10,... | collective-permute-start | bytes 196616 | tf_op jit(solution)/shard_map/ppermute | solution.py:401
  70.2 4.3 %collective-permute-start.22 = (bf16[16,16,128]{2,1,0:T(8,128)(2,1)S(1)}, bf16[16,16,128]{2,1,0:T(8,128)(2,1)S(1)}, u32[]{:S(2)}, u32[]{:S(2)}) collective-permute-start(bf16[16,16,128]{2,1,0:T(8,128)(2,1)S(1)} %add_convert_fusion.3.old_ref), channel_id=1, source_target_pairs={{0,1},{1,0},{2,3},{3,2},{4,5},{5,4},{6,7},{7,6},{8,9},{9,8},{10,11... | collective-permute-start | bytes 196616 | tf_op jit(solution)/shard_map/ppermute | solution.py:401
